TPU v7x, 32 devices: a whole 2x2x4 slice. The times are simulated.
32 devices in a mesh: parts: 2 (over y), space: 16 (over z, x, core).
Axes of the slice: x: 2, y: 2, z: 4, core: 2. Of those that a mesh axis runs over, the one named last changes fastest.
Arguments:
- outer_grad: bfloat16 [32, 4, 128, 1024], P(('parts', 'space')), parts along dimension 0, may hold values from -6 to 6
- block_input: bfloat16 [32, 4, 128, 1024], P(('parts', 'space')), parts along dimension 0, may hold values from -6 to 6
- third_input: bfloat16 [32, 4, 128, 1024], P(('parts', 'space')), parts along dimension 0, as said below
- second_input: bfloat16 [32, 8, 256, 256], P(('parts', 'space')), parts along dimension 0, as said below
- third_weight: bfloat16 [1024, 1024], replicated, may hold values from -0.1875 to 0.1875
- group_weight: bfloat16 [1024, 288], replicated, may hold values from -0.375 to 0.375
- first_weight: bfloat16 [1024, 1024], replicated, may hold values from -0.1875 to 0.1875
Outputs:
- input_grad: bfloat16 [32, 4, 128, 1024], P(('parts', 'space')), parts along dimension 0
- third_wgrad: float32 [2048, 1024], P(('parts', 'space')), parts along dimension 0
- group_wgrad: float32 [2048, 288], P(('parts', 'space')), parts along dimension 0
- first_wgrad: float32 [2048, 1024], P(('parts', 'space')), parts along dimension 0
There are 2 independent parts, one for each index of `parts`. A program takes and returns all parts, laid end to end along the dimension named above; an argument that names none is the same for every part. Nothing has to cross between parts.
Inputs may be any that keep to these rules, and one draw needn't show every extreme that they name: `third_input`: rectified values: zero or positive, about half of them zero. `second_input`: rectified values: zero or positive, about half of them zero.
All inputs are finite; a program needn't handle non-finite values.
Results may differ from a plain program's by a relative error of at most 0.0049.
Values may be sent and summed in bfloat16 or wider, within the bound.
A program may use at most 128 MiB of HBM per device.

v0:
```python
import math

import jax
import jax.numpy as jnp
from jax import lax
from jax.sharding import PartitionSpec as P


def partner(block, axis, distance):
    count = lax.axis_size(axis)
    route = []
    for low in range(count):
        high = low | 1 << distance
        if high != low and high < count:
            route += [(low, high), (high, low)]
    return lax.ppermute(block, axis, route)


def from_behind(array, axis, by):
    count = lax.axis_size(axis)
    pairs = [(i, i + by) for i in range(count) if 0 <= i + by < count]
    return lax.ppermute(array, axis, pairs)


def to_groups(tile, col_parity, row_parity, row_bit):
    tile_rows, tile_width, channels = tile.shape
    shard_width = channels // 4
    split = tile.reshape(tile_rows, tile_width, 2, 2, shard_width)
    kept_part = lax.dynamic_index_in_dim(split, col_parity, 3, keepdims=False)
    sent_part = lax.dynamic_index_in_dim(split, 1 - col_parity, 3, keepdims=False)
    received = partner(sent_part, "space", 0)
    joined = jnp.where(
        col_parity == 0, jnp.stack([kept_part, received], 1), jnp.stack([received, kept_part], 1)
    )
    joined = joined.reshape(tile_rows, 2 * tile_width, 2, shard_width)
    kept_rows = lax.dynamic_index_in_dim(joined, row_parity, 2, keepdims=False)
    sent_rows = lax.dynamic_index_in_dim(joined, 1 - row_parity, 2, keepdims=False)
    received_rows = partner(sent_rows, "space", row_bit)
    stacked = jnp.where(
        row_parity == 0,
        jnp.stack([kept_rows, received_rows], 0),
        jnp.stack([received_rows, kept_rows], 0),
    )
    return stacked.reshape(2 * tile_rows, 2 * tile_width, shard_width)


def to_tiles(block, col_parity, row_parity, row_bit):
    double_rows, double_cols, shard_width = block.shape
    tile_rows = double_rows // 2
    tile_width = double_cols // 2
    split = block.reshape(2, tile_rows, double_cols, shard_width)
    kept_part = lax.dynamic_index_in_dim(split, row_parity, 0, keepdims=False)
    sent_part = lax.dynamic_index_in_dim(split, 1 - row_parity, 0, keepdims=False)
    received = partner(sent_part, "space", row_bit)
    joined = jnp.where(
        row_parity == 0, jnp.stack([kept_part, received], 2), jnp.stack([received, kept_part], 2)
    )
    joined = joined.reshape(tile_rows, 2, tile_width, 2, shard_width)
    kept_cols = lax.dynamic_index_in_dim(joined, col_parity, 1, keepdims=False)
    sent_cols = lax.dynamic_index_in_dim(joined, 1 - col_parity, 1, keepdims=False)
    received_cols = partner(sent_cols, "space", 0)
    stacked = jnp.where(
        col_parity == 0,
        jnp.stack([kept_cols, received_cols], 3),
        jnp.stack([received_cols, kept_cols], 3),
    )
    return stacked.reshape(tile_rows, tile_width, 4 * shard_width)


def with_rims(block, row_step):
    top = from_behind(block[-1:], "space", row_step)
    bottom = from_behind(block[:1], "space", -row_step)
    tall = jnp.concatenate([top, block, bottom], 0)
    empty = jnp.zeros_like(tall[:, :1])
    return jnp.concatenate([empty, tall, empty], 1)


def group_backward(padded, second_block, kernel, normalizer):
    tile_rows, tile_width, channels = second_block.shape
    group_width = kernel.shape[3]
    groups = channels // group_width
    second_groups = second_block.reshape(tile_rows, tile_width, groups, group_width)
    back_second = jnp.zeros((tile_rows, tile_width, groups, group_width), jnp.float32)
    tap_terms = []
    for tap_row in range(3):
        for tap_col in range(3):
            window = padded[
                2 - tap_row : 2 - tap_row + tile_rows, 2 - tap_col : 2 - tap_col + tile_width
            ]
            window = window.reshape(tile_rows, tile_width, groups, group_width)
            back_second = back_second + jnp.einsum(
                "hwgo,goi->hwgi",
                window,
                kernel[:, :, 3 * tap_row + tap_col, :],
                preferred_element_type=jnp.float32,
            )
            tap_terms.append(
                jnp.einsum(
                    "hwgi,hwgo->goi", second_groups, window, preferred_element_type=jnp.float32
                )
            )
    local_term = jnp.stack(tap_terms, 2).reshape(channels, 9 * group_width) * normalizer
    return (back_second.reshape(tile_rows, tile_width, channels), local_term)


def per_device(
    outer_grad, block_input, third_input, second_input, third_weight, group_weight, first_weight
):
    devices = lax.axis_size("space")
    position = lax.axis_index("space")
    row_bit = 1
    col_parity = position % 2
    row_parity = position // 2 % 2
    tile_rows = outer_grad.shape[1]
    tile_width = outer_grad.shape[2]
    channels = outer_grad.shape[3]
    shard_width = channels // 4
    group_width = group_weight.shape[1] // 9
    normalizer = 1.0 / math.sqrt(tile_rows * tile_width * devices)
    grad_rows = outer_grad.reshape(tile_rows * tile_width, channels)
    third_rows = third_input.reshape(tile_rows * tile_width, channels)
    input_rows = block_input.reshape(tile_rows * tile_width, channels)
    back_third = lax.dot_general(
        grad_rows, third_weight, (((1,), (1,)), ((), ())), preferred_element_type=jnp.float32
    )
    inner_grad = jnp.where(third_rows > 0, back_third, 0.0).astype(jnp.bfloat16)
    left_cols = third_rows
    third_wgrad = lax.psum_scatter(
        lax.dot_general(
            left_cols, grad_rows, (((0,), (0,)), ((), ())), preferred_element_type=jnp.float32
        )
        * normalizer,
        "space",
        scatter_dimension=0,
        tiled=True,
    )
    inner_block = to_groups(
        inner_grad.reshape(tile_rows, tile_width, channels), col_parity, row_parity, row_bit
    )
    second_block = second_input[0]
    row_step = 4
    offset = (2 * row_parity + col_parity) * shard_width
    padded = with_rims(inner_block, row_step)
    kernel = lax.dynamic_slice_in_dim(group_weight, offset, shard_width, 0)
    kernel = kernel.reshape(shard_width // group_width, group_width, 9, group_width)
    back_second, local_term = group_backward(padded, second_block, kernel, normalizer)
    full_term = lax.dynamic_update_slice_in_dim(
        jnp.zeros((channels, 9 * group_width), jnp.float32), local_term, offset, 0
    )
    group_wgrad = lax.psum_scatter(full_term, "space", scatter_dimension=0, tiled=True)
    first_block = jnp.where(second_block > 0, back_second, 0.0).astype(jnp.bfloat16)
    first_tile = to_tiles(first_block, col_parity, row_parity, row_bit)
    first_rows = first_tile.reshape(tile_rows * tile_width, channels)
    summed = lax.dot_general(
        first_rows, first_weight, (((1,), (1,)), ((), ())), preferred_element_type=jnp.float32
    )
    input_grad = (
        (summed + grad_rows.astype(jnp.float32))
        .astype(jnp.bfloat16)
        .reshape(1, tile_rows, tile_width, channels)
    )
    left_cols = input_rows
    first_wgrad = lax.psum_scatter(
        lax.dot_general(
            left_cols, first_rows, (((0,), (0,)), ((), ())), preferred_element_type=jnp.float32
        )
        * normalizer,
        "space",
        scatter_dimension=0,
        tiled=True,
    )
    return (input_grad, third_wgrad, group_wgrad, first_wgrad)


def solution(mesh):
    in_specs = (
        P(("parts", "space"), None, None, None),
        P(("parts", "space"), None, None, None),
        P(("parts", "space"), None, None, None),
        P(("parts", "space"), None, None, None),
        P(),
        P(),
        P(),
    )
    out_specs = (
        P(("parts", "space"), None, None, None),
        P(("parts", "space"), None),
        P(("parts", "space"), None),
        P(("parts", "space"), None),
    )
    return jax.shard_map(
        per_device, mesh=mesh, in_specs=in_specs, out_specs=out_specs, check_vma=False
    )
```

profile of v0, /device:TPU:0, one launch (start us, length us, event | category | flops | bytes accessed | tf_op | source)
XLA Modules:
  0.0 278.1 jit_solution(1105585685217040148)
XLA Ops:
  7.2 1.6 broadcast_compare_fusion
  9.1 2.5 select_convert_fusion.1
  12.4 2.2 constant_dynamic-slice_fusion.5
  15.3 1.4 collective-permute-done
  17.0 2.9 %collective-permute-start.1 = (bf16[4,256,256]{2,1,0:T(8,128)(2,1)S(1)}, bf16[4,256,256]{2,1,0:T(8,128)(2,1)S(1)}, u32[]{:S(2)}, u32[]{:S(2)}) collective-permute-start(bf16[4,256,256]{2,1,0:T(8,128)(2,1)S(1)} %get-tuple-element.39), channel_id=1, source_target_pairs={{0,2},{2,0},{1,3},{3,1},{4,6},{6,4},{5,7},{7,5},{8,10},{10,8},{9,1... | collective-permute-start | bytes 1572872 | tf_op jit(solution)/shard_map/ppermute | solution.py:16
  19.9 12.2 %collective-permute-done.1 = bf16[4,256,256]{2,1,0:T(8,128)(2,1)S(1)} collective-permute-done((bf16[4,256,256]{2,1,0:T(8,128)(2,1)S(1)}, bf16[4,256,256]{2,1,0:T(8,128)(2,1)S(1)}, u32[]{:S(2)}, u32[]{:S(2)}) %collective-permute-start.1) | collective-permute-done | bytes 524320 | tf_op jit(solution)/shard_map/ppermute | solution.py:16
  33.5 3.7 %collective-permute-start.2 = (bf16[1,256,256]{1,2,0:T(8,128)(2,1)}, bf16[1,256,256]{1,2,0:T(8,128)(2,1)S(1)}, u32[]{:S(2)}, u32[]{:S(2)}) collective-permute-start(bf16[1,256,256]{1,2,0:T(8,128)(2,1)} %get-tuple-element.36), channel_id=1, source_target_pairs={{0,4},{1,5},{2,6},{3,7},{4,8},{5,9},{6,10},{7,11},{8,12},{9,13},{1... | collective-permute-start | bytes 393224 | tf_op jit(solution)/shard_map/ppermute | solution.py:22
  38.6 1.5 copy.179
  40.1 1.3 copy.161
  41.4 2.7 collective-permute-done.3
  44.3 2.4 pad_slice_fusion.5
  52.4 1.4 copy.180
  53.8 1.6 mul.29
  57.9 4.5 %bitcast_multiply_fusion = f32[1024,1024]{1,0:T(8,128)} fusion(bf16[1,4,128,1024]{3,2,1,0:T(8,128)(2,1)} %param.7, bf16[1,4,128,1024]{3,2,1,0:T(8,128)(2,1)S(1)} %copy-done.17), kind=kOutput, calls=%fused_computation | convolution fusion | flops 1074790400 | bytes 6291456 | tf_op jit(solution)/shard_map/dot_general | solution.py:129
  65.7 1.9 copy.144
  76.7 1.5 collective-permute-start.4
  78.4 13.0 %collective-permute-done.4 = bf16[4,256,256]{2,1,0:T(8,128)(2,1)S(1)} collective-permute-done((bf16[4,256,256]{2,1,0:T(8,128)(2,1)S(1)}, bf16[4,256,256]{2,1,0:T(8,128)(2,1)S(1)}, u32[]{:S(2)}, u32[]{:S(2)}) %collective-permute-start.4) | collective-permute-done | bytes 524320 | tf_op jit(solution)/shard_map/ppermute | solution.py:16
  91.8 1.9 collective-permute-done.5
  96.1 3.3 %multiply_bitcast_fusion = f32[1024,1024]{0,1:T(8,128)} fusion(bf16[512,1024]{1,0:T(8,128)(2,1)S(1)} %select_n.125, bf16[512,1024]{1,0:T(8,128)(2,1)S(1)} %bitcast.217), kind=kOutput, calls=%fused_computation.1 | convolution fusion | flops 1074790400 | bytes 6291456 | tf_op jit(solution)/shard_map/dot_general | solution.py:164
  99.4 5.5 %copy.193 = f32[1024,1024]{1,0:T(8,128)} copy(f32[1024,1024]{0,1:T(8,128)} %multiply_bitcast_fusion) | data formatting | bytes 8388608
  104.9 4.3 %add_convert_fusion = bf16[512,1024]{1,0:T(8,128)(2,1)} fusion(bf16[512,1024]{1,0:T(8,128)(2,1)} %bitcast.219, bf16[512,1024]{1,0:T(8,128)(2,1)S(1)} %select_n.125, bf16[1024,1024]{1,0:T(8,128)(2,1)} %param.13), kind=kOutput, calls=%fused_computation.9 | convolution fusion | flops 1075314688 | bytes 5242880 | tf_op jit(solution)/shard_map/dot_general | solution.py:154
  109.2 9.7 %reduce-scatter.8.cloned.1.call-done = f32[64,288]{1,0:T(8,128)} async-done(((f32[1024,288]{1,0:T(8,128)}), f32[64,288]{1,0:T(8,128)}) %reduce-scatter.8.cloned.1.call-update) | async-done | bytes 73744 | tf_op jit(solution)/shard_map/reduce_scatter | solution.py:150
  118.9 76.6 %reduce-scatter.6.cloned.1.call-done = f32[64,1024]{1,0:T(8,128)} async-done(((f32[1024,1024]{1,0:T(8,128)}), f32[64,1024]{1,0:T(8,128)}) %reduce-scatter.6.cloned.1.call-update) | async-done | bytes 262160 | tf_op jit(solution)/shard_map/reduce_scatter | solution.py:128
  195.5 76.0 %reduce-scatter.10.cloned.1.call-done = f32[64,1024]{1,0:T(8,128)} async-done(((f32[1024,1024]{1,0:T(8,128)}), f32[64,1024]{1,0:T(8,128)}) %reduce-scatter.10.cloned.1.call-update) | async-done | bytes 262160
  (99 shorter events, 28.2 us)
Async XLA Ops:
  7.2 1.9 copy-start
  7.2 111.7 %reduce-scatter.8.cloned.1.call-start = ((), (), s32[]{:S(2)}) async-start(), calls=%async_computation.4 | async-start | bytes 1671168 | tf_op jit(solution)/shard_map/reduce_scatter | solution.py:150
  14.7 2.1 collective-permute-start
  17.0 15.2 %collective-permute-start.1 = (bf16[4,256,256]{2,1,0:T(8,128)(2,1)S(1)}, bf16[4,256,256]{2,1,0:T(8,128)(2,1)S(1)}, u32[]{:S(2)}, u32[]{:S(2)}) collective-permute-start(bf16[4,256,256]{2,1,0:T(8,128)(2,1)S(1)} %get-tuple-element.39), channel_id=1, source_target_pairs={{0,2},{2,0},{1,3},{3,1},{4,6},{6,4},{5,7},{7,5},{8,10},{10,8},{9,1... | collective-permute-start | bytes 1572872 | tf_op jit(solution)/shard_map/ppermute | solution.py:16
  33.5 7.8 %collective-permute-start.2 = (bf16[1,256,256]{1,2,0:T(8,128)(2,1)}, bf16[1,256,256]{1,2,0:T(8,128)(2,1)S(1)}, u32[]{:S(2)}, u32[]{:S(2)}) collective-permute-start(bf16[1,256,256]{1,2,0:T(8,128)(2,1)} %get-tuple-element.36), channel_id=1, source_target_pairs={{0,4},{1,5},{2,6},{3,7},{4,8},{5,9},{6,10},{7,11},{8,12},{9,13},{1... | collective-permute-start | bytes 393224 | tf_op jit(solution)/shard_map/ppermute | solution.py:22
  37.3 6.9 %collective-permute-start.3 = (bf16[1,256,256]{1,2,0:T(8,128)(2,1)S(1)}, bf16[1,256,256]{1,2,0:T(8,128)(2,1)S(1)}, u32[]{:S(2)}, u32[]{:S(2)}) collective-permute-start(bf16[1,256,256]{1,2,0:T(8,128)(2,1)S(1)} %get-tuple-element.37), channel_id=1, source_target_pairs={{4,0},{5,1},{6,2},{7,3},{8,4},{9,5},{10,6},{11,7},{12,8},{13,9},{1... | collective-permute-start | bytes 393224 | tf_op jit(solution)/shard_map/ppermute | solution.py:22
  46.7 1.4 copy-start.13
  46.7 2.6 copy-start.15
  46.7 3.8 %copy-start.9 = (bf16[8,256,256]{1,2,0:T(8,128)(2,1)}, bf16[8,256,256]{1,2,0:T(8,128)(2,1)S(1)}, u32[]{:S(2)}) copy-start(bf16[8,256,256]{1,2,0:T(8,128)(2,1)S(1)} %get-tuple-element.27) | copy-start | bytes 3145732
  46.7 4.2 %copy-start.7 = (bf16[8,256,256]{1,2,0:T(8,128)(2,1)}, bf16[8,256,256]{1,2,0:T(8,128)(2,1)S(1)}, u32[]{:S(2)}) copy-start(bf16[8,256,256]{1,2,0:T(8,128)(2,1)S(1)} %get-tuple-element.26) | copy-start | bytes 3145732
  46.7 5.1 %copy-start.5 = (bf16[8,256,256]{1,2,0:T(8,128)(2,1)}, bf16[8,256,256]{1,2,0:T(8,128)(2,1)S(1)}, u32[]{:S(2)}) copy-start(bf16[8,256,256]{1,2,0:T(8,128)(2,1)S(1)} %get-tuple-element.28) | copy-start | bytes 3145732
  47.7 1.6 copy-start.3
  48.1 2.0 copy-start.2
  55.6 2.3 copy-start.17
  57.7 137.8 %reduce-scatter.6.cloned.1.call-start = ((), (), s32[]{:S(2)}) async-start(), calls=%async_computation.3 | async-start | bytes 4456448 | tf_op jit(solution)/shard_map/reduce_scatter | solution.py:128
  62.4 2.2 copy-start.18
  62.4 209.1 %reduce-scatter.10.cloned.1.call-start = ((), (), s32[]{:S(2)}) async-start(), calls=%async_computation.5 | async-start | bytes 4456448
  67.5 1.7 copy-start.4
  69.6 1.3 copy-start.14
  71.4 1.3 copy-start.10
  73.1 1.3 copy-start.6
  76.7 14.7 %collective-permute-start.4 = (bf16[4,256,256]{2,1,0:T(8,128)(2,1)S(1)}, bf16[4,256,256]{2,1,0:T(8,128)(2,1)S(1)}, u32[]{:S(2)}, u32[]{:S(2)}) collective-permute-start(bf16[4,256,256]{2,1,0:T(8,128)(2,1)S(1)} %bitcast.225), channel_id=1, source_target_pairs={{0,2},{2,0},{1,3},{3,1},{4,6},{6,4},{5,7},{7,5},{8,10},{10,8},{9,1... | collective-permute-start | bytes 1572872 | tf_op jit(solution)/shard_map/ppermute | solution.py:16
  91.7 2.0 collective-permute-start.5
  104.9 166.7 %copy-start.1 = (bf16[1024,1024]{1,0:T(8,128)(2,1)S(1)}, bf16[1024,1024]{1,0:T(8,128)(2,1)}, u32[]{:S(2)}) copy-start(bf16[1024,1024]{1,0:T(8,128)(2,1)} %param.11) | copy-start | bytes 6291460
  (5 other events, 6.1 us)
Sparse Core Ops, SparseCore 0:
  57.8 61.0 reduce-scatter.7
  123.8 71.6 reduce-scatter.5
  200.0 71.5 reduce-scatter.9
where the time goes:
time: 279 us; the launch traced here: 278 us
  waiting for transfers between devices  194 us (70%)
  local copies, waits for them, and re-layouts  33.1 us (12%)
  matrix products  22.7 us (8%)
  between operations  14.2 us (5%)
  starting transfers between devices  10.4 us (4%)
  other arithmetic  4.05 us (1%)
    reduce_scatter x1, waiting for transfers between devices, per_device(): lax.psum_scatter(lax.dot_general(left_cols, grad_rows, (((0,), (0,)), (()...  76.6 us
    unnamed x4, waiting for transfers between devices  76.1 us
    ppermute x4, waiting for transfers between devices, partner(): return lax.ppermute(block, axis, route)  28.5 us
    unnamed x44, local copies, waits for them, and re-layouts  12.1 us
    reduce_scatter x1, waiting for transfers between devices, per_device(): lax.psum_scatter(full_term, 'space', scatter_dimension=0, tiled=True)  9.7 us
  transfers between devices with their start and end apart: 9, of which 8 were waited for; matrix products, arithmetic and copies ran while one was open for 12% of the time, Pallas kernels for 0%

commit v1 on v0

--- a/solution.py
+++ b/solution.py
@@ -20,6 +20,39 @@
     count = lax.axis_size(axis)
     pairs = [(i, i + by) for i in range(count) if 0 <= i + by < count]
     return lax.ppermute(array, axis, pairs)
+
+
+def halve(piece, order, bits):
+    position = lax.axis_index("space")
+    left = list(range(bits))[::-1]
+    for bit in order:
+        axis = left.index(bit)
+        mine = position // (1 << bit) % 2
+        sent = lax.dynamic_index_in_dim(piece, 1 - mine, axis, keepdims=False)
+        kept = lax.dynamic_index_in_dim(piece, mine, axis, keepdims=False)
+        received = partner(sent.astype(jnp.bfloat16), "space", bit)
+        piece = kept + received.astype(jnp.float32)
+        left.remove(bit)
+    return piece
+
+
+def sum_shards(term, pieces):
+    devices = lax.axis_size("space")
+    bits = devices.bit_length() - 1
+    rows, columns = term.shape
+    view = term.reshape((2,) * bits + (rows // devices, columns))
+    low_first = list(range(bits))
+    high_first = [0] + list(range(2, bits)) + [1]
+    width = columns // pieces
+    done = [
+        halve(
+            view[..., at * width : (at + 1) * width],
+            (low_first, high_first)[at % 2],
+            bits,
+        )
+        for at in range(pieces)
+    ]
+    return done[0] if pieces == 1 else jnp.concatenate(done, -1)
 
 
 def to_groups(tile, col_parity, row_parity, row_bit):
@@ -125,14 +158,12 @@
     )
     inner_grad = jnp.where(third_rows > 0, back_third, 0.0).astype(jnp.bfloat16)
     left_cols = third_rows
-    third_wgrad = lax.psum_scatter(
+    third_wgrad = sum_shards(
         lax.dot_general(
             left_cols, grad_rows, (((0,), (0,)), ((), ())), preferred_element_type=jnp.float32
         )
         * normalizer,
-        "space",
-        scatter_dimension=0,
-        tiled=True,
+        2,
     )
     inner_block = to_groups(
         inner_grad.reshape(tile_rows, tile_width, channels), col_parity, row_parity, row_bit
@@ -147,7 +178,7 @@
     full_term = lax.dynamic_update_slice_in_dim(
         jnp.zeros((channels, 9 * group_width), jnp.float32), local_term, offset, 0
     )
-    group_wgrad = lax.psum_scatter(full_term, "space", scatter_dimension=0, tiled=True)
+    group_wgrad = sum_shards(full_term, 1)
     first_block = jnp.where(second_block > 0, back_second, 0.0).astype(jnp.bfloat16)
     first_tile = to_tiles(first_block, col_parity, row_parity, row_bit)
     first_rows = first_tile.reshape(tile_rows * tile_width, channels)
@@ -160,14 +191,12 @@
         .reshape(1, tile_rows, tile_width, channels)
     )
     left_cols = input_rows
-    first_wgrad = lax.psum_scatter(
+    first_wgrad = sum_shards(
         lax.dot_general(
             left_cols, first_rows, (((0,), (0,)), ((), ())), preferred_element_type=jnp.float32
         )
         * normalizer,
-        "space",
-        scatter_dimension=0,
-        tiled=True,
+        2,
     )
     return (input_grad, third_wgrad, group_wgrad, first_wgrad)
 

time: 279 us -> 168 us (0.60)
  waiting for transfers between devices: 194 us -> 53.7 us
  starting transfers between devices: 10.4 us -> 28.2 us
  local copies, waits for them, and re-layouts: 33.1 us -> 46.5 us
  between operations: 14.2 us -> 1.65 us
  other arithmetic: 4.05 us -> 15.1 us
    reduce_scatter x2 -> x0, waiting for transfers between devices: 86.3 us -> none  [the longest x1 76.6 us: per_device(): lax.psum_scatter(lax.dot_general(left_cols, grad_rows, (((0,), (0,)), (()...]
    unnamed x4 -> x0, waiting for transfers between devices: 76.1 us -> none
    ppermute x4 -> x24, waiting for transfers between devices: 28.5 us -> 50.7 us  [partner(): return lax.ppermute(block, axis, route)]
    ppermute x4 -> x24, starting transfers between devices: 5.05 us -> 23.5 us  [partner(): return lax.ppermute(block, axis, route)]
    add x0 -> x20, other arithmetic: none -> 5.58 us  [halve(): piece = kept + received.astype(jnp.float32)]
    mul x0 -> x1, local copies, waits for them, and re-layouts: none -> 5.43 us  [per_device(): lax.dot_general(left_cols, first_rows, (((0,), (0,)), ((), ())), preferre...]
    dot_general x9, matrix products: 4.38 us -> 8.49 us  [group_backward(): jnp.einsum('hwgo,goi->hwgi', window, kernel[:, :, 3 * tap_row + tap_col,...]
    convert_element_type x0 -> x20, local copies, waits for them, and re-layouts: none -> 3.73 us  [halve(): received = partner(sent.astype(jnp.bfloat16), 'space', bit)]
  transfers between devices with their start and end apart: 9 -> 26, of which waited for: 8 -> 11; matrix products, arithmetic and copies ran while one was open for 12% -> 31% of each run, Pallas kernels for 0% -> 0%
where the time goes in v1:
time: 168 us; the launch traced here: 167 us
  waiting for transfers between devices  53.7 us (32%)
  local copies, waits for them, and re-layouts  46.5 us (28%)
  starting transfers between devices  28.2 us (17%)
  matrix products  21.6 us (13%)
  other arithmetic  15.1 us (9%)
    ppermute x24, waiting for transfers between devices, partner(): return lax.ppermute(block, axis, route)  50.7 us
    ppermute x24, starting transfers between devices, partner(): return lax.ppermute(block, axis, route)  23.5 us
    unnamed x81, local copies, waits for them, and re-layouts  11.8 us
    dot_general x9, matrix products, group_backward(): jnp.einsum('hwgo,goi->hwgi', window, kernel[:, :, 3 * tap_row + tap_col,...  8.49 us
    add x20, other arithmetic, halve(): piece = kept + received.astype(jnp.float32)  5.58 us
    mul x1, local copies, waits for them, and re-layouts, per_device(): lax.dot_general(left_cols, first_rows, (((0,), (0,)), ((), ())), preferre...  5.43 us
    ppermute x2, starting transfers between devices, from_behind(): return lax.ppermute(array, axis, pairs)  4.77 us
    dot_general x9, matrix products, group_backward(): jnp.einsum('hwgi,hwgo->goi', second_groups, window, preferred_element_typ...  3.75 us
  transfers between devices with their start and end apart: 26, of which 11 were waited for; matrix products, arithmetic and copies ran while one was open for 31% of the time, Pallas kernels for 0%

profile of v1, /device:TPU:0, one launch (start us, length us, event | category | flops | bytes accessed | tf_op | source)
XLA Modules:
  0.0 166.8 jit_solution(3639090410695743008)
XLA Ops:
  2.5 2.5 %select_convert_fusion.1 = bf16[512,1024]{1,0:T(8,128)(2,1)S(1)} fusion(pred[1,4,128,1024]{3,2,1,0:T(32,128)(4,1)S(1)} %broadcast_compare_fusion, bf16[512,1024]{1,0:T(8,128)(2,1)} %bitcast.310, bf16[1024,1024]{1,0:T(8,128)(2,1)S(1)} %copy-done), kind=kOutput, calls=%fused_computation.11 | convolution fusion | flops 1074790400 | bytes 4718592 | tf_op jit(solution)/shard_map/dot_general | solution.py:156
  14.7 2.3 %broadcast_compare_fusion.1 = pred[1,8,256,256]{3,2,1,0:T(8,128)(4,1)} fusion(bf16[1,8,256,256]{3,2,1,0:T(8,128)(2,1)} %param.10), kind=kLoop, calls=%fused_computation.89 | loop fusion | flops 524288 | bytes 1572864 | tf_op jit(solution)/shard_map/gt | solution.py:182
  17.0 2.8 %constant_dynamic-slice_fusion.3 = (f32[2,2,2,1,64,512]{5,4,3,2,1,0:T(8,128)}, f32[2,2,2,1,64,512]{5,4,3,2,1,0:T(8,128)}) fusion(f32[2,2,2,2,64,512]{5,4,3,2,1,0:T(8,128)} %copy-done.19, s32[]{:T(128)S(6)} %select_n.239, f32[2,2,2,2,64,512]{5,4,3,2,1,0:T(8,128)S(1)} %get-tuple-element.6), kind=kLoop, calls=%fused_computation.143 | loop fusion | bytes 4194308 | tf_op jit(solution)/shard_map/jit(dynamic_index_in_dim)/dynamic_slice | solution.py:32
  22.6 2.4 %copy.117 = pred[1,8,256,256]{2,3,1,0:T(8,128)(4,1)} copy(pred[1,8,256,256]{3,2,1,0:T(8,128)(4,1)} %broadcast_compare_fusion.1) | data formatting | bytes 1048576 | tf_op jit(solution)/shard_map/gt | solution.py:182
  28.5 2.6 %collective-permute-start.1 = (bf16[4,256,256]{2,1,0:T(8,128)(2,1)S(1)}, bf16[4,256,256]{2,1,0:T(8,128)(2,1)S(1)}, u32[]{:S(2)}, u32[]{:S(2)}) collective-permute-start(bf16[4,256,256]{2,1,0:T(8,128)(2,1)S(1)} %get-tuple-element.23), channel_id=1, source_target_pairs={{0,2},{2,0},{1,3},{3,1},{4,6},{6,4},{5,7},{7,5},{8,10},{10,8},{9,1... | collective-permute-start | bytes 1572872 | tf_op jit(solution)/shard_map/ppermute | solution.py:16
  36.3 4.5 %collective-permute-done.11 = bf16[2,2,64,512]{3,2,1,0:T(8,128)(2,1)S(1)} collective-permute-done((bf16[2,2,64,512]{3,2,1,0:T(8,128)(2,1)S(1)}, bf16[2,2,64,512]{3,2,1,0:T(8,128)(2,1)S(1)}, u32[]{:S(2)}, u32[]{:S(2)}) %collective-permute-start.11) | collective-permute-done | bytes 262176 | tf_op jit(solution)/shard_map/ppermute | solution.py:16
  41.0 2.7 %collective-permute-start.12 = (bf16[2,64,512]{2,1,0:T(8,128)(2,1)S(1)}, bf16[2,64,512]{2,1,0:T(8,128)(2,1)S(1)}, u32[]{:S(2)}, u32[]{:S(2)}) collective-permute-start(bf16[2,64,512]{2,1,0:T(8,128)(2,1)S(1)} %fusion.42), channel_id=1, source_target_pairs={{0,8},{8,0},{1,9},{9,1},{2,10},{10,2},{3,11},{11,3},{4,12},{12,4},... | collective-permute-start | bytes 393224 | tf_op jit(solution)/shard_map/ppermute | solution.py:16
  43.6 5.6 %collective-permute-done.7 = bf16[2,2,64,512]{3,2,0,1:T(8,128)(2,1)S(1)} collective-permute-done((bf16[2,2,64,512]{3,2,0,1:T(8,128)(2,1)S(1)}, bf16[2,2,64,512]{3,2,0,1:T(8,128)(2,1)S(1)}, u32[]{:S(2)}, u32[]{:S(2)}) %collective-permute-start.7) | collective-permute-done | bytes 262176 | tf_op jit(solution)/shard_map/ppermute | solution.py:16
  55.5 2.6 %collective-permute-start.9 = (bf16[64,512]{1,0:T(8,128)(2,1)}, bf16[64,512]{1,0:T(8,128)(2,1)}, u32[]{:S(2)}, u32[]{:S(2)}) collective-permute-start(bf16[64,512]{1,0:T(8,128)(2,1)} %fusion.46), channel_id=1, source_target_pairs={{0,8},{8,0},{1,9},{9,1},{2,10},{10,2},{3,11},{11,3},{4,12},{12,4},... | collective-permute-start | bytes 196616 | tf_op jit(solution)/shard_map/ppermute | solution.py:16
  61.8 3.5 %collective-permute-start.2 = (bf16[1,256,256]{1,2,0:T(8,128)(2,1)S(1)}, bf16[1,256,256]{1,2,0:T(8,128)(2,1)S(1)}, u32[]{:S(2)}, u32[]{:S(2)}) collective-permute-start(bf16[1,256,256]{1,2,0:T(8,128)(2,1)S(1)} %get-tuple-element.20), channel_id=1, source_target_pairs={{0,4},{1,5},{2,6},{3,7},{4,8},{5,9},{6,10},{7,11},{8,12},{9,13},{1... | collective-permute-start | bytes 393224 | tf_op jit(solution)/shard_map/ppermute | solution.py:22
  66.6 2.6 %fusion.21 = f32[8,32,8,256]{3,1,2,0:T(8,128)} fusion(bf16[8,256,8,32]{1,3,2,0:T(8,128)(2,1)S(1)} %bitcast.284, bf16[8,32,1,32]{1,0,3,2:T(8,128)(2,1)} %get-tuple-element.29), kind=kOutput, calls=%fused_computation.56 | convolution fusion | flops 33554432 | bytes 3162112 | tf_op jit(solution)/shard_map/hwgo,goi->hwgi/dot_general | solution.py:124
  69.2 3.0 %collective-permute-done.3 = bf16[1,256,256]{1,2,0:T(8,128)(2,1)S(1)} collective-permute-done((bf16[1,256,256]{1,2,0:T(8,128)(2,1)S(1)}, bf16[1,256,256]{1,2,0:T(8,128)(2,1)S(1)}, u32[]{:S(2)}, u32[]{:S(2)}) %collective-permute-start.3) | collective-permute-done | bytes 131104 | tf_op jit(solution)/shard_map/ppermute | solution.py:22
  72.3 2.5 %pad_slice_fusion.5 = (bf16[8,256,256]{1,2,0:T(8,128)(2,1)S(1)}, bf16[8,256,256]{1,2,0:T(8,128)(2,1)S(1)}, bf16[8,256,256]{1,2,0:T(8,128)(2,1)S(1)}, bf16[8,256,...) fusion(bf16[10,256,256]{1,2,0:T(8,128)(2,1)S(1)} %pad_maximum_fusion), kind=kLoop, calls=%fused_computation.7 | loop fusion | bytes 7602176 | tf_op jit(solution)/shard_map/slice | solution.py:120
  75.8 2.4 %fusion.27 = f32[8,32,8,256]{3,1,2,0:T(8,128)} fusion(bf16[8,256,8,32]{1,3,2,0:T(8,128)(2,1)S(1)} %bitcast.286, bf16[8,32,1,32]{1,0,3,2:T(8,128)(2,1)S(1)} %copy-done.37), kind=kOutput, calls=%fused_computation.62 | convolution fusion | flops 33554432 | bytes 3162112 | tf_op jit(solution)/shard_map/hwgo,goi->hwgi/dot_general | solution.py:124
  100.0 14.8 %collective-permute-done.15 = bf16[2,2,64,288]{3,2,1,0:T(8,128)(2,1)S(1)} collective-permute-done((bf16[2,2,64,288]{3,2,1,0:T(8,128)(2,1)S(1)}, bf16[2,2,64,288]{3,2,1,0:T(8,128)(2,1)S(1)}, u32[]{:S(2)}, u32[]{:S(2)}) %collective-permute-start.15) | collective-permute-done | bytes 147488 | tf_op jit(solution)/shard_map/ppermute | solution.py:16
  116.6 3.0 %collective-permute-done.16 = bf16[2,64,288]{2,1,0:T(8,128)(2,1)S(1)} collective-permute-done((bf16[2,64,288]{2,1,0:T(8,128)(2,1)S(1)}, bf16[2,64,288]{2,1,0:T(8,128)(2,1)S(1)}, u32[]{:S(2)}, u32[]{:S(2)}) %collective-permute-start.16) | collective-permute-done | bytes 73760 | tf_op jit(solution)/shard_map/ppermute | solution.py:16
  120.8 3.9 %collective-permute-done.17 = bf16[64,288]{1,0:T(8,128)(2,1)S(1)} collective-permute-done((bf16[64,288]{1,0:T(8,128)(2,1)S(1)}, bf16[64,288]{1,0:T(8,128)(2,1)S(1)}, u32[]{:S(2)}, u32[]{:S(2)}) %collective-permute-start.17) | collective-permute-done | bytes 36896 | tf_op jit(solution)/shard_map/ppermute | solution.py:16
  127.8 3.3 %multiply_bitcast_fusion = f32[1024,1024]{0,1:T(8,128)} fusion(bf16[512,1024]{1,0:T(8,128)(2,1)S(1)} %select_n.251, bf16[512,1024]{1,0:T(8,128)(2,1)S(1)} %bitcast.309), kind=kOutput, calls=%fused_computation.1 | convolution fusion | flops 1074790400 | bytes 6291456 | tf_op jit(solution)/shard_map/dot_general | solution.py:195
  131.1 5.4 %copy.158 = f32[1024,1024]{1,0:T(8,128)} copy(f32[1024,1024]{0,1:T(8,128)} %multiply_bitcast_fusion) | data formatting | bytes 8388608 | tf_op jit(solution)/shard_map/mul | solution.py:195
  136.5 3.0 %fusion.51 = (f32[2,2,2,2,64,512]{5,4,3,2,1,0:T(8,128)S(1)}, f32[2,2,2,2,64,512]{5,4,3,2,1,0:T(8,128)S(1)}) fusion(f32[2,2,2,2,64,1024]{5,4,3,2,1,0:T(8,128)} %bitcast.281), kind=kLoop, calls=%fused_computation.153 | loop fusion | bytes 8388608 | tf_op jit(solution)/shard_map/slice | solution.py:49
  145.2 6.0 %collective-permute-done.23 = bf16[2,2,64,512]{3,2,1,0:T(8,128)(2,1)S(1)} collective-permute-done((bf16[2,2,64,512]{3,2,1,0:T(8,128)(2,1)S(1)}, bf16[2,2,64,512]{3,2,1,0:T(8,128)(2,1)S(1)}, u32[]{:S(2)}, u32[]{:S(2)}) %collective-permute-start.23) | collective-permute-done | bytes 262176 | tf_op jit(solution)/shard_map/ppermute | solution.py:16
  153.4 5.8 %collective-permute-done.24 = bf16[2,64,512]{2,1,0:T(8,128)(2,1)S(1)} collective-permute-done((bf16[2,64,512]{2,1,0:T(8,128)(2,1)S(1)}, bf16[2,64,512]{2,1,0:T(8,128)(2,1)S(1)}, u32[]{:S(2)}, u32[]{:S(2)}) %collective-permute-start.24) | collective-permute-done | bytes 131104 | tf_op jit(solution)/shard_map/ppermute | solution.py:16
  160.9 2.6 %collective-permute-done.25 = bf16[64,512]{1,0:T(8,128)(2,1)S(1)} collective-permute-done((bf16[64,512]{1,0:T(8,128)(2,1)S(1)}, bf16[64,512]{1,0:T(8,128)(2,1)S(1)}, u32[]{:S(2)}, u32[]{:S(2)}) %collective-permute-start.25) | collective-permute-done | bytes 65568 | tf_op jit(solution)/shard_map/ppermute | solution.py:16
  163.6 2.5 %collective-permute-done.21 = bf16[64,512]{1,0:T(8,128)(2,1)S(1)} collective-permute-done((bf16[64,512]{1,0:T(8,128)(2,1)S(1)}, bf16[64,512]{1,0:T(8,128)(2,1)S(1)}, u32[]{:S(2)}, u32[]{:S(2)}) %collective-permute-start.21) | collective-permute-done | bytes 65568 | tf_op jit(solution)/shard_map/ppermute | solution.py:16
  (213 shorter events, 72.9 us)
Async XLA Ops:
  9.0 17.7 %collective-permute-start = (bf16[4,128,2,256]{3,1,2,0:T(8,128)(2,1)}, bf16[4,128,2,256]{3,1,2,0:T(8,128)(2,1)}, u32[]{:S(2)}, u32[]{:S(2)}) collective-permute-start(bf16[4,128,2,256]{3,1,2,0:T(8,128)(2,1)} %bitcast.267), channel_id=1, source_target_pairs={{0,1},{1,0},{2,3},{3,2},{4,5},{5,4},{6,7},{7,6},{8,9},{9,8},{10,11... | collective-permute-start | bytes 1572872 | tf_op jit(solution)/shard_map/ppermute | solution.py:16
  13.3 17.8 %collective-permute-start.10 = (bf16[2,2,2,64,512]{4,3,2,0,1:T(8,128)(2,1)}, bf16[2,2,2,64,512]{4,3,2,0,1:T(8,128)(2,1)}, u32[]{:S(2)}, u32[]{:S(2)}) collective-permute-start(bf16[2,2,2,64,512]{4,3,2,0,1:T(8,128)(2,1)} %fusion.33), channel_id=1, source_target_pairs={{0,1},{1,0},{2,3},{3,2},{4,5},{5,4},{6,7},{7,6},{8,9},{9,8},{10,11... | collective-permute-start | bytes 1572872 | tf_op jit(solution)/shard_map/ppermute | solution.py:16
  14.3 19.8 %collective-permute-start.6 = (bf16[2,2,2,64,512]{4,3,0,1,2:T(8,128)(2,1)}, bf16[2,2,2,64,512]{4,3,0,1,2:T(8,128)(2,1)}, u32[]{:S(2)}, u32[]{:S(2)}) collective-permute-start(bf16[2,2,2,64,512]{4,3,0,1,2:T(8,128)(2,1)} %fusion.32), channel_id=1, source_target_pairs={{0,1},{1,0},{2,3},{3,2},{4,5},{5,4},{6,7},{7,6},{8,9},{9,8},{10,11... | collective-permute-start | bytes 1572872 | tf_op jit(solution)/shard_map/ppermute | solution.py:16
  28.5 30.3 %collective-permute-start.1 = (bf16[4,256,256]{2,1,0:T(8,128)(2,1)S(1)}, bf16[4,256,256]{2,1,0:T(8,128)(2,1)S(1)}, u32[]{:S(2)}, u32[]{:S(2)}) collective-permute-start(bf16[4,256,256]{2,1,0:T(8,128)(2,1)S(1)} %get-tuple-element.23), channel_id=1, source_target_pairs={{0,2},{2,0},{1,3},{3,1},{4,6},{6,4},{5,7},{7,5},{8,10},{10,8},{9,1... | collective-permute-start | bytes 1572872 | tf_op jit(solution)/shard_map/ppermute | solution.py:16
  32.4 8.5 %collective-permute-start.11 = (bf16[2,2,64,512]{3,2,1,0:T(8,128)(2,1)S(1)}, bf16[2,2,64,512]{3,2,1,0:T(8,128)(2,1)S(1)}, u32[]{:S(2)}, u32[]{:S(2)}) collective-permute-start(bf16[2,2,64,512]{3,2,1,0:T(8,128)(2,1)S(1)} %fusion.37), channel_id=1, source_target_pairs={{0,4},{4,0},{1,5},{5,1},{2,6},{6,2},{3,7},{7,3},{8,12},{12,8},{9,1... | collective-permute-start | bytes 786440 | tf_op jit(solution)/shard_map/ppermute | solution.py:16
  35.3 14.0 %collective-permute-start.7 = (bf16[2,2,64,512]{3,2,0,1:T(8,128)(2,1)S(1)}, bf16[2,2,64,512]{3,2,0,1:T(8,128)(2,1)S(1)}, u32[]{:S(2)}, u32[]{:S(2)}) collective-permute-start(bf16[2,2,64,512]{3,2,0,1:T(8,128)(2,1)S(1)} %fusion.36), channel_id=1, source_target_pairs={{0,2},{2,0},{1,3},{3,1},{4,6},{6,4},{5,7},{7,5},{8,10},{10,8},{9,1... | collective-permute-start | bytes 786440 | tf_op jit(solution)/shard_map/ppermute | solution.py:16
  41.0 10.3 %collective-permute-start.12 = (bf16[2,64,512]{2,1,0:T(8,128)(2,1)S(1)}, bf16[2,64,512]{2,1,0:T(8,128)(2,1)S(1)}, u32[]{:S(2)}, u32[]{:S(2)}) collective-permute-start(bf16[2,64,512]{2,1,0:T(8,128)(2,1)S(1)} %fusion.42), channel_id=1, source_target_pairs={{0,8},{8,0},{1,9},{9,1},{2,10},{10,2},{3,11},{11,3},{4,12},{12,4},... | collective-permute-start | bytes 393224 | tf_op jit(solution)/shard_map/ppermute | solution.py:16
  49.4 5.4 %collective-permute-start.8 = (bf16[2,64,512]{2,1,0:T(8,128)(2,1)S(1)}, bf16[2,64,512]{2,1,0:T(8,128)(2,1)S(1)}, u32[]{:S(2)}, u32[]{:S(2)}) collective-permute-start(bf16[2,64,512]{2,1,0:T(8,128)(2,1)S(1)} %fusion.41), channel_id=1, source_target_pairs={{0,4},{4,0},{1,5},{5,1},{2,6},{6,2},{3,7},{7,3},{8,12},{12,8},{9,1... | collective-permute-start | bytes 393224 | tf_op jit(solution)/shard_map/ppermute | solution.py:16
  51.4 6.7 %collective-permute-start.13 = (bf16[64,512]{1,0:T(8,128)(2,1)S(1)}, bf16[64,512]{1,0:T(8,128)(2,1)S(1)}, u32[]{:S(2)}, u32[]{:S(2)}) collective-permute-start(bf16[64,512]{1,0:T(8,128)(2,1)S(1)} %fusion.47), channel_id=1, source_target_pairs={{0,2},{2,0},{1,3},{3,1},{4,6},{6,4},{5,7},{7,5},{8,10},{10,8},{9,1... | collective-permute-start | bytes 196616 | tf_op jit(solution)/shard_map/ppermute | solution.py:16
  55.5 43.5 %collective-permute-start.9 = (bf16[64,512]{1,0:T(8,128)(2,1)}, bf16[64,512]{1,0:T(8,128)(2,1)}, u32[]{:S(2)}, u32[]{:S(2)}) collective-permute-start(bf16[64,512]{1,0:T(8,128)(2,1)} %fusion.46), channel_id=1, source_target_pairs={{0,8},{8,0},{1,9},{9,1},{2,10},{10,2},{3,11},{11,3},{4,12},{12,4},... | collective-permute-start | bytes 196616 | tf_op jit(solution)/shard_map/ppermute | solution.py:16
  61.8 7.4 %collective-permute-start.2 = (bf16[1,256,256]{1,2,0:T(8,128)(2,1)S(1)}, bf16[1,256,256]{1,2,0:T(8,128)(2,1)S(1)}, u32[]{:S(2)}, u32[]{:S(2)}) collective-permute-start(bf16[1,256,256]{1,2,0:T(8,128)(2,1)S(1)} %get-tuple-element.20), channel_id=1, source_target_pairs={{0,4},{1,5},{2,6},{3,7},{4,8},{5,9},{6,10},{7,11},{8,12},{9,13},{1... | collective-permute-start | bytes 393224 | tf_op jit(solution)/shard_map/ppermute | solution.py:22
  65.3 6.9 %collective-permute-start.3 = (bf16[1,256,256]{1,2,0:T(8,128)(2,1)S(1)}, bf16[1,256,256]{1,2,0:T(8,128)(2,1)S(1)}, u32[]{:S(2)}, u32[]{:S(2)}) collective-permute-start(bf16[1,256,256]{1,2,0:T(8,128)(2,1)S(1)} %get-tuple-element.21), channel_id=1, source_target_pairs={{4,0},{5,1},{6,2},{7,3},{8,4},{9,5},{10,6},{11,7},{12,8},{13,9},{1... | collective-permute-start | bytes 393224 | tf_op jit(solution)/shard_map/ppermute | solution.py:22
  86.8 11.4 %collective-permute-start.14 = (bf16[2,2,2,64,288]{4,3,2,1,0:T(8,128)(2,1)}, bf16[2,2,2,64,288]{4,3,2,1,0:T(8,128)(2,1)S(1)}, u32[]{:S(2)}, u32[]{:S(2)}) collective-permute-start(bf16[2,2,2,64,288]{4,3,2,1,0:T(8,128)(2,1)} %fusion.35), channel_id=1, source_target_pairs={{0,1},{1,0},{2,3},{3,2},{4,5},{5,4},{6,7},{7,6},{8,9},{9,8},{10,11... | collective-permute-start | bytes 884744 | tf_op jit(solution)/shard_map/ppermute | solution.py:16
  96.7 18.3 %collective-permute-start.4 = (bf16[4,256,256]{2,1,0:T(8,128)(2,1)}, bf16[4,256,256]{2,1,0:T(8,128)(2,1)}, u32[]{:S(2)}, u32[]{:S(2)}) collective-permute-start(bf16[4,256,256]{2,1,0:T(8,128)(2,1)} %bitcast.50), channel_id=1, source_target_pairs={{0,2},{2,0},{1,3},{3,1},{4,6},{6,4},{5,7},{7,5},{8,10},{10,8},{9,1... | collective-permute-start | bytes 1572872 | tf_op jit(solution)/shard_map/ppermute | solution.py:16
  98.3 16.5 %collective-permute-start.15 = (bf16[2,2,64,288]{3,2,1,0:T(8,128)(2,1)S(1)}, bf16[2,2,64,288]{3,2,1,0:T(8,128)(2,1)S(1)}, u32[]{:S(2)}, u32[]{:S(2)}) collective-permute-start(bf16[2,2,64,288]{3,2,1,0:T(8,128)(2,1)S(1)} %fusion.40), channel_id=1, source_target_pairs={{0,2},{2,0},{1,3},{3,1},{4,6},{6,4},{5,7},{7,5},{8,10},{10,8},{9,1... | collective-permute-start | bytes 442376 | tf_op jit(solution)/shard_map/ppermute | solution.py:16
  114.9 4.7 %collective-permute-start.16 = (bf16[2,64,288]{2,1,0:T(8,128)(2,1)S(1)}, bf16[2,64,288]{2,1,0:T(8,128)(2,1)S(1)}, u32[]{:S(2)}, u32[]{:S(2)}) collective-permute-start(bf16[2,64,288]{2,1,0:T(8,128)(2,1)S(1)} %fusion.45), channel_id=1, source_target_pairs={{0,4},{4,0},{1,5},{5,1},{2,6},{6,2},{3,7},{7,3},{8,12},{12,8},{9,1... | collective-permute-start | bytes 221192 | tf_op jit(solution)/shard_map/ppermute | solution.py:16
  116.5 8.8 %collective-permute-start.5 = (bf16[4,128,2,256]{3,1,2,0:T(8,128)(2,1)S(1)}, bf16[4,128,2,256]{3,1,2,0:T(8,128)(2,1)S(1)}, u32[]{:S(2)}, u32[]{:S(2)}) collective-permute-start(bf16[4,128,2,256]{3,1,2,0:T(8,128)(2,1)S(1)} %bitcast.314), channel_id=1, source_target_pairs={{0,1},{1,0},{2,3},{3,2},{4,5},{5,4},{6,7},{7,6},{8,9},{9,8},{10,11... | collective-permute-start | bytes 1572872 | tf_op jit(solution)/shard_map/ppermute | solution.py:16
  119.7 5.1 %collective-permute-start.17 = (bf16[64,288]{1,0:T(8,128)(2,1)S(1)}, bf16[64,288]{1,0:T(8,128)(2,1)S(1)}, u32[]{:S(2)}, u32[]{:S(2)}) collective-permute-start(bf16[64,288]{1,0:T(8,128)(2,1)S(1)} %fusion.50), channel_id=1, source_target_pairs={{0,8},{8,0},{1,9},{9,1},{2,10},{10,2},{3,11},{11,3},{4,12},{12,4},... | collective-permute-start | bytes 110600 | tf_op jit(solution)/shard_map/ppermute | solution.py:16
  143.3 7.9 %collective-permute-start.23 = (bf16[2,2,64,512]{3,2,1,0:T(8,128)(2,1)S(1)}, bf16[2,2,64,512]{3,2,1,0:T(8,128)(2,1)S(1)}, u32[]{:S(2)}, u32[]{:S(2)}) collective-permute-start(bf16[2,2,64,512]{3,2,1,0:T(8,128)(2,1)S(1)} %fusion.39), channel_id=1, source_target_pairs={{0,4},{4,0},{1,5},{5,1},{2,6},{6,2},{3,7},{7,3},{8,12},{12,8},{9,1... | collective-permute-start | bytes 786440 | tf_op jit(solution)/shard_map/ppermute | solution.py:16
  143.6 8.1 %collective-permute-start.19 = (bf16[2,2,64,512]{3,2,0,1:T(8,128)(2,1)S(1)}, bf16[2,2,64,512]{3,2,0,1:T(8,128)(2,1)S(1)}, u32[]{:S(2)}, u32[]{:S(2)}) collective-permute-start(bf16[2,2,64,512]{3,2,0,1:T(8,128)(2,1)S(1)} %fusion.38), channel_id=1, source_target_pairs={{0,2},{2,0},{1,3},{3,1},{4,6},{6,4},{5,7},{7,5},{8,10},{10,8},{9,1... | collective-permute-start | bytes 786440 | tf_op jit(solution)/shard_map/ppermute | solution.py:16
  151.3 7.9 %collective-permute-start.24 = (bf16[2,64,512]{2,1,0:T(8,128)(2,1)S(1)}, bf16[2,64,512]{2,1,0:T(8,128)(2,1)S(1)}, u32[]{:S(2)}, u32[]{:S(2)}) collective-permute-start(bf16[2,64,512]{2,1,0:T(8,128)(2,1)S(1)} %fusion.44), channel_id=1, source_target_pairs={{0,8},{8,0},{1,9},{9,1},{2,10},{10,2},{3,11},{11,3},{4,12},{12,4},... | collective-permute-start | bytes 393224 | tf_op jit(solution)/shard_map/ppermute | solution.py:16
  151.8 9.0 %collective-permute-start.20 = (bf16[2,64,512]{2,1,0:T(8,128)(2,1)S(1)}, bf16[2,64,512]{2,1,0:T(8,128)(2,1)S(1)}, u32[]{:S(2)}, u32[]{:S(2)}) collective-permute-start(bf16[2,64,512]{2,1,0:T(8,128)(2,1)S(1)} %fusion.43), channel_id=1, source_target_pairs={{0,4},{4,0},{1,5},{5,1},{2,6},{6,2},{3,7},{7,3},{8,12},{12,8},{9,1... | collective-permute-start | bytes 393224 | tf_op jit(solution)/shard_map/ppermute | solution.py:16
  159.2 4.3 %collective-permute-start.25 = (bf16[64,512]{1,0:T(8,128)(2,1)S(1)}, bf16[64,512]{1,0:T(8,128)(2,1)S(1)}, u32[]{:S(2)}, u32[]{:S(2)}) collective-permute-start(bf16[64,512]{1,0:T(8,128)(2,1)S(1)} %fusion.49), channel_id=1, source_target_pairs={{0,2},{2,0},{1,3},{3,1},{4,6},{6,4},{5,7},{7,5},{8,10},{10,8},{9,1... | collective-permute-start | bytes 196616 | tf_op jit(solution)/shard_map/ppermute | solution.py:16
  160.8 5.2 %collective-permute-start.21 = (bf16[64,512]{1,0:T(8,128)(2,1)S(1)}, bf16[64,512]{1,0:T(8,128)(2,1)S(1)}, u32[]{:S(2)}, u32[]{:S(2)}) collective-permute-start(bf16[64,512]{1,0:T(8,128)(2,1)S(1)} %fusion.48), channel_id=1, source_target_pairs={{0,8},{8,0},{1,9},{9,1},{2,10},{10,2},{3,11},{11,3},{4,12},{12,4},... | collective-permute-start | bytes 196616 | tf_op jit(solution)/shard_map/ppermute | solution.py:16
  (41 other events, 122.9 us)

commit v2 on v1

v2 whole, which is shorter than its diff:
```python
import functools
import math

import jax
import jax.numpy as jnp
from jax import lax
from jax.experimental import pallas as pl
from jax.experimental.pallas import tpu as pltpu
from jax.sharding import PartitionSpec as P


def partner(block, axis, distance):
    count = lax.axis_size(axis)
    route = []
    for low in range(count):
        high = low | 1 << distance
        if high != low and high < count:
            route += [(low, high), (high, low)]
    return lax.ppermute(block, axis, route)


def from_behind(array, axis, by):
    count = lax.axis_size(axis)
    pairs = [(i, i + by) for i in range(count) if 0 <= i + by < count]
    return lax.ppermute(array, axis, pairs)


def halve(piece, order, bits):
    position = lax.axis_index("space")
    left = list(range(bits))[::-1]
    for bit in order:
        axis = left.index(bit)
        mine = position // (1 << bit) % 2
        sent = lax.dynamic_index_in_dim(piece, 1 - mine, axis, keepdims=False)
        kept = lax.dynamic_index_in_dim(piece, mine, axis, keepdims=False)
        received = partner(sent.astype(jnp.bfloat16), "space", bit)
        piece = kept + received.astype(jnp.float32)
        left.remove(bit)
    return piece


def sum_shards(terms):
    devices = lax.axis_size("space")
    bits = devices.bit_length() - 1
    low_first = list(range(bits))
    high_first = [0] + list(range(2, bits)) + [1]
    done = []
    for at, term in enumerate(terms):
        rows, columns = term.shape
        view = term.reshape((2,) * bits + (rows // devices, columns))
        done.append(halve(view, (low_first, high_first)[at % 2], bits))
    return done[0] if len(done) == 1 else jnp.concatenate(done, -1)


def to_tiles(block, col_parity, row_parity, row_bit):
    double_rows, double_cols, shard_width = block.shape
    tile_rows = double_rows // 2
    tile_width = double_cols // 2
    split = block.reshape(2, tile_rows, double_cols, shard_width)
    kept_part = lax.dynamic_index_in_dim(split, row_parity, 0, keepdims=False)
    sent_part = lax.dynamic_index_in_dim(split, 1 - row_parity, 0, keepdims=False)
    received = partner(sent_part, "space", row_bit)
    joined = jnp.where(
        row_parity == 0, jnp.stack([kept_part, received], 2), jnp.stack([received, kept_part], 2)
    )
    joined = joined.reshape(tile_rows, 2, tile_width, 2, shard_width)
    kept_cols = lax.dynamic_index_in_dim(joined, col_parity, 1, keepdims=False)
    sent_cols = lax.dynamic_index_in_dim(joined, 1 - col_parity, 1, keepdims=False)
    received_cols = partner(sent_cols, "space", 0)
    stacked = jnp.where(
        col_parity == 0,
        jnp.stack([kept_cols, received_cols], 3),
        jnp.stack([received_cols, kept_cols], 3),
    )
    return stacked.reshape(tile_rows, tile_width, 4 * shard_width)


def group_kernel(
    tile_rows, width, group_width, normalizer,
    inner_ref, top_ref, bottom_ref, left_ref, right_ref, second_ref, weight_ref,
    first_ref, wgrad_ref, shifted, flipped,
):
    channels = inner_ref.shape[1]
    column = lax.broadcasted_iota(jnp.int32, (width, channels), 0)
    left = left_ref[...]
    right = right_ref[...]
    for y in range(tile_rows + 2):
        if y == 0:
            piece = top_ref[...]
        elif y == tile_rows + 1:
            piece = bottom_ref[...]
        else:
            piece = inner_ref[(y - 1) * width : y * width, :]
        wide = piece.astype(jnp.float32)
        before = jnp.where(column == width - 1, right[y : y + 1], pltpu.roll(wide, width - 1, 0))
        after = jnp.where(column == 0, left[y : y + 1], pltpu.roll(wide, 1, 0))
        for at, moved in enumerate((before, wide, after)):
            shifted[at, y * width : (y + 1) * width, :] = moved.astype(jnp.bfloat16)
            flipped[at, :, y * width : (y + 1) * width] = moved.T.astype(jnp.bfloat16)
    lanes = 128
    per = lanes // group_width
    own = (
        lax.broadcasted_iota(jnp.int32, (channels, channels), 0) // group_width
        == lax.broadcasted_iota(jnp.int32, (channels, channels), 1) // group_width
    )
    lane_group = lax.broadcasted_iota(jnp.int32, (channels, lanes), 1) // group_width

    def spread(array):
        step = group_width
        while step < lanes:
            array = array + pltpu.roll(array, step, 1)
            step *= 2
        return array

    second = second_ref[...]
    size = tile_rows * width
    back = jnp.zeros((size, channels), jnp.float32)
    row = None
    for tap in range(9):
        u, v = tap // 3 - 1, tap % 3 - 1
        start = (1 - u) * width
        chunk, slot = tap // per, tap % per
        if tap < 8:
            taps = weight_ref[:, chunk * lanes : (chunk + 1) * lanes].astype(jnp.float32)
            taps = jnp.where(lane_group == slot, taps, 0.0)
        else:
            taps = weight_ref[:, 8 * group_width : 9 * group_width].astype(jnp.float32)
            taps = jnp.concatenate(
                [taps, jnp.zeros((channels, lanes - group_width), jnp.float32)], 1
            )
        taps = spread(taps)
        dense = jnp.concatenate([taps] * (channels // lanes), 1)
        dense = jnp.where(own, dense, 0.0).astype(jnp.bfloat16)
        back = back + jnp.dot(
            shifted[v + 1, start : start + size, :], dense, preferred_element_type=jnp.float32
        )
        term = jnp.dot(
            flipped[v + 1, :, start : start + size], second, preferred_element_type=jnp.float32
        )
        term = jnp.where(own, term, 0.0)
        folded = term[:, :lanes]
        for at in range(1, channels // lanes):
            folded = folded + term[:, at * lanes : (at + 1) * lanes]
        folded = spread(folded) * normalizer
        row = folded if slot == 0 else jnp.where(lane_group == slot, folded, row)
        if slot == per - 1:
            wgrad_ref[:, chunk * lanes : (chunk + 1) * lanes] = row
        elif tap == 8:
            wgrad_ref[:, 8 * group_width : 9 * group_width] = row[:, :group_width]
    first_ref[...] = jnp.where(second > 0, back, 0.0).astype(jnp.bfloat16)


def group_backward(inner, top, bottom, left, right, second, weight, tile_rows, normalizer):
    size, channels = inner.shape
    width = size // tile_rows
    taps = weight.shape[1]
    block = 256
    tall = tile_rows + 2

    def by_channels(rows):
        return pl.BlockSpec((rows, block), lambda at: (0, at))

    by_rows = pl.BlockSpec((block, taps), lambda at: (at, 0))
    return pl.pallas_call(
        functools.partial(group_kernel, tile_rows, width, taps // 9, normalizer),
        grid=(channels // block,),
        in_specs=[
            by_channels(size),
            by_channels(width),
            by_channels(width),
            by_channels(tall),
            by_channels(tall),
            by_channels(size),
            by_rows,
        ],
        out_specs=[by_channels(size), by_rows],
        out_shape=[
            jax.ShapeDtypeStruct((size, channels), jnp.bfloat16),
            jax.ShapeDtypeStruct((channels, taps), jnp.float32),
        ],
        scratch_shapes=[
            pltpu.VMEM((3, tall * width, block), jnp.bfloat16),
            pltpu.VMEM((3, block, tall * width), jnp.bfloat16),
        ],
        compiler_params=pltpu.CompilerParams(vmem_limit_bytes=32 * 2**20),
        cost_estimate=pl.CostEstimate(
            flops=36 * size * block * channels, bytes_accessed=8 * size * channels, transcendentals=0
        ),
    )(inner, top, bottom, left, right, second, weight)


def per_device(
    outer_grad, block_input, third_input, second_input, third_weight, group_weight, first_weight
):
    devices = lax.axis_size("space")
    position = lax.axis_index("space")
    row_bit = 1
    col_parity = position % 2
    row_parity = position // 2 % 2
    tile_rows = outer_grad.shape[1]
    tile_width = outer_grad.shape[2]
    channels = outer_grad.shape[3]
    normalizer = 1.0 / math.sqrt(tile_rows * tile_width * devices)
    grad_rows = outer_grad.reshape(tile_rows * tile_width, channels)
    third_rows = third_input.reshape(tile_rows * tile_width, channels)
    input_rows = block_input.reshape(tile_rows * tile_width, channels)
    back_third = lax.dot_general(
        grad_rows, third_weight, (((1,), (1,)), ((), ())), preferred_element_type=jnp.float32
    )
    inner_grad = jnp.where(third_rows > 0, back_third, 0.0).astype(jnp.bfloat16)
    half = channels // 2
    inner_tile = inner_grad.reshape(tile_rows, tile_width, channels)
    top = from_behind(inner_tile[-1:], "space", 2)
    bottom = from_behind(inner_tile[:1], "space", -2)

    def edge(tile):
        return jnp.where(col_parity == 0, tile[:, -1], tile[:, 0])

    rims = partner(
        jnp.concatenate([edge(top), edge(inner_tile), edge(bottom)], 0), "space", 0
    ).astype(jnp.float32)
    left = jnp.where(col_parity == 1, rims, 0.0)
    right = jnp.where(col_parity == 0, rims, 0.0)
    second_tile = to_tiles(second_input[0], col_parity, row_parity, row_bit)
    first_rows, local_term = group_backward(
        inner_grad,
        top[0],
        bottom[0],
        left,
        right,
        second_tile.reshape(tile_rows * tile_width, channels),
        group_weight,
        tile_rows,
        normalizer,
    )

    def half_terms(rows, columns):
        return [
            lax.dot_general(
                rows,
                columns[:, at : at + half],
                (((0,), (0,)), ((), ())),
                preferred_element_type=jnp.float32,
            )
            * normalizer
            for at in (0, half)
        ]

    third_wgrad = sum_shards(half_terms(third_rows, grad_rows))
    group_wgrad = sum_shards([local_term])
    summed = lax.dot_general(
        first_rows, first_weight, (((1,), (1,)), ((), ())), preferred_element_type=jnp.float32
    )
    input_grad = (
        (summed + grad_rows.astype(jnp.float32))
        .astype(jnp.bfloat16)
        .reshape(1, tile_rows, tile_width, channels)
    )
    first_wgrad = sum_shards(half_terms(input_rows, first_rows))
    return (input_grad, third_wgrad, group_wgrad, first_wgrad)


def solution(mesh):
    in_specs = (
        P(("parts", "space"), None, None, None),
        P(("parts", "space"), None, None, None),
        P(("parts", "space"), None, None, None),
        P(("parts", "space"), None, None, None),
        P(),
        P(),
        P(),
    )
    out_specs = (
        P(("parts", "space"), None, None, None),
        P(("parts", "space"), None),
        P(("parts", "space"), None),
        P(("parts", "space"), None),
    )
    return jax.shard_map(
        per_device, mesh=mesh, in_specs=in_specs, out_specs=out_specs, check_vma=False
    )
```

time: 168 us -> 130 us (0.77)
  waiting for transfers between devices: 53.7 us -> 31 us
  local copies, waits for them, and re-layouts: 46.5 us -> 27.8 us
  Pallas kernels: 0 us -> 10.9 us
  other arithmetic: 15.1 us -> 8.13 us
  starting transfers between devices: 28.2 us -> 34.3 us
  matrix products: 21.6 us -> 16.2 us
    ppermute x24 -> x23, waiting for transfers between devices: 50.7 us -> 31 us  [partner(): return lax.ppermute(block, axis, route)]
    pallas_call x0 -> x1, Pallas kernels: none -> 10.9 us  [group_backward(): pl.pallas_call(functools.partial(group_kernel, tile_rows, width, taps //...]
    dynamic_slice x4 -> x0, local copies, waits for them, and re-layouts: 6.89 us -> none  [the longest x1 2.81 us: halve(): kept = lax.dynamic_index_in_dim(piece, mine, axis, keepdims=False)]
    slice x5 -> x2, local copies, waits for them, and re-layouts: 6.84 us -> 0.91 us  [the longest x1 0.88 us: per_device(): bottom = from_behind(inner_tile[:1], 'space', -2)]
    dot_general x20 -> x4, matrix products: 16.8 us -> 11.1 us  [half_terms(): lax.dot_general(rows, columns[:, at:at + half], (((0,), (0,)), ((), ())),...]
    unnamed x81 -> x23, local copies, waits for them, and re-layouts: 11.8 us -> 7.53 us
    gt x2 -> x0, other arithmetic: 3.93 us -> none  [the longest x1 2.29 us: per_device(): second_block > 0]
    convert_element_type x20, local copies, waits for them, and re-layouts: 3.73 us -> 7.21 us  [halve(): received = partner(sent.astype(jnp.bfloat16), 'space', bit)]
  transfers between devices with their start and end apart: 26 -> 25, of which waited for: 11 -> 11; matrix products, arithmetic and copies ran while one was open for 31% -> 30% of each run, Pallas kernels for 0% -> 0%
where the time goes in v2:
time: 130 us; the launch traced here: 129 us
  starting transfers between devices  34.3 us (26%)
  waiting for transfers between devices  31 us (24%)
  local copies, waits for them, and re-layouts  27.8 us (21%)
  matrix products  16.2 us (12%)
  Pallas kernels  10.9 us (8%)
  other arithmetic  8.13 us (6%)
    ppermute x23, waiting for transfers between devices, partner(): return lax.ppermute(block, axis, route)  31 us
    ppermute x23, starting transfers between devices, partner(): return lax.ppermute(block, axis, route)  26.8 us
    dot_general x4, matrix products, half_terms(): lax.dot_general(rows, columns[:, at:at + half], (((0,), (0,)), ((), ())),...  11.1 us
    pallas_call x1, Pallas kernels, group_backward(): pl.pallas_call(functools.partial(group_kernel, tile_rows, width, taps //...  10.9 us
    unnamed x23, local copies, waits for them, and re-layouts  7.53 us
    ppermute x2, starting transfers between devices, from_behind(): return lax.ppermute(array, axis, pairs)  7.5 us
    convert_element_type x20, local copies, waits for them, and re-layouts, halve(): received = partner(sent.astype(jnp.bfloat16), 'space', bit)  7.21 us
    mul x2, local copies, waits for them, and re-layouts, half_terms(): lax.dot_general(rows, columns[:, at:at + half], (((0,), (0,)), ((), ())),...  5.86 us
  transfers between devices with their start and end apart: 25, of which 11 were waited for; matrix products, arithmetic and copies ran while one was open for 30% of the time, Pallas kernels for 0%

profile of v2, /device:TPU:0, one launch (start us, length us, event | category | flops | bytes accessed | tf_op | source)
XLA Modules:
  0.0 129.5 jit_solution(16245023766229752773)
XLA Ops:
  2.2 2.8 %select_convert_fusion.inner_ref = bf16[512,1024]{1,0:T(8,128)(2,1)S(1)} fusion(bf16[512,1024]{1,0:T(8,128)(2,1)} %bitcast.145, bf16[512,1024]{1,0:T(8,128)(2,1)} %bitcast.148, bf16[1024,1024]{1,0:T(8,128)(2,1)S(1)} %copy-done), kind=kOutput, calls=%fused_computation.3 | convolution fusion | flops 1075314688 | bytes 5242880 | tf_op jit(solution)/shard_map/dot_general | solution.py:207
  7.2 6.2 %collective-permute-start = (bf16[1,128,1024]{2,1,0:T(8,128)(2,1)}, bf16[1,128,1024]{2,1,0:T(8,128)(2,1)}, u32[]{:S(2)}, u32[]{:S(2)}) collective-permute-start(bf16[1,128,1024]{2,1,0:T(8,128)(2,1)} %get-tuple-element.15), channel_id=1, source_target_pairs={{0,2},{1,3},{2,4},{3,5},{4,6},{5,7},{6,8},{7,9},{8,10},{9,11},{10,... | collective-permute-start | bytes 786440 | tf_op jit(solution)/shard_map/ppermute | solution.py:25
  13.5 2.3 %constant_dynamic-slice_fusion.10 = (bf16[1,4,256,256]{3,2,1,0:T(8,128)(2,1)}, bf16[4,256,256]{2,1,0:T(8,128)(2,1)}) fusion(bf16[2,4,256,256]{3,2,1,0:T(8,128)(2,1)} %bitcast.142, s32[]{:T(128)S(6)} %select_n.257, s32[]{:T(128)S(6)} %select_n.258), kind=kLoop, calls=%fused_computation.92 | loop fusion | bytes 2097160 | tf_op jit(solution)/shard_map/jit(dynamic_index_in_dim)/dynamic_slice | solution.py:60
  15.7 2.2 %collective-permute-start.3 = (bf16[4,256,256]{2,1,0:T(8,128)(2,1)}, bf16[4,256,256]{2,1,0:T(8,128)(2,1)}, u32[]{:S(2)}, u32[]{:S(2)}) collective-permute-start(bf16[4,256,256]{2,1,0:T(8,128)(2,1)} %get-tuple-element.11), channel_id=1, source_target_pairs={{0,2},{2,0},{1,3},{3,1},{4,6},{6,4},{5,7},{7,5},{8,10},{10,8},{9,1... | collective-permute-start | bytes 1572872 | tf_op jit(solution)/shard_map/ppermute | solution.py:19
  17.9 3.5 %convolution_multiply_fusion = f32[1024,512]{1,0:T(8,128)} fusion(bf16[512,1024]{1,0:T(8,128)(2,1)} %bitcast.146, bf16[512,1024]{1,0:T(8,128)(2,1)} %bitcast.149), kind=kOutput, calls=%fused_computation.4 | convolution fusion | flops 537395200 | bytes 3670016 | tf_op jit(solution)/shard_map/dot_general | solution.py:239
  23.5 3.4 %convolution_multiply_fusion.1 = f32[1024,512]{1,0:T(8,128)} fusion(bf16[512,1024]{1,0:T(8,128)(2,1)} %bitcast.147, bf16[512,1024]{1,0:T(8,128)(2,1)} %bitcast.150), kind=kOutput, calls=%fused_computation.5 | convolution fusion | flops 537395200 | bytes 3670016 | tf_op jit(solution)/shard_map/dot_general | solution.py:239
  29.8 2.3 %copy.42.weight_ref = bf16[1024,288]{1,0:T(8,128)(2,1)} copy(bf16[1024,288]{0,1:T(8,128)(2,1)} %param.12) | data formatting | bytes 1179648 | tf_op args[5]
  32.1 2.3 %collective-permute-done.3 = bf16[4,256,256]{2,1,0:T(8,128)(2,1)} collective-permute-done((bf16[4,256,256]{2,1,0:T(8,128)(2,1)}, bf16[4,256,256]{2,1,0:T(8,128)(2,1)}, u32[]{:S(2)}, u32[]{:S(2)}) %collective-permute-start.3) | collective-permute-done | bytes 524320 | tf_op jit(solution)/shard_map/ppermute | solution.py:19
  41.0 2.5 %collective-permute-start.6 = (bf16[2,2,64,512]{3,2,0,1:T(8,128)(2,1)S(1)}, bf16[2,2,64,512]{3,2,0,1:T(8,128)(2,1)S(1)}, u32[]{:S(2)}, u32[]{:S(2)}) collective-permute-start(bf16[2,2,64,512]{3,2,0,1:T(8,128)(2,1)S(1)} %fusion.9), channel_id=1, source_target_pairs={{0,2},{2,0},{1,3},{3,1},{4,6},{6,4},{5,7},{7,5},{8,10},{10,8},{9,1... | collective-permute-start | bytes 786440 | tf_op jit(solution)/shard_map/ppermute | solution.py:19
  43.4 3.9 %collective-permute-done.10 = bf16[2,2,64,512]{3,2,1,0:T(8,128)(2,1)S(1)} collective-permute-done((bf16[2,2,64,512]{3,2,1,0:T(8,128)(2,1)S(1)}, bf16[2,2,64,512]{3,2,1,0:T(8,128)(2,1)S(1)}, u32[]{:S(2)}, u32[]{:S(2)}) %collective-permute-start.10) | collective-permute-done | bytes 262176 | tf_op jit(solution)/shard_map/ppermute | solution.py:19
  47.4 2.7 %collective-permute-start.11 = (bf16[2,64,512]{2,1,0:T(8,128)(2,1)S(1)}, bf16[2,64,512]{2,1,0:T(8,128)(2,1)S(1)}, u32[]{:S(2)}, u32[]{:S(2)}) collective-permute-start(bf16[2,64,512]{2,1,0:T(8,128)(2,1)S(1)} %fusion.15), channel_id=1, source_target_pairs={{0,8},{8,0},{1,9},{9,1},{2,10},{10,2},{3,11},{11,3},{4,12},{12,4},... | collective-permute-start | bytes 393224 | tf_op jit(solution)/shard_map/ppermute | solution.py:19
  51.1 4.8 %collective-permute-done.11 = bf16[2,64,512]{2,1,0:T(8,128)(2,1)S(1)} collective-permute-done((bf16[2,64,512]{2,1,0:T(8,128)(2,1)S(1)}, bf16[2,64,512]{2,1,0:T(8,128)(2,1)S(1)}, u32[]{:S(2)}, u32[]{:S(2)}) %collective-permute-start.11) | collective-permute-done | bytes 131104 | tf_op jit(solution)/shard_map/ppermute | solution.py:19
  55.9 2.5 %collective-permute-start.12 = (bf16[64,512]{1,0:T(8,128)(2,1)S(1)}, bf16[64,512]{1,0:T(8,128)(2,1)S(1)}, u32[]{:S(2)}, u32[]{:S(2)}) collective-permute-start(bf16[64,512]{1,0:T(8,128)(2,1)S(1)} %fusion.20), channel_id=1, source_target_pairs={{0,2},{2,0},{1,3},{3,1},{4,6},{6,4},{5,7},{7,5},{8,10},{10,8},{9,1... | collective-permute-start | bytes 196616 | tf_op jit(solution)/shard_map/ppermute | solution.py:19
  60.7 3.4 %collective-permute-done.8 = bf16[64,512]{1,0:T(8,128)(2,1)S(1)} collective-permute-done((bf16[64,512]{1,0:T(8,128)(2,1)S(1)}, bf16[64,512]{1,0:T(8,128)(2,1)S(1)}, u32[]{:S(2)}, u32[]{:S(2)}) %collective-permute-start.8) | collective-permute-done | bytes 65568 | tf_op jit(solution)/shard_map/ppermute | solution.py:19
  71.1 10.9 %shard_map.102 = (bf16[512,1024]{1,0:T(8,128)(2,1)S(1)}, f32[1024,288]{1,0:T(8,128)S(1)}) custom-call(bf16[512,1024]{1,0:T(8,128)(2,1)S(1)} %copy-done.3, bf16[128,1024]{1,0:T(8,128)(2,1)} %bitcast.3.top_ref, bf16[128,1024]{1,0:T(8,128)(2,1)S(1)} %bitcast.129, f32[6,1024]{1,0:T(8,128)S(1)} %get-tuple-element.17.left_ref, ...), custom_call_target="tpu_custom_call" | custom-call | flops 4831838208 | bytes 4194304 | tf_op jit(solution)/shard_map/pallas_call | solution.py:164
  82.3 2.3 %add_convert_fusion = bf16[512,1024]{1,0:T(8,128)(2,1)} fusion(bf16[512,1024]{1,0:T(8,128)(2,1)S(1)} %bitcast.151, bf16[512,1024]{1,0:T(8,128)(2,1)S(1)} %get-tuple-element.6, bf16[1024,1024]{1,0:T(8,128)(2,1)S(1)} %copy-done.9), kind=kOutput, calls=%fused_computation.2 | convolution fusion | flops 1075314688 | bytes 5242880 | tf_op jit(solution)/shard_map/dot_general | solution.py:251
  84.5 2.1 %multiply_bitcast_fusion = f32[1024,512]{0,1:T(8,128)} fusion(bf16[512,1024]{1,0:T(8,128)(2,1)S(1)} %bitcast.134, bf16[512,1024]{1,0:T(8,128)(2,1)S(1)} %get-tuple-element.6), kind=kOutput, calls=%fused_computation | convolution fusion | flops 537395200 | bytes 3670016 | tf_op jit(solution)/shard_map/dot_general | solution.py:239
  89.0 2.9 %copy.50 = f32[1024,512]{1,0:T(8,128)} copy(f32[1024,512]{0,1:T(8,128)} %multiply_bitcast_fusion) | data formatting | bytes 4194304 | tf_op jit(solution)/shard_map/mul | solution.py:239
  94.4 2.9 %copy.49 = f32[1024,512]{1,0:T(8,128)} copy(f32[1024,512]{0,1:T(8,128)} %multiply_bitcast_fusion.1) | data formatting | bytes 4194304 | tf_op jit(solution)/shard_map/mul | solution.py:239
  99.8 2.4 %collective-permute-done.15 = bf16[2,64,288]{2,1,0:T(8,128)(2,1)S(1)} collective-permute-done((bf16[2,64,288]{2,1,0:T(8,128)(2,1)S(1)}, bf16[2,64,288]{2,1,0:T(8,128)(2,1)S(1)}, u32[]{:S(2)}, u32[]{:S(2)}) %collective-permute-start.15) | collective-permute-done | bytes 73760 | tf_op jit(solution)/shard_map/ppermute | solution.py:19
  109.7 3.3 %collective-permute-done.22 = bf16[2,2,64,512]{3,2,1,0:T(8,128)(2,1)S(1)} collective-permute-done((bf16[2,2,64,512]{3,2,1,0:T(8,128)(2,1)S(1)}, bf16[2,2,64,512]{3,2,1,0:T(8,128)(2,1)S(1)}, u32[]{:S(2)}, u32[]{:S(2)}) %collective-permute-start.22) | collective-permute-done | bytes 262176 | tf_op jit(solution)/shard_map/ppermute | solution.py:19
  116.1 4.7 %collective-permute-done.23 = bf16[2,64,512]{2,1,0:T(8,128)(2,1)S(1)} collective-permute-done((bf16[2,64,512]{2,1,0:T(8,128)(2,1)S(1)}, bf16[2,64,512]{2,1,0:T(8,128)(2,1)S(1)}, u32[]{:S(2)}, u32[]{:S(2)}) %collective-permute-start.23) | collective-permute-done | bytes 131104 | tf_op jit(solution)/shard_map/ppermute | solution.py:19
  120.9 2.5 %collective-permute-start.24 = (bf16[64,512]{1,0:T(8,128)(2,1)S(1)}, bf16[64,512]{1,0:T(8,128)(2,1)S(1)}, u32[]{:S(2)}, u32[]{:S(2)}) collective-permute-start(bf16[64,512]{1,0:T(8,128)(2,1)S(1)} %fusion.22), channel_id=1, source_target_pairs={{0,2},{2,0},{1,3},{3,1},{4,6},{6,4},{5,7},{7,5},{8,10},{10,8},{9,1... | collective-permute-start | bytes 196616 | tf_op jit(solution)/shard_map/ppermute | solution.py:19
  125.7 3.0 %collective-permute-done.20 = bf16[64,512]{1,0:T(8,128)(2,1)S(1)} collective-permute-done((bf16[64,512]{1,0:T(8,128)(2,1)S(1)}, bf16[64,512]{1,0:T(8,128)(2,1)S(1)}, u32[]{:S(2)}, u32[]{:S(2)}) %collective-permute-start.20) | collective-permute-done | bytes 65568 | tf_op jit(solution)/shard_map/ppermute | solution.py:19
  (115 shorter events, 46.5 us)
Async XLA Ops:
  6.0 21.0 %collective-permute-start.1 = (bf16[1,128,1024]{2,1,0:T(8,128)(2,1)}, bf16[1,128,1024]{2,1,0:T(8,128)(2,1)S(1)}, u32[]{:S(2)}, u32[]{:S(2)}) collective-permute-start(bf16[1,128,1024]{2,1,0:T(8,128)(2,1)} %get-tuple-element.14), channel_id=1, source_target_pairs={{2,0},{3,1},{4,2},{5,3},{6,4},{7,5},{8,6},{9,7},{10,8},{11,9},{12,... | collective-permute-start | bytes 786440 | tf_op jit(solution)/shard_map/ppermute | solution.py:25
  7.2 19.8 %collective-permute-start = (bf16[1,128,1024]{2,1,0:T(8,128)(2,1)}, bf16[1,128,1024]{2,1,0:T(8,128)(2,1)}, u32[]{:S(2)}, u32[]{:S(2)}) collective-permute-start(bf16[1,128,1024]{2,1,0:T(8,128)(2,1)} %get-tuple-element.15), channel_id=1, source_target_pairs={{0,2},{1,3},{2,4},{3,5},{4,6},{5,7},{6,8},{7,9},{8,10},{9,11},{10,... | collective-permute-start | bytes 786440 | tf_op jit(solution)/shard_map/ppermute | solution.py:25
  15.7 18.7 %collective-permute-start.3 = (bf16[4,256,256]{2,1,0:T(8,128)(2,1)}, bf16[4,256,256]{2,1,0:T(8,128)(2,1)}, u32[]{:S(2)}, u32[]{:S(2)}) collective-permute-start(bf16[4,256,256]{2,1,0:T(8,128)(2,1)} %get-tuple-element.11), channel_id=1, source_target_pairs={{0,2},{2,0},{1,3},{3,1},{4,6},{6,4},{5,7},{7,5},{8,10},{10,8},{9,1... | collective-permute-start | bytes 1572872 | tf_op jit(solution)/shard_map/ppermute | solution.py:19
  23.5 12.9 %collective-permute-start.9 = (bf16[2,2,2,64,512]{4,3,2,0,1:T(8,128)(2,1)}, bf16[2,2,2,64,512]{4,3,2,0,1:T(8,128)(2,1)}, u32[]{:S(2)}, u32[]{:S(2)}) collective-permute-start(bf16[2,2,2,64,512]{4,3,2,0,1:T(8,128)(2,1)} %fusion.2), channel_id=1, source_target_pairs={{0,1},{1,0},{2,3},{3,2},{4,5},{5,4},{6,7},{7,6},{8,9},{9,8},{10,11... | collective-permute-start | bytes 1572872 | tf_op jit(solution)/shard_map/ppermute | solution.py:19
  29.7 11.1 %collective-permute-start.5 = (bf16[2,2,2,64,512]{4,3,0,1,2:T(8,128)(2,1)S(1)}, bf16[2,2,2,64,512]{4,3,0,1,2:T(8,128)(2,1)S(1)}, u32[]{:S(2)}, u32[]{:S(2)}) collective-permute-start(bf16[2,2,2,64,512]{4,3,0,1,2:T(8,128)(2,1)S(1)} %fusion.1), channel_id=1, source_target_pairs={{0,1},{1,0},{2,3},{3,2},{4,5},{5,4},{6,7},{7,6},{8,9},{9,8},{10,11... | collective-permute-start | bytes 1572872 | tf_op jit(solution)/shard_map/ppermute | solution.py:19
  36.3 28.5 %collective-permute-start.4 = (bf16[4,128,2,256]{3,1,2,0:T(8,128)(2,1)S(1)}, bf16[4,128,2,256]{3,1,2,0:T(8,128)(2,1)S(1)}, u32[]{:S(2)}, u32[]{:S(2)}) collective-permute-start(bf16[4,128,2,256]{3,1,2,0:T(8,128)(2,1)S(1)} %bitcast.144), channel_id=1, source_target_pairs={{0,1},{1,0},{2,3},{3,2},{4,5},{5,4},{6,7},{7,6},{8,9},{9,8},{10,11... | collective-permute-start | bytes 1572872 | tf_op jit(solution)/shard_map/ppermute | solution.py:19
  39.0 8.3 %collective-permute-start.10 = (bf16[2,2,64,512]{3,2,1,0:T(8,128)(2,1)S(1)}, bf16[2,2,64,512]{3,2,1,0:T(8,128)(2,1)S(1)}, u32[]{:S(2)}, u32[]{:S(2)}) collective-permute-start(bf16[2,2,64,512]{3,2,1,0:T(8,128)(2,1)S(1)} %fusion.10), channel_id=1, source_target_pairs={{0,4},{4,0},{1,5},{5,1},{2,6},{6,2},{3,7},{7,3},{8,12},{12,8},{9,1... | collective-permute-start | bytes 786440 | tf_op jit(solution)/shard_map/ppermute | solution.py:19
  41.0 9.1 %collective-permute-start.6 = (bf16[2,2,64,512]{3,2,0,1:T(8,128)(2,1)S(1)}, bf16[2,2,64,512]{3,2,0,1:T(8,128)(2,1)S(1)}, u32[]{:S(2)}, u32[]{:S(2)}) collective-permute-start(bf16[2,2,64,512]{3,2,0,1:T(8,128)(2,1)S(1)} %fusion.9), channel_id=1, source_target_pairs={{0,2},{2,0},{1,3},{3,1},{4,6},{6,4},{5,7},{7,5},{8,10},{10,8},{9,1... | collective-permute-start | bytes 786440 | tf_op jit(solution)/shard_map/ppermute | solution.py:19
  47.4 8.5 %collective-permute-start.11 = (bf16[2,64,512]{2,1,0:T(8,128)(2,1)S(1)}, bf16[2,64,512]{2,1,0:T(8,128)(2,1)S(1)}, u32[]{:S(2)}, u32[]{:S(2)}) collective-permute-start(bf16[2,64,512]{2,1,0:T(8,128)(2,1)S(1)} %fusion.15), channel_id=1, source_target_pairs={{0,8},{8,0},{1,9},{9,1},{2,10},{10,2},{3,11},{11,3},{4,12},{12,4},... | collective-permute-start | bytes 393224 | tf_op jit(solution)/shard_map/ppermute | solution.py:19
  50.2 8.2 %collective-permute-start.7 = (bf16[2,64,512]{2,1,0:T(8,128)(2,1)S(1)}, bf16[2,64,512]{2,1,0:T(8,128)(2,1)S(1)}, u32[]{:S(2)}, u32[]{:S(2)}) collective-permute-start(bf16[2,64,512]{2,1,0:T(8,128)(2,1)S(1)} %fusion.14), channel_id=1, source_target_pairs={{0,4},{4,0},{1,5},{5,1},{2,6},{6,2},{3,7},{7,3},{8,12},{12,8},{9,1... | collective-permute-start | bytes 393224 | tf_op jit(solution)/shard_map/ppermute | solution.py:19
  55.9 4.7 %collective-permute-start.12 = (bf16[64,512]{1,0:T(8,128)(2,1)S(1)}, bf16[64,512]{1,0:T(8,128)(2,1)S(1)}, u32[]{:S(2)}, u32[]{:S(2)}) collective-permute-start(bf16[64,512]{1,0:T(8,128)(2,1)S(1)} %fusion.20), channel_id=1, source_target_pairs={{0,2},{2,0},{1,3},{3,1},{4,6},{6,4},{5,7},{7,5},{8,10},{10,8},{9,1... | collective-permute-start | bytes 196616 | tf_op jit(solution)/shard_map/ppermute | solution.py:19
  58.5 5.6 %collective-permute-start.8 = (bf16[64,512]{1,0:T(8,128)(2,1)S(1)}, bf16[64,512]{1,0:T(8,128)(2,1)S(1)}, u32[]{:S(2)}, u32[]{:S(2)}) collective-permute-start(bf16[64,512]{1,0:T(8,128)(2,1)S(1)} %fusion.19), channel_id=1, source_target_pairs={{0,8},{8,0},{1,9},{9,1},{2,10},{10,2},{3,11},{11,3},{4,12},{12,4},... | collective-permute-start | bytes 196616 | tf_op jit(solution)/shard_map/ppermute | solution.py:19
  82.1 4.5 %collective-permute-start.13 = (bf16[2,2,2,64,288]{4,3,0,1,2:T(8,128)(2,1)S(1)}, bf16[2,2,2,64,288]{4,3,0,1,2:T(8,128)(2,1)S(1)}, u32[]{:S(2)}, u32[]{:S(2)}) collective-permute-start(bf16[2,2,2,64,288]{4,3,0,1,2:T(8,128)(2,1)S(1)} %fusion.8), channel_id=1, source_target_pairs={{0,1},{1,0},{2,3},{3,2},{4,5},{5,4},{6,7},{7,6},{8,9},{9,8},{10,11... | collective-permute-start | bytes 884744 | tf_op jit(solution)/shard_map/ppermute | solution.py:19
  86.8 10.6 %collective-permute-start.14 = (bf16[2,2,64,288]{3,2,0,1:T(8,128)(2,1)S(1)}, bf16[2,2,64,288]{3,2,0,1:T(8,128)(2,1)S(1)}, u32[]{:S(2)}, u32[]{:S(2)}) collective-permute-start(bf16[2,2,64,288]{3,2,0,1:T(8,128)(2,1)S(1)} %fusion.13), channel_id=1, source_target_pairs={{0,2},{2,0},{1,3},{3,1},{4,6},{6,4},{5,7},{7,5},{8,10},{10,8},{9,1... | collective-permute-start | bytes 442376 | tf_op jit(solution)/shard_map/ppermute | solution.py:19
  93.9 9.9 %collective-permute-start.21 = (bf16[2,2,2,64,512]{4,3,2,0,1:T(8,128)(2,1)}, bf16[2,2,2,64,512]{4,3,2,0,1:T(8,128)(2,1)}, u32[]{:S(2)}, u32[]{:S(2)}) collective-permute-start(bf16[2,2,2,64,512]{4,3,2,0,1:T(8,128)(2,1)} %fusion.3), channel_id=1, source_target_pairs={{0,1},{1,0},{2,3},{3,2},{4,5},{5,4},{6,7},{7,6},{8,9},{9,8},{10,11... | collective-permute-start | bytes 1572872 | tf_op jit(solution)/shard_map/ppermute | solution.py:19
  97.4 4.8 %collective-permute-start.15 = (bf16[2,64,288]{2,1,0:T(8,128)(2,1)S(1)}, bf16[2,64,288]{2,1,0:T(8,128)(2,1)S(1)}, u32[]{:S(2)}, u32[]{:S(2)}) collective-permute-start(bf16[2,64,288]{2,1,0:T(8,128)(2,1)S(1)} %fusion.18), channel_id=1, source_target_pairs={{0,4},{4,0},{1,5},{5,1},{2,6},{6,2},{3,7},{7,3},{8,12},{12,8},{9,1... | collective-permute-start | bytes 221192 | tf_op jit(solution)/shard_map/ppermute | solution.py:19
  99.7 7.2 %collective-permute-start.17 = (bf16[2,2,2,64,512]{4,3,2,1,0:T(8,128)(2,1)S(1)}, bf16[2,2,2,64,512]{4,3,2,1,0:T(8,128)(2,1)S(1)}, u32[]{:S(2)}, u32[]{:S(2)}) collective-permute-start(bf16[2,2,2,64,512]{4,3,2,1,0:T(8,128)(2,1)S(1)} %fusion), channel_id=1, source_target_pairs={{0,1},{1,0},{2,3},{3,2},{4,5},{5,4},{6,7},{7,6},{8,9},{9,8},{10,11... | collective-permute-start | bytes 1572872 | tf_op jit(solution)/shard_map/ppermute | solution.py:19
  102.3 6.7 %collective-permute-start.16 = (bf16[64,288]{1,0:T(8,128)(2,1)S(1)}, bf16[64,288]{1,0:T(8,128)(2,1)S(1)}, u32[]{:S(2)}, u32[]{:S(2)}) collective-permute-start(bf16[64,288]{1,0:T(8,128)(2,1)S(1)} %fusion.23), channel_id=1, source_target_pairs={{0,8},{8,0},{1,9},{9,1},{2,10},{10,2},{3,11},{11,3},{4,12},{12,4},... | collective-permute-start | bytes 110600 | tf_op jit(solution)/shard_map/ppermute | solution.py:19
  105.1 7.8 %collective-permute-start.22 = (bf16[2,2,64,512]{3,2,1,0:T(8,128)(2,1)S(1)}, bf16[2,2,64,512]{3,2,1,0:T(8,128)(2,1)S(1)}, u32[]{:S(2)}, u32[]{:S(2)}) collective-permute-start(bf16[2,2,64,512]{3,2,1,0:T(8,128)(2,1)S(1)} %fusion.12), channel_id=1, source_target_pairs={{0,4},{4,0},{1,5},{5,1},{2,6},{6,2},{3,7},{7,3},{8,12},{12,8},{9,1... | collective-permute-start | bytes 786440 | tf_op jit(solution)/shard_map/ppermute | solution.py:19
  107.2 7.2 %collective-permute-start.18 = (bf16[2,2,64,512]{3,2,1,0:T(8,128)(2,1)S(1)}, bf16[2,2,64,512]{3,2,1,0:T(8,128)(2,1)S(1)}, u32[]{:S(2)}, u32[]{:S(2)}) collective-permute-start(bf16[2,2,64,512]{3,2,1,0:T(8,128)(2,1)S(1)} %fusion.11), channel_id=1, source_target_pairs={{0,2},{2,0},{1,3},{3,1},{4,6},{6,4},{5,7},{7,5},{8,10},{10,8},{9,1... | collective-permute-start | bytes 786440 | tf_op jit(solution)/shard_map/ppermute | solution.py:19
  113.1 7.8 %collective-permute-start.23 = (bf16[2,64,512]{2,1,0:T(8,128)(2,1)S(1)}, bf16[2,64,512]{2,1,0:T(8,128)(2,1)S(1)}, u32[]{:S(2)}, u32[]{:S(2)}) collective-permute-start(bf16[2,64,512]{2,1,0:T(8,128)(2,1)S(1)} %fusion.17), channel_id=1, source_target_pairs={{0,8},{8,0},{1,9},{9,1},{2,10},{10,2},{3,11},{11,3},{4,12},{12,4},... | collective-permute-start | bytes 393224 | tf_op jit(solution)/shard_map/ppermute | solution.py:19
  114.5 8.9 %collective-permute-start.19 = (bf16[2,64,512]{2,1,0:T(8,128)(2,1)S(1)}, bf16[2,64,512]{2,1,0:T(8,128)(2,1)S(1)}, u32[]{:S(2)}, u32[]{:S(2)}) collective-permute-start(bf16[2,64,512]{2,1,0:T(8,128)(2,1)S(1)} %fusion.16), channel_id=1, source_target_pairs={{0,4},{4,0},{1,5},{5,1},{2,6},{6,2},{3,7},{7,3},{8,12},{12,8},{9,1... | collective-permute-start | bytes 393224 | tf_op jit(solution)/shard_map/ppermute | solution.py:19
  120.9 4.8 %collective-permute-start.24 = (bf16[64,512]{1,0:T(8,128)(2,1)S(1)}, bf16[64,512]{1,0:T(8,128)(2,1)S(1)}, u32[]{:S(2)}, u32[]{:S(2)}) collective-permute-start(bf16[64,512]{1,0:T(8,128)(2,1)S(1)} %fusion.22), channel_id=1, source_target_pairs={{0,2},{2,0},{1,3},{3,1},{4,6},{6,4},{5,7},{7,5},{8,10},{10,8},{9,1... | collective-permute-start | bytes 196616 | tf_op jit(solution)/shard_map/ppermute | solution.py:19
  123.5 5.2 %collective-permute-start.20 = (bf16[64,512]{1,0:T(8,128)(2,1)S(1)}, bf16[64,512]{1,0:T(8,128)(2,1)S(1)}, u32[]{:S(2)}, u32[]{:S(2)}) collective-permute-start(bf16[64,512]{1,0:T(8,128)(2,1)S(1)} %fusion.21), channel_id=1, source_target_pairs={{0,8},{8,0},{1,9},{9,1},{2,10},{10,2},{3,11},{11,3},{4,12},{12,4},... | collective-permute-start | bytes 196616 | tf_op jit(solution)/shard_map/ppermute | solution.py:19
  (12 other events, 74.4 us)

commit v3 on v2

--- a/solution.py
+++ b/solution.py
@@ -25,10 +25,14 @@
     return lax.ppermute(array, axis, pairs)
 
 
-def halve(piece, order, bits):
+def halve(sent, kept, order, bits, gate=None):
     position = lax.axis_index("space")
     left = list(range(bits))[::-1]
-    for bit in order:
+    left.remove(order[0])
+    piece = kept + partner(sent, "space", order[0]).astype(jnp.float32)
+    for at, bit in enumerate(order[1:]):
+        if at == 1 and gate is not None:
+            piece, _ = lax.optimization_barrier((piece, gate))
         axis = left.index(bit)
         mine = position // (1 << bit) % 2
         sent = lax.dynamic_index_in_dim(piece, 1 - mine, axis, keepdims=False)
@@ -39,17 +43,75 @@
     return piece
 
 
-def sum_shards(terms):
-    devices = lax.axis_size("space")
-    bits = devices.bit_length() - 1
+def shards_view(array, bits):
+    rows, columns = array.shape
+    return array.reshape((2,) * bits + (rows >> bits, columns))
+
+
+def sum_shards(terms, bits, gate=None):
     low_first = list(range(bits))
     high_first = [0] + list(range(2, bits)) + [1]
     done = []
-    for at, term in enumerate(terms):
-        rows, columns = term.shape
-        view = term.reshape((2,) * bits + (rows // devices, columns))
-        done.append(halve(view, (low_first, high_first)[at % 2], bits))
+    for at, (sent, kept) in enumerate(terms):
+        order = (low_first, high_first)[at % 2]
+        done.append(
+            halve(
+                shards_view(sent, bits - 1), shards_view(kept, bits - 1), order, bits, gate
+            )
+        )
     return done[0] if len(done) == 1 else jnp.concatenate(done, -1)
+
+
+def split_term(term, unit):
+    mine = lax.axis_index("space") % 2
+    view = term.reshape(-1, 2, unit, term.shape[1])
+    sent = lax.dynamic_index_in_dim(view, 1 - mine, 1, keepdims=False)
+    kept = lax.dynamic_index_in_dim(view, mine, 1, keepdims=False)
+    columns = term.shape[1]
+    return sent.astype(jnp.bfloat16).reshape(-1, columns), kept.reshape(-1, columns)
+
+
+def wgrad_kernel(unit, normalizer, rows_ref, columns_ref, sent_ref, kept_ref):
+    even = lax.axis_index("space") % 2 == 0
+    term = lax.dot_general(
+        rows_ref[...],
+        columns_ref[...],
+        (((0,), (0,)), ((), ())),
+        preferred_element_type=jnp.float32,
+    )
+    term = term * normalizer
+    sent, kept = [], []
+    for at in range(0, term.shape[0], 2 * unit):
+        low = term[at : at + unit]
+        high = term[at + unit : at + 2 * unit]
+        kept.append(jnp.where(even, low, high))
+        sent.append(jnp.where(even, high, low))
+    kept_ref[...] = jnp.concatenate(kept, 0)
+    sent_ref[...] = jnp.concatenate(sent, 0).astype(jnp.bfloat16)
+
+
+def wgrad_half(rows, columns, at, unit, normalizer):
+    size, channels = rows.shape
+    block = 256
+    width = columns.shape[1] // 2
+    out_spec = pl.BlockSpec((block // 2, width), lambda step: (step, 0))
+    return pl.pallas_call(
+        functools.partial(wgrad_kernel, unit, normalizer),
+        grid=(channels // block,),
+        in_specs=[
+            pl.BlockSpec((size, block), lambda step: (0, step)),
+            pl.BlockSpec((size, width), lambda step: (0, at)),
+        ],
+        out_specs=[out_spec, out_spec],
+        out_shape=[
+            jax.ShapeDtypeStruct((channels // 2, width), jnp.bfloat16),
+            jax.ShapeDtypeStruct((channels // 2, width), jnp.float32),
+        ],
+        compiler_params=pltpu.CompilerParams(vmem_limit_bytes=24 * 2**20),
+        cost_estimate=pl.CostEstimate(
+            flops=2 * size * channels * width, bytes_accessed=6 * channels * width, transcendentals=0
+        ),
+    )(rows, columns)
 
 
 def to_tiles(block, col_parity, row_parity, row_bit):
@@ -60,6 +122,7 @@
     kept_part = lax.dynamic_index_in_dim(split, row_parity, 0, keepdims=False)
     sent_part = lax.dynamic_index_in_dim(split, 1 - row_parity, 0, keepdims=False)
     received = partner(sent_part, "space", row_bit)
+    kept_part, received = lax.optimization_barrier((kept_part, received))
     joined = jnp.where(
         row_parity == 0, jnp.stack([kept_part, received], 2), jnp.stack([received, kept_part], 2)
     )
@@ -72,7 +135,7 @@
         jnp.stack([kept_cols, received_cols], 3),
         jnp.stack([received_cols, kept_cols], 3),
     )
-    return stacked.reshape(tile_rows, tile_width, 4 * shard_width)
+    return stacked.reshape(tile_rows, tile_width, 4 * shard_width), received
 
 
 def group_kernel(
@@ -184,7 +247,7 @@
         ],
         compiler_params=pltpu.CompilerParams(vmem_limit_bytes=32 * 2**20),
         cost_estimate=pl.CostEstimate(
-            flops=36 * size * block * channels, bytes_accessed=8 * size * channels, transcendentals=0
+            flops=90 * size * block * channels, bytes_accessed=8 * size * channels, transcendentals=0
         ),
     )(inner, top, bottom, left, right, second, weight)
 
@@ -208,7 +271,8 @@
         grad_rows, third_weight, (((1,), (1,)), ((), ())), preferred_element_type=jnp.float32
     )
     inner_grad = jnp.where(third_rows > 0, back_third, 0.0).astype(jnp.bfloat16)
-    half = channels // 2
+    bits = devices.bit_length() - 1
+    unit = channels // devices
     inner_tile = inner_grad.reshape(tile_rows, tile_width, channels)
     top = from_behind(inner_tile[-1:], "space", 2)
     bottom = from_behind(inner_tile[:1], "space", -2)
@@ -221,7 +285,7 @@
     ).astype(jnp.float32)
     left = jnp.where(col_parity == 1, rims, 0.0)
     right = jnp.where(col_parity == 0, rims, 0.0)
-    second_tile = to_tiles(second_input[0], col_parity, row_parity, row_bit)
+    second_tile, arrived = to_tiles(second_input[0], col_parity, row_parity, row_bit)
     first_rows, local_term = group_backward(
         inner_grad,
         top[0],
@@ -234,20 +298,13 @@
         normalizer,
     )
 
-    def half_terms(rows, columns):
-        return [
-            lax.dot_general(
-                rows,
-                columns[:, at : at + half],
-                (((0,), (0,)), ((), ())),
-                preferred_element_type=jnp.float32,
-            )
-            * normalizer
-            for at in (0, half)
-        ]
-
-    third_wgrad = sum_shards(half_terms(third_rows, grad_rows))
-    group_wgrad = sum_shards([local_term])
+    gated_rows, _ = lax.optimization_barrier((third_rows, arrived))
+    third_terms = [wgrad_half(gated_rows, grad_rows, at, unit, normalizer) for at in (0, 1)]
+    third_wgrad = sum_shards(third_terms, bits, first_rows)
+    first_terms = [wgrad_half(input_rows, first_rows, at, unit, normalizer) for at in (0, 1)]
+    first_wgrad = sum_shards(first_terms, bits)
+    group_wgrad = sum_shards([split_term(local_term, unit)], bits)
+    first_rows, _ = lax.optimization_barrier((first_rows, first_terms[1][0]))
     summed = lax.dot_general(
         first_rows, first_weight, (((1,), (1,)), ((), ())), preferred_element_type=jnp.float32
     )
@@ -256,7 +313,6 @@
         .astype(jnp.bfloat16)
         .reshape(1, tile_rows, tile_width, channels)
     )
-    first_wgrad = sum_shards(half_terms(input_rows, first_rows))
     return (input_grad, third_wgrad, group_wgrad, first_wgrad)
 
 

time: 130 us -> 126 us (0.969)
  matrix products: 16.2 us -> 5.08 us
  local copies, waits for them, and re-layouts: 27.8 us -> 20.8 us
  Pallas kernels: 10.9 us -> 17.2 us
  waiting for transfers between devices: 31 us -> 34.9 us
  starting transfers between devices: 34.3 us -> 36.7 us
    dot_general x4 -> x0, matrix products: 11.1 us -> none  [half_terms(): lax.dot_general(rows, columns[:, at:at + half], (((0,), (0,)), ((), ())),...]
    convert_element_type x20 -> x15, local copies, waits for them, and re-layouts: 7.21 us -> 0.42 us  [halve(): received = partner(sent.astype(jnp.bfloat16), 'space', bit)]
    pallas_call x0 -> x4, Pallas kernels: none -> 6.31 us  [wgrad_half(): pl.pallas_call(functools.partial(wgrad_kernel, unit, normalizer), grid=(c...]
    mul x2 -> x0, local copies, waits for them, and re-layouts: 5.86 us -> none  [half_terms(): lax.dot_general(rows, columns[:, at:at + half], (((0,), (0,)), ((), ())),...]
    ppermute x23, waiting for transfers between devices: 31 us -> 34.9 us  [partner(): return lax.ppermute(block, axis, route)]
    add x0 -> x5, other arithmetic: none -> 2.94 us  [halve(): piece = kept + partner(sent, 'space', order[0]).astype(jnp.float32)]
    add x20 -> x15, other arithmetic: 4.08 us -> 1.18 us  [halve(): piece = kept + received.astype(jnp.float32)]
    ppermute x23, starting transfers between devices: 26.8 us -> 29.2 us  [partner(): return lax.ppermute(block, axis, route)]
  transfers between devices with their start and end apart: 25 -> 25, of which waited for: 11 -> 13; matrix products, arithmetic and copies ran while one was open for 30% -> 20% of each run, Pallas kernels for 0% -> 14%
where the time goes in v3:
time: 126 us; the launch traced here: 125 us
  starting transfers between devices  36.7 us (29%)
  waiting for transfers between devices  34.9 us (28%)
  local copies, waits for them, and re-layouts  20.8 us (17%)
  Pallas kernels  17.2 us (14%)
  other arithmetic  9.42 us (7%)
  matrix products  5.08 us (4%)
    ppermute x23, waiting for transfers between devices, partner(): return lax.ppermute(block, axis, route)  34.9 us
    ppermute x23, starting transfers between devices, partner(): return lax.ppermute(block, axis, route)  29.2 us
    pallas_call x1, Pallas kernels, group_backward(): pl.pallas_call(functools.partial(group_kernel, tile_rows, width, taps //...  10.9 us
    unnamed x27, local copies, waits for them, and re-layouts  8.64 us
    ppermute x2, starting transfers between devices, from_behind(): return lax.ppermute(array, axis, pairs)  7.48 us
    pallas_call x4, Pallas kernels, wgrad_half(): pl.pallas_call(functools.partial(wgrad_kernel, unit, normalizer), grid=(c...  6.31 us
    select_n x2, local copies, waits for them, and re-layouts, to_tiles(): jnp.where(col_parity == 0, jnp.stack([kept_cols, received_cols], 3), jnp....  3.83 us
    add x5, other arithmetic, halve(): piece = kept + partner(sent, 'space', order[0]).astype(jnp.float32)  2.94 us
  transfers between devices with their start and end apart: 25, of which 13 were waited for; matrix products, arithmetic and copies ran while one was open for 20% of the time, Pallas kernels for 14%

profile of v3, /device:TPU:0, one launch (start us, length us, event | category | flops | bytes accessed | tf_op | source)
XLA Modules:
  0.0 125.2 jit_solution(6895777064979536000)
XLA Ops:
  2.2 2.8 %select_convert_fusion.inner_ref = bf16[512,1024]{1,0:T(8,128)(2,1)S(1)} fusion(bf16[512,1024]{1,0:T(8,128)(2,1)} %bitcast.110, bf16[512,1024]{1,0:T(8,128)(2,1)} %bitcast.115, bf16[1024,1024]{1,0:T(8,128)(2,1)S(1)} %copy-done), kind=kOutput, calls=%fused_computation.1 | convolution fusion | flops 1075314688 | bytes 5242880 | tf_op jit(solution)/shard_map/dot_general | solution.py:270
  7.2 6.2 %collective-permute-start = (bf16[1,128,1024]{2,1,0:T(8,128)(2,1)}, bf16[1,128,1024]{2,1,0:T(8,128)(2,1)}, u32[]{:S(2)}, u32[]{:S(2)}) collective-permute-start(bf16[1,128,1024]{2,1,0:T(8,128)(2,1)} %get-tuple-element.43), channel_id=1, source_target_pairs={{0,2},{1,3},{2,4},{3,5},{4,6},{5,7},{6,8},{7,9},{8,10},{9,11},{10,... | collective-permute-start | bytes 786440 | tf_op jit(solution)/shard_map/ppermute | solution.py:25
  13.4 2.3 %dynamic-slice_bitcast_fusion = (bf16[4,256,256]{2,1,0:T(8,128)(2,1)}, bf16[4,256,256]{2,1,0:T(8,128)(2,1)}) fusion(bf16[2,4,256,256]{3,2,1,0:T(8,128)(2,1)} %bitcast.134, s32[]{:T(128)S(6)} %select_n.236, s32[]{:T(128)S(6)} %select_n.235), kind=kLoop, calls=%fused_computation.20 | loop fusion | bytes 2097160 | tf_op jit(solution)/shard_map/jit(dynamic_index_in_dim)/squeeze | solution.py:123
  15.7 2.2 %collective-permute-start.3 = (bf16[4,256,256]{2,1,0:T(8,128)(2,1)}, bf16[4,256,256]{2,1,0:T(8,128)(2,1)}, u32[]{:S(2)}, u32[]{:S(2)}) collective-permute-start(bf16[4,256,256]{2,1,0:T(8,128)(2,1)} %get-tuple-element.38), channel_id=1, source_target_pairs={{0,2},{2,0},{1,3},{3,1},{4,6},{6,4},{5,7},{7,5},{8,10},{10,8},{9,1... | collective-permute-start | bytes 1572872 | tf_op jit(solution)/shard_map/ppermute | solution.py:19
  18.1 16.3 %collective-permute-done.3 = bf16[4,256,256]{2,1,0:T(8,128)(2,1)} collective-permute-done((bf16[4,256,256]{2,1,0:T(8,128)(2,1)}, bf16[4,256,256]{2,1,0:T(8,128)(2,1)}, u32[]{:S(2)}, u32[]{:S(2)}) %collective-permute-start.3) | collective-permute-done | bytes 524320 | tf_op jit(solution)/shard_map/ppermute | solution.py:19
  34.4 1.7 %maximum_select_fusion = bf16[4,2,128,2,256]{4,2,1,0,3:T(8,128)(2,1)S(1)} fusion(bf16[4,2,128,1,256]{4,2,1,0,3:T(8,128)(2,1)} %bitcast.14, bf16[4,2,128,1,256]{4,2,1,0,3:T(8,128)(2,1)} %bitcast.133, pred[]{:T(512)S(6)} %eq.34), kind=kLoop, calls=%fused_computation.2 | loop fusion | flops 1572864 | bytes 2097153 | tf_op jit(solution)/shard_map/jit(_where)/select_n | solution.py:126
  39.2 2.2 %copy.42.weight_ref = bf16[1024,288]{1,0:T(8,128)(2,1)} copy(bf16[1024,288]{0,1:T(8,128)(2,1)} %param.12) | data formatting | bytes 1179648 | tf_op args[5]
  51.8 2.0 %copy.41 = bf16[4,128,2,2,256]{4,3,2,1,0:T(2,128)(2,1)} copy(bf16[4,128,2,2,256]{4,1,3,2,0:T(8,128)(2,1)S(1)} %maximum_select_fusion.1) | data formatting | bytes 2097152 | tf_op jit(solution)/shard_map/jit(_where)/select_n | solution.py:133
  53.9 1.8 %select_n.241.second_ref = bf16[512,1024]{1,0:T(8,128)(2,1)S(1)} reshape(bf16[4,128,2,2,256]{4,3,2,1,0:T(2,128)(2,1)} %copy.41) | data formatting | bytes 2097152 | tf_op jit(solution)/shard_map/jit(_where)/select_n | solution.py:133
  58.0 10.9 %shard_map.102 = (bf16[512,1024]{1,0:T(8,128)(2,1)S(1)}, f32[1024,288]{1,0:T(8,128)S(1)}) custom-call(bf16[512,1024]{1,0:T(8,128)(2,1)S(1)} %copy-done.11, bf16[128,1024]{1,0:T(8,128)(2,1)} %bitcast.3.top_ref, bf16[128,1024]{1,0:T(8,128)(2,1)S(1)} %bitcast.130, f32[6,1024]{1,0:T(8,128)S(1)} %get-tuple-element.45.left_ref, ...), custom_call_target="tpu_custom_call" | custom-call | flops 12079595520 | bytes 4194304 | tf_op jit(solution)/shard_map/pallas_call | solution.py:227
  74.4 1.7 %collective-permute-start.10 = (bf16[2,2,64,512]{3,2,1,0:T(8,128)(2,1)S(1)}, bf16[2,2,64,512]{3,2,1,0:T(8,128)(2,1)S(1)}, u32[]{:S(2)}, u32[]{:S(2)}) collective-permute-start(bf16[2,2,64,512]{3,2,1,0:T(8,128)(2,1)S(1)} %fusion.1), channel_id=1, source_target_pairs={{0,4},{4,0},{1,5},{5,1},{2,6},{6,2},{3,7},{7,3},{8,12},{12,8},{9,1... | collective-permute-start | bytes 786440 | tf_op jit(solution)/shard_map/ppermute | solution.py:19
  77.4 2.5 %collective-permute-start.6 = (bf16[2,2,64,512]{3,2,0,1:T(8,128)(2,1)S(1)}, bf16[2,2,64,512]{3,2,0,1:T(8,128)(2,1)S(1)}, u32[]{:S(2)}, u32[]{:S(2)}) collective-permute-start(bf16[2,2,64,512]{3,2,0,1:T(8,128)(2,1)S(1)} %fusion), channel_id=1, source_target_pairs={{0,2},{2,0},{1,3},{3,1},{4,6},{6,4},{5,7},{7,5},{8,10},{10,8},{9,1... | collective-permute-start | bytes 786440 | tf_op jit(solution)/shard_map/ppermute | solution.py:19
  79.9 2.3 %add_convert_fusion = bf16[512,1024]{1,0:T(8,128)(2,1)} fusion(bf16[512,1024]{1,0:T(8,128)(2,1)S(1)} %bitcast.118, bf16[512,1024]{1,0:T(8,128)(2,1)S(1)} %get-tuple-element.24.columns_ref, bf16[1024,1024]{1,0:T(8,128)(2,1)S(1)} %copy-done.12), kind=kOutput, calls=%fused_computation | convolution fusion | flops 1075314688 | bytes 5242880 | tf_op jit(solution)/shard_map/dot_general | solution.py:308
  83.1 2.7 %collective-permute-start.11 = (bf16[2,64,512]{2,1,0:T(8,128)(2,1)S(1)}, bf16[2,64,512]{2,1,0:T(8,128)(2,1)S(1)}, u32[]{:S(2)}, u32[]{:S(2)}) collective-permute-start(bf16[2,64,512]{2,1,0:T(8,128)(2,1)S(1)} %fusion.6), channel_id=1, source_target_pairs={{0,8},{8,0},{1,9},{9,1},{2,10},{10,2},{3,11},{11,3},{4,12},{12,4},... | collective-permute-start | bytes 393224 | tf_op jit(solution)/shard_map/ppermute | solution.py:19
  89.1 2.9 %collective-permute-done.11 = bf16[2,64,512]{2,1,0:T(8,128)(2,1)S(1)} collective-permute-done((bf16[2,64,512]{2,1,0:T(8,128)(2,1)S(1)}, bf16[2,64,512]{2,1,0:T(8,128)(2,1)S(1)}, u32[]{:S(2)}, u32[]{:S(2)}) %collective-permute-start.11) | collective-permute-done | bytes 131104 | tf_op jit(solution)/shard_map/ppermute | solution.py:19
  92.0 2.5 %collective-permute-start.12 = (bf16[64,512]{1,0:T(8,128)(2,1)S(1)}, bf16[64,512]{1,0:T(8,128)(2,1)S(1)}, u32[]{:S(2)}, u32[]{:S(2)}) collective-permute-start(bf16[64,512]{1,0:T(8,128)(2,1)S(1)} %fusion.11), channel_id=1, source_target_pairs={{0,2},{2,0},{1,3},{3,1},{4,6},{6,4},{5,7},{7,5},{8,10},{10,8},{9,1... | collective-permute-start | bytes 196616 | tf_op jit(solution)/shard_map/ppermute | solution.py:19
  95.8 2.1 %collective-permute-start.15 = (bf16[2,64,288]{2,1,0:T(8,128)(2,1)S(1)}, bf16[2,64,288]{2,1,0:T(8,128)(2,1)S(1)}, u32[]{:S(2)}, u32[]{:S(2)}) collective-permute-start(bf16[2,64,288]{2,1,0:T(8,128)(2,1)S(1)} %fusion.9), channel_id=1, source_target_pairs={{0,4},{4,0},{1,5},{5,1},{2,6},{6,2},{3,7},{7,3},{8,12},{12,8},{9,1... | collective-permute-start | bytes 221192 | tf_op jit(solution)/shard_map/ppermute | solution.py:19
  98.0 2.3 %collective-permute-done.8 = bf16[64,512]{1,0:T(8,128)(2,1)S(1)} collective-permute-done((bf16[64,512]{1,0:T(8,128)(2,1)S(1)}, bf16[64,512]{1,0:T(8,128)(2,1)S(1)}, u32[]{:S(2)}, u32[]{:S(2)}) %collective-permute-start.8) | collective-permute-done | bytes 65568 | tf_op jit(solution)/shard_map/ppermute | solution.py:19
  103.4 2.0 %collective-permute-start.22 = (bf16[2,2,64,512]{3,2,1,0:T(8,128)(2,1)S(1)}, bf16[2,2,64,512]{3,2,1,0:T(8,128)(2,1)S(1)}, u32[]{:S(2)}, u32[]{:S(2)}) collective-permute-start(bf16[2,2,64,512]{3,2,1,0:T(8,128)(2,1)S(1)} %fusion.3), channel_id=1, source_target_pairs={{0,4},{4,0},{1,5},{5,1},{2,6},{6,2},{3,7},{7,3},{8,12},{12,8},{9,1... | collective-permute-start | bytes 786440 | tf_op jit(solution)/shard_map/ppermute | solution.py:19
  107.1 2.1 %collective-permute-done.18 = bf16[2,2,64,512]{3,2,0,1:T(8,128)(2,1)S(1)} collective-permute-done((bf16[2,2,64,512]{3,2,0,1:T(8,128)(2,1)S(1)}, bf16[2,2,64,512]{3,2,0,1:T(8,128)(2,1)S(1)}, u32[]{:S(2)}, u32[]{:S(2)}) %collective-permute-start.18) | collective-permute-done | bytes 262176 | tf_op jit(solution)/shard_map/ppermute | solution.py:19
  109.3 1.8 %collective-permute-start.19 = (bf16[2,64,512]{2,1,0:T(8,128)(2,1)S(1)}, bf16[2,64,512]{2,1,0:T(8,128)(2,1)S(1)}, u32[]{:S(2)}, u32[]{:S(2)}) collective-permute-start(bf16[2,64,512]{2,1,0:T(8,128)(2,1)S(1)} %fusion.7), channel_id=1, source_target_pairs={{0,4},{4,0},{1,5},{5,1},{2,6},{6,2},{3,7},{7,3},{8,12},{12,8},{9,1... | collective-permute-start | bytes 393224 | tf_op jit(solution)/shard_map/ppermute | solution.py:19
  112.5 2.1 %collective-permute-start.23 = (bf16[2,64,512]{2,1,0:T(8,128)(2,1)S(1)}, bf16[2,64,512]{2,1,0:T(8,128)(2,1)S(1)}, u32[]{:S(2)}, u32[]{:S(2)}) collective-permute-start(bf16[2,64,512]{2,1,0:T(8,128)(2,1)S(1)} %fusion.8), channel_id=1, source_target_pairs={{0,8},{8,0},{1,9},{9,1},{2,10},{10,2},{3,11},{11,3},{4,12},{12,4},... | collective-permute-start | bytes 393224 | tf_op jit(solution)/shard_map/ppermute | solution.py:19
  117.0 3.1 %collective-permute-done.23 = bf16[2,64,512]{2,1,0:T(8,128)(2,1)S(1)} collective-permute-done((bf16[2,64,512]{2,1,0:T(8,128)(2,1)S(1)}, bf16[2,64,512]{2,1,0:T(8,128)(2,1)S(1)}, u32[]{:S(2)}, u32[]{:S(2)}) %collective-permute-start.23) | collective-permute-done | bytes 131104 | tf_op jit(solution)/shard_map/ppermute | solution.py:19
  121.5 3.0 %collective-permute-done.24 = bf16[64,512]{1,0:T(8,128)(2,1)S(1)} collective-permute-done((bf16[64,512]{1,0:T(8,128)(2,1)S(1)}, bf16[64,512]{1,0:T(8,128)(2,1)S(1)}, u32[]{:S(2)}, u32[]{:S(2)}) %collective-permute-start.24) | collective-permute-done | bytes 65568 | tf_op jit(solution)/shard_map/ppermute | solution.py:19
  (118 shorter events, 42.5 us)
Async XLA Ops:
  6.0 12.1 %collective-permute-start.1 = (bf16[1,128,1024]{2,1,0:T(8,128)(2,1)}, bf16[1,128,1024]{2,1,0:T(8,128)(2,1)S(1)}, u32[]{:S(2)}, u32[]{:S(2)}) collective-permute-start(bf16[1,128,1024]{2,1,0:T(8,128)(2,1)} %get-tuple-element.42), channel_id=1, source_target_pairs={{2,0},{3,1},{4,2},{5,3},{6,4},{7,5},{8,6},{9,7},{10,8},{11,9},{12,... | collective-permute-start | bytes 786440 | tf_op jit(solution)/shard_map/ppermute | solution.py:25
  7.2 30.7 %collective-permute-start = (bf16[1,128,1024]{2,1,0:T(8,128)(2,1)}, bf16[1,128,1024]{2,1,0:T(8,128)(2,1)}, u32[]{:S(2)}, u32[]{:S(2)}) collective-permute-start(bf16[1,128,1024]{2,1,0:T(8,128)(2,1)} %get-tuple-element.43), channel_id=1, source_target_pairs={{0,2},{1,3},{2,4},{3,5},{4,6},{5,7},{6,8},{7,9},{8,10},{9,11},{10,... | collective-permute-start | bytes 786440 | tf_op jit(solution)/shard_map/ppermute | solution.py:25
  15.7 18.7 %collective-permute-start.3 = (bf16[4,256,256]{2,1,0:T(8,128)(2,1)}, bf16[4,256,256]{2,1,0:T(8,128)(2,1)}, u32[]{:S(2)}, u32[]{:S(2)}) collective-permute-start(bf16[4,256,256]{2,1,0:T(8,128)(2,1)} %get-tuple-element.38), channel_id=1, source_target_pairs={{0,2},{2,0},{1,3},{3,1},{4,6},{6,4},{5,7},{7,5},{8,10},{10,8},{9,1... | collective-permute-start | bytes 1572872 | tf_op jit(solution)/shard_map/ppermute | solution.py:19
  37.9 12.6 %collective-permute-start.4 = (bf16[4,128,2,256]{3,1,2,0:T(8,128)(2,1)}, bf16[4,128,2,256]{3,1,2,0:T(8,128)(2,1)}, u32[]{:S(2)}, u32[]{:S(2)}) collective-permute-start(bf16[4,128,2,256]{3,1,2,0:T(8,128)(2,1)} %bitcast.108), channel_id=1, source_target_pairs={{0,1},{1,0},{2,3},{3,2},{4,5},{5,4},{6,7},{7,6},{8,9},{9,8},{10,11... | collective-permute-start | bytes 1572872 | tf_op jit(solution)/shard_map/ppermute | solution.py:19
  46.5 26.5 %collective-permute-start.9 = (bf16[2,2,2,64,512]{4,3,2,0,1:T(8,128)(2,1)}, bf16[2,2,2,64,512]{4,3,2,0,1:T(8,128)(2,1)}, u32[]{:S(2)}, u32[]{:S(2)}) collective-permute-start(bf16[2,2,2,64,512]{4,3,2,0,1:T(8,128)(2,1)} %copy.45), channel_id=1, source_target_pairs={{0,1},{1,0},{2,3},{3,2},{4,5},{5,4},{6,7},{7,6},{8,9},{9,8},{10,11... | collective-permute-start | bytes 1572872 | tf_op jit(solution)/shard_map/ppermute | solution.py:19
  50.0 26.1 %collective-permute-start.5 = (bf16[2,2,2,64,512]{4,3,0,1,2:T(8,128)(2,1)}, bf16[2,2,2,64,512]{4,3,0,1,2:T(8,128)(2,1)}, u32[]{:S(2)}, u32[]{:S(2)}) collective-permute-start(bf16[2,2,2,64,512]{4,3,0,1,2:T(8,128)(2,1)} %copy.43), channel_id=1, source_target_pairs={{0,1},{1,0},{2,3},{3,2},{4,5},{5,4},{6,7},{7,6},{8,9},{9,8},{10,11... | collective-permute-start | bytes 1572872 | tf_op jit(solution)/shard_map/ppermute | solution.py:19
  68.9 18.7 %collective-permute-start.13 = (bf16[2,2,2,64,288]{4,3,2,1,0:T(8,128)(2,1)S(1)}, bf16[2,2,2,64,288]{4,3,2,1,0:T(8,128)(2,1)S(1)}, u32[]{:S(2)}, u32[]{:S(2)}) collective-permute-start(bf16[2,2,2,64,288]{4,3,2,1,0:T(8,128)(2,1)S(1)} %bitcast.135), channel_id=1, source_target_pairs={{0,1},{1,0},{2,3},{3,2},{4,5},{5,4},{6,7},{7,6},{8,9},{9,8},{10,11... | collective-permute-start | bytes 884744 | tf_op jit(solution)/shard_map/ppermute | solution.py:19
  70.7 31.8 %collective-permute-start.17 = (bf16[2,2,2,64,512]{4,3,0,1,2:T(8,128)(2,1)S(1)}, bf16[2,2,2,64,512]{4,3,0,1,2:T(8,128)(2,1)S(1)}, u32[]{:S(2)}, u32[]{:S(2)}) collective-permute-start(bf16[2,2,2,64,512]{4,3,0,1,2:T(8,128)(2,1)S(1)} %copy.49), channel_id=1, source_target_pairs={{0,1},{1,0},{2,3},{3,2},{4,5},{5,4},{6,7},{7,6},{8,9},{9,8},{10,11... | collective-permute-start | bytes 1572872 | tf_op jit(solution)/shard_map/ppermute | solution.py:19
  72.9 30.3 %collective-permute-start.21 = (bf16[2,2,2,64,512]{4,3,2,0,1:T(8,128)(2,1)S(1)}, bf16[2,2,2,64,512]{4,3,2,0,1:T(8,128)(2,1)S(1)}, u32[]{:S(2)}, u32[]{:S(2)}) collective-permute-start(bf16[2,2,2,64,512]{4,3,2,0,1:T(8,128)(2,1)S(1)} %copy.51), channel_id=1, source_target_pairs={{0,1},{1,0},{2,3},{3,2},{4,5},{5,4},{6,7},{7,6},{8,9},{9,8},{10,11... | collective-permute-start | bytes 1572872 | tf_op jit(solution)/shard_map/ppermute | solution.py:19
  74.4 8.6 %collective-permute-start.10 = (bf16[2,2,64,512]{3,2,1,0:T(8,128)(2,1)S(1)}, bf16[2,2,64,512]{3,2,1,0:T(8,128)(2,1)S(1)}, u32[]{:S(2)}, u32[]{:S(2)}) collective-permute-start(bf16[2,2,64,512]{3,2,1,0:T(8,128)(2,1)S(1)} %fusion.1), channel_id=1, source_target_pairs={{0,4},{4,0},{1,5},{5,1},{2,6},{6,2},{3,7},{7,3},{8,12},{12,8},{9,1... | collective-permute-start | bytes 786440 | tf_op jit(solution)/shard_map/ppermute | solution.py:19
  77.4 9.0 %collective-permute-start.6 = (bf16[2,2,64,512]{3,2,0,1:T(8,128)(2,1)S(1)}, bf16[2,2,64,512]{3,2,0,1:T(8,128)(2,1)S(1)}, u32[]{:S(2)}, u32[]{:S(2)}) collective-permute-start(bf16[2,2,64,512]{3,2,0,1:T(8,128)(2,1)S(1)} %fusion), channel_id=1, source_target_pairs={{0,2},{2,0},{1,3},{3,1},{4,6},{6,4},{5,7},{7,5},{8,10},{10,8},{9,1... | collective-permute-start | bytes 786440 | tf_op jit(solution)/shard_map/ppermute | solution.py:19
  83.1 8.8 %collective-permute-start.11 = (bf16[2,64,512]{2,1,0:T(8,128)(2,1)S(1)}, bf16[2,64,512]{2,1,0:T(8,128)(2,1)S(1)}, u32[]{:S(2)}, u32[]{:S(2)}) collective-permute-start(bf16[2,64,512]{2,1,0:T(8,128)(2,1)S(1)} %fusion.6), channel_id=1, source_target_pairs={{0,8},{8,0},{1,9},{9,1},{2,10},{10,2},{3,11},{11,3},{4,12},{12,4},... | collective-permute-start | bytes 393224 | tf_op jit(solution)/shard_map/ppermute | solution.py:19
  86.5 8.0 %collective-permute-start.7 = (bf16[2,64,512]{2,1,0:T(8,128)(2,1)S(1)}, bf16[2,64,512]{2,1,0:T(8,128)(2,1)S(1)}, u32[]{:S(2)}, u32[]{:S(2)}) collective-permute-start(bf16[2,64,512]{2,1,0:T(8,128)(2,1)S(1)} %fusion.5), channel_id=1, source_target_pairs={{0,4},{4,0},{1,5},{5,1},{2,6},{6,2},{3,7},{7,3},{8,12},{12,8},{9,1... | collective-permute-start | bytes 393224 | tf_op jit(solution)/shard_map/ppermute | solution.py:19
  87.8 8.0 %collective-permute-start.14 = (bf16[2,2,64,288]{3,2,1,0:T(8,128)(2,1)S(1)}, bf16[2,2,64,288]{3,2,1,0:T(8,128)(2,1)S(1)}, u32[]{:S(2)}, u32[]{:S(2)}) collective-permute-start(bf16[2,2,64,288]{3,2,1,0:T(8,128)(2,1)S(1)} %fusion.4), channel_id=1, source_target_pairs={{0,2},{2,0},{1,3},{3,1},{4,6},{6,4},{5,7},{7,5},{8,10},{10,8},{9,1... | collective-permute-start | bytes 442376 | tf_op jit(solution)/shard_map/ppermute | solution.py:19
  92.0 5.9 %collective-permute-start.12 = (bf16[64,512]{1,0:T(8,128)(2,1)S(1)}, bf16[64,512]{1,0:T(8,128)(2,1)S(1)}, u32[]{:S(2)}, u32[]{:S(2)}) collective-permute-start(bf16[64,512]{1,0:T(8,128)(2,1)S(1)} %fusion.11), channel_id=1, source_target_pairs={{0,2},{2,0},{1,3},{3,1},{4,6},{6,4},{5,7},{7,5},{8,10},{10,8},{9,1... | collective-permute-start | bytes 196616 | tf_op jit(solution)/shard_map/ppermute | solution.py:19
  94.6 5.7 %collective-permute-start.8 = (bf16[64,512]{1,0:T(8,128)(2,1)S(1)}, bf16[64,512]{1,0:T(8,128)(2,1)S(1)}, u32[]{:S(2)}, u32[]{:S(2)}) collective-permute-start(bf16[64,512]{1,0:T(8,128)(2,1)S(1)} %fusion.10), channel_id=1, source_target_pairs={{0,8},{8,0},{1,9},{9,1},{2,10},{10,2},{3,11},{11,3},{4,12},{12,4},... | collective-permute-start | bytes 196616 | tf_op jit(solution)/shard_map/ppermute | solution.py:19
  95.8 5.4 %collective-permute-start.15 = (bf16[2,64,288]{2,1,0:T(8,128)(2,1)S(1)}, bf16[2,64,288]{2,1,0:T(8,128)(2,1)S(1)}, u32[]{:S(2)}, u32[]{:S(2)}) collective-permute-start(bf16[2,64,288]{2,1,0:T(8,128)(2,1)S(1)} %fusion.9), channel_id=1, source_target_pairs={{0,4},{4,0},{1,5},{5,1},{2,6},{6,2},{3,7},{7,3},{8,12},{12,8},{9,1... | collective-permute-start | bytes 221192 | tf_op jit(solution)/shard_map/ppermute | solution.py:19
  101.2 5.2 %collective-permute-start.16 = (bf16[64,288]{1,0:T(8,128)(2,1)S(1)}, bf16[64,288]{1,0:T(8,128)(2,1)S(1)}, u32[]{:S(2)}, u32[]{:S(2)}) collective-permute-start(bf16[64,288]{1,0:T(8,128)(2,1)S(1)} %fusion.14), channel_id=1, source_target_pairs={{0,8},{8,0},{1,9},{9,1},{2,10},{10,2},{3,11},{11,3},{4,12},{12,4},... | collective-permute-start | bytes 110600 | tf_op jit(solution)/shard_map/ppermute | solution.py:19
  102.7 6.4 %collective-permute-start.18 = (bf16[2,2,64,512]{3,2,0,1:T(8,128)(2,1)S(1)}, bf16[2,2,64,512]{3,2,0,1:T(8,128)(2,1)S(1)}, u32[]{:S(2)}, u32[]{:S(2)}) collective-permute-start(bf16[2,2,64,512]{3,2,0,1:T(8,128)(2,1)S(1)} %fusion.2), channel_id=1, source_target_pairs={{0,2},{2,0},{1,3},{3,1},{4,6},{6,4},{5,7},{7,5},{8,10},{10,8},{9,1... | collective-permute-start | bytes 786440 | tf_op jit(solution)/shard_map/ppermute | solution.py:19
  103.4 9.0 %collective-permute-start.22 = (bf16[2,2,64,512]{3,2,1,0:T(8,128)(2,1)S(1)}, bf16[2,2,64,512]{3,2,1,0:T(8,128)(2,1)S(1)}, u32[]{:S(2)}, u32[]{:S(2)}) collective-permute-start(bf16[2,2,64,512]{3,2,1,0:T(8,128)(2,1)S(1)} %fusion.3), channel_id=1, source_target_pairs={{0,4},{4,0},{1,5},{5,1},{2,6},{6,2},{3,7},{7,3},{8,12},{12,8},{9,1... | collective-permute-start | bytes 786440 | tf_op jit(solution)/shard_map/ppermute | solution.py:19
  109.3 6.0 %collective-permute-start.19 = (bf16[2,64,512]{2,1,0:T(8,128)(2,1)S(1)}, bf16[2,64,512]{2,1,0:T(8,128)(2,1)S(1)}, u32[]{:S(2)}, u32[]{:S(2)}) collective-permute-start(bf16[2,64,512]{2,1,0:T(8,128)(2,1)S(1)} %fusion.7), channel_id=1, source_target_pairs={{0,4},{4,0},{1,5},{5,1},{2,6},{6,2},{3,7},{7,3},{8,12},{12,8},{9,1... | collective-permute-start | bytes 393224 | tf_op jit(solution)/shard_map/ppermute | solution.py:19
  112.5 7.6 %collective-permute-start.23 = (bf16[2,64,512]{2,1,0:T(8,128)(2,1)S(1)}, bf16[2,64,512]{2,1,0:T(8,128)(2,1)S(1)}, u32[]{:S(2)}, u32[]{:S(2)}) collective-permute-start(bf16[2,64,512]{2,1,0:T(8,128)(2,1)S(1)} %fusion.8), channel_id=1, source_target_pairs={{0,8},{8,0},{1,9},{9,1},{2,10},{10,2},{3,11},{11,3},{4,12},{12,4},... | collective-permute-start | bytes 393224 | tf_op jit(solution)/shard_map/ppermute | solution.py:19
  115.4 6.1 %collective-permute-start.20 = (bf16[64,512]{1,0:T(8,128)(2,1)S(1)}, bf16[64,512]{1,0:T(8,128)(2,1)S(1)}, u32[]{:S(2)}, u32[]{:S(2)}) collective-permute-start(bf16[64,512]{1,0:T(8,128)(2,1)S(1)} %fusion.12), channel_id=1, source_target_pairs={{0,8},{8,0},{1,9},{9,1},{2,10},{10,2},{3,11},{11,3},{4,12},{12,4},... | collective-permute-start | bytes 196616 | tf_op jit(solution)/shard_map/ppermute | solution.py:19
  120.2 4.3 %collective-permute-start.24 = (bf16[64,512]{1,0:T(8,128)(2,1)S(1)}, bf16[64,512]{1,0:T(8,128)(2,1)S(1)}, u32[]{:S(2)}, u32[]{:S(2)}) collective-permute-start(bf16[64,512]{1,0:T(8,128)(2,1)S(1)} %fusion.13), channel_id=1, source_target_pairs={{0,2},{2,0},{1,3},{3,1},{4,6},{6,4},{5,7},{7,5},{8,10},{10,8},{9,1... | collective-permute-start | bytes 196616 | tf_op jit(solution)/shard_map/ppermute | solution.py:19
  (14 other events, 74.5 us)

commit v4 on v3

--- a/solution.py
+++ b/solution.py
@@ -25,41 +25,25 @@
     return lax.ppermute(array, axis, pairs)
 
 
-def halve(sent, kept, order, bits, gate=None):
-    position = lax.axis_index("space")
-    left = list(range(bits))[::-1]
-    left.remove(order[0])
-    piece = kept + partner(sent, "space", order[0]).astype(jnp.float32)
-    for at, bit in enumerate(order[1:]):
-        if at == 1 and gate is not None:
-            piece, _ = lax.optimization_barrier((piece, gate))
-        axis = left.index(bit)
-        mine = position // (1 << bit) % 2
-        sent = lax.dynamic_index_in_dim(piece, 1 - mine, axis, keepdims=False)
-        kept = lax.dynamic_index_in_dim(piece, mine, axis, keepdims=False)
-        received = partner(sent.astype(jnp.bfloat16), "space", bit)
-        piece = kept + received.astype(jnp.float32)
-        left.remove(bit)
-    return piece
+def halve_round(piece, left, bit):
+    axis = left.index(bit)
+    mine = lax.axis_index("space") // (1 << bit) % 2
+    sent = lax.dynamic_index_in_dim(piece, 1 - mine, axis, keepdims=False)
+    kept = lax.dynamic_index_in_dim(piece, mine, axis, keepdims=False)
+    received = partner(sent.astype(jnp.bfloat16), "space", bit)
+    left.remove(bit)
+    return kept + received.astype(jnp.float32)
+
+
+def halve_start(pair, bits):
+    sent, kept = pair
+    received = partner(shards_view(sent, bits - 1), "space", 0)
+    return shards_view(kept, bits - 1) + received.astype(jnp.float32)
 
 
 def shards_view(array, bits):
     rows, columns = array.shape
     return array.reshape((2,) * bits + (rows >> bits, columns))
-
-
-def sum_shards(terms, bits, gate=None):
-    low_first = list(range(bits))
-    high_first = [0] + list(range(2, bits)) + [1]
-    done = []
-    for at, (sent, kept) in enumerate(terms):
-        order = (low_first, high_first)[at % 2]
-        done.append(
-            halve(
-                shards_view(sent, bits - 1), shards_view(kept, bits - 1), order, bits, gate
-            )
-        )
-    return done[0] if len(done) == 1 else jnp.concatenate(done, -1)
 
 
 def split_term(term, unit):
@@ -114,28 +98,22 @@
     )(rows, columns)
 
 
-def to_tiles(block, col_parity, row_parity, row_bit):
-    double_rows, double_cols, shard_width = block.shape
-    tile_rows = double_rows // 2
-    tile_width = double_cols // 2
-    split = block.reshape(2, tile_rows, double_cols, shard_width)
-    kept_part = lax.dynamic_index_in_dim(split, row_parity, 0, keepdims=False)
-    sent_part = lax.dynamic_index_in_dim(split, 1 - row_parity, 0, keepdims=False)
+def to_tiles(kept_part, sent_part, col_parity, row_parity, row_bit):
+    tile_rows, double_cols, shard_width = kept_part.shape
     received = partner(sent_part, "space", row_bit)
-    kept_part, received = lax.optimization_barrier((kept_part, received))
     joined = jnp.where(
-        row_parity == 0, jnp.stack([kept_part, received], 2), jnp.stack([received, kept_part], 2)
-    )
-    joined = joined.reshape(tile_rows, 2, tile_width, 2, shard_width)
-    kept_cols = lax.dynamic_index_in_dim(joined, col_parity, 1, keepdims=False)
-    sent_cols = lax.dynamic_index_in_dim(joined, 1 - col_parity, 1, keepdims=False)
+        row_parity == 0, jnp.stack([kept_part, received], 0), jnp.stack([received, kept_part], 0)
+    )
+    joined = joined.reshape(2, tile_rows, 2, double_cols // 2, shard_width)
+    kept_cols = lax.dynamic_index_in_dim(joined, col_parity, 2, keepdims=False)
+    sent_cols = lax.dynamic_index_in_dim(joined, 1 - col_parity, 2, keepdims=False)
     received_cols = partner(sent_cols, "space", 0)
     stacked = jnp.where(
         col_parity == 0,
-        jnp.stack([kept_cols, received_cols], 3),
-        jnp.stack([received_cols, kept_cols], 3),
-    )
-    return stacked.reshape(tile_rows, tile_width, 4 * shard_width), received
+        jnp.stack([kept_cols, received_cols], 1),
+        jnp.stack([received_cols, kept_cols], 1),
+    )
+    return stacked.reshape(4, tile_rows * double_cols // 2, shard_width)
 
 
 def group_kernel(
@@ -217,7 +195,7 @@
     size, channels = inner.shape
     width = size // tile_rows
     taps = weight.shape[1]
-    block = 256
+    block = second.shape[2]
     tall = tile_rows + 2
 
     def by_channels(rows):
@@ -233,7 +211,7 @@
             by_channels(width),
             by_channels(tall),
             by_channels(tall),
-            by_channels(size),
+            pl.BlockSpec((None, size, block), lambda at: (at, 0, 0)),
             by_rows,
         ],
         out_specs=[by_channels(size), by_rows],
@@ -267,8 +245,12 @@
     grad_rows = outer_grad.reshape(tile_rows * tile_width, channels)
     third_rows = third_input.reshape(tile_rows * tile_width, channels)
     input_rows = block_input.reshape(tile_rows * tile_width, channels)
+    split = second_input[0].reshape(2, tile_rows, 2 * tile_width, second_input.shape[3])
+    kept_part = lax.dynamic_index_in_dim(split, row_parity, 0, keepdims=False)
+    sent_part = lax.dynamic_index_in_dim(split, 1 - row_parity, 0, keepdims=False)
+    sent_part, early_rows = lax.optimization_barrier((sent_part, grad_rows))
     back_third = lax.dot_general(
-        grad_rows, third_weight, (((1,), (1,)), ((), ())), preferred_element_type=jnp.float32
+        early_rows, third_weight, (((1,), (1,)), ((), ())), preferred_element_type=jnp.float32
     )
     inner_grad = jnp.where(third_rows > 0, back_third, 0.0).astype(jnp.bfloat16)
     bits = devices.bit_length() - 1
@@ -285,25 +267,49 @@
     ).astype(jnp.float32)
     left = jnp.where(col_parity == 1, rims, 0.0)
     right = jnp.where(col_parity == 0, rims, 0.0)
-    second_tile, arrived = to_tiles(second_input[0], col_parity, row_parity, row_bit)
+    second_tile = to_tiles(kept_part, sent_part, col_parity, row_parity, row_bit)
     first_rows, local_term = group_backward(
         inner_grad,
         top[0],
         bottom[0],
         left,
         right,
-        second_tile.reshape(tile_rows * tile_width, channels),
+        second_tile,
         group_weight,
         tile_rows,
         normalizer,
     )
 
-    gated_rows, _ = lax.optimization_barrier((third_rows, arrived))
-    third_terms = [wgrad_half(gated_rows, grad_rows, at, unit, normalizer) for at in (0, 1)]
-    third_wgrad = sum_shards(third_terms, bits, first_rows)
+    high_first = list(range(2, bits)) + [1]
+    low_first = list(range(1, bits))
+    third = []
+    third_left = []
+    for at in (0, 1):
+        piece = halve_start(wgrad_half(third_rows, grad_rows, at, unit, normalizer), bits)
+        left = list(range(1, bits))[::-1]
+        third.append(halve_round(piece, left, high_first[0]))
+        third_left.append(left)
     first_terms = [wgrad_half(input_rows, first_rows, at, unit, normalizer) for at in (0, 1)]
-    first_wgrad = sum_shards(first_terms, bits)
-    group_wgrad = sum_shards([split_term(local_term, unit)], bits)
+    group_pair = split_term(local_term, unit)
+    third[0], third[1], _ = lax.optimization_barrier((third[0], third[1], first_terms[0][0]))
+    last = [halve_start(pair, bits) for pair in first_terms + [group_pair]]
+    last_left = [list(range(1, bits))[::-1] for _ in last]
+    last_order = [low_first, high_first, high_first]
+    for at in range(len(high_first)):
+        if at + 1 < len(high_first):
+            third = [
+                halve_round(piece, left, high_first[at + 1])
+                for piece, left in zip(third, third_left)
+            ]
+        tied = lax.optimization_barrier((*third, *last))
+        third, last = list(tied[:2]), list(tied[2:])
+        last = [
+            halve_round(piece, left, order[at])
+            for piece, left, order in zip(last, last_left, last_order)
+        ]
+    third_wgrad = jnp.concatenate(third, -1)
+    first_wgrad = jnp.concatenate(last[:2], -1)
+    group_wgrad = last[2]
     first_rows, _ = lax.optimization_barrier((first_rows, first_terms[1][0]))
     summed = lax.dot_general(
         first_rows, first_weight, (((1,), (1,)), ((), ())), preferred_element_type=jnp.float32

time: 126 us -> 114 us (0.905)
  local copies, waits for them, and re-layouts: 20.8 us -> 8.38 us
  waiting for transfers between devices: 34.9 us -> 44.8 us
  starting transfers between devices: 36.7 us -> 30 us
  matrix products: 5.08 us -> 3.55 us
    unnamed x27 -> x25, local copies, waits for them, and re-layouts: 8.64 us -> 2.68 us
    ppermute x23, starting transfers between devices: 29.2 us -> 23.4 us  [partner(): return lax.ppermute(block, axis, route)]
    ppermute x2, waiting for transfers between devices: 0.01 us -> 5.71 us  [from_behind(): return lax.ppermute(array, axis, pairs)]
    ppermute x23, waiting for transfers between devices: 34.9 us -> 39.1 us  [partner(): return lax.ppermute(block, axis, route)]
    select_n x2 -> x0, local copies, waits for them, and re-layouts: 3.83 us -> none  [to_tiles(): jnp.where(col_parity == 0, jnp.stack([kept_cols, received_cols], 3), jnp....]
    squeeze x1 -> x0, local copies, waits for them, and re-layouts: 2.27 us -> none  [to_tiles(): lax.dynamic_index_in_dim(split, 1 - row_parity, 0, keepdims=False)]
    dot_general x1, matrix products: 2.82 us -> 1.28 us  [per_device(): lax.dot_general(early_rows, third_weight, (((1,), (1,)), ((), ())), prefe...]
    dynamic_slice x3 -> x1, local copies, waits for them, and re-layouts: 2.82 us -> 2.39 us  [per_device(): kept_part = lax.dynamic_index_in_dim(split, row_parity, 0, keepdims=False)]
  transfers between devices with their start and end apart: 25 -> 25, of which waited for: 13 -> 13; matrix products, arithmetic and copies ran while one was open for 20% -> 13% of each run, Pallas kernels for 14% -> 3%
where the time goes in v4:
time: 114 us; the launch traced here: 113 us
  waiting for transfers between devices  44.8 us (39%)
  starting transfers between devices  30 us (26%)
  Pallas kernels  17.2 us (15%)
  local copies, waits for them, and re-layouts  8.38 us (7%)
  other arithmetic  8.24 us (7%)
  matrix products  3.55 us (3%)
  between operations  1.37 us (1%)
    ppermute x23, waiting for transfers between devices, partner(): return lax.ppermute(block, axis, route)  39.1 us
    ppermute x23, starting transfers between devices, partner(): return lax.ppermute(block, axis, route)  23.4 us
    pallas_call x1, Pallas kernels, group_backward(): pl.pallas_call(functools.partial(group_kernel, tile_rows, width, taps //...  10.8 us
    ppermute x2, starting transfers between devices, from_behind(): return lax.ppermute(array, axis, pairs)  6.53 us
    pallas_call x4, Pallas kernels, wgrad_half(): pl.pallas_call(functools.partial(wgrad_kernel, unit, normalizer), grid=(c...  6.34 us
    ppermute x2, waiting for transfers between devices, from_behind(): return lax.ppermute(array, axis, pairs)  5.71 us
    add x5, other arithmetic, halve_start(): return shards_view(kept, bits - 1) + received.astype(jnp.float32)  2.88 us
    unnamed x25, local copies, waits for them, and re-layouts  2.68 us
  transfers between devices with their start and end apart: 25, of which 13 were waited for; matrix products, arithmetic and copies ran while one was open for 13% of the time, Pallas kernels for 3%

profile of v4, /device:TPU:0, one launch (start us, length us, event | category | flops | bytes accessed | tf_op | source)
XLA Modules:
  0.0 113.5 jit_solution(15619420359853913078)
XLA Ops:
  0.7 2.4 %constant_dynamic-slice_fusion.1 = (bf16[1,4,256,256]{3,2,1,0:T(8,128)(2,1)}, bf16[4,256,256]{2,1,0:T(8,128)(2,1)}) fusion(bf16[2,4,256,256]{3,2,1,0:T(8,128)(2,1)} %bitcast.131, s32[]{:T(128)S(6)} %select_n.236, s32[]{:T(128)S(6)} %select_n.219), kind=kLoop, calls=%fused_computation.66 | loop fusion | bytes 2097160 | tf_op jit(solution)/shard_map/jit(dynamic_index_in_dim)/dynamic_slice | solution.py:249
  3.1 2.9 %collective-permute-start.3 = (bf16[4,256,256]{2,1,0:T(8,128)(2,1)}, bf16[4,256,256]{2,1,0:T(8,128)(2,1)}, u32[]{:S(2)}, u32[]{:S(2)}) collective-permute-start(bf16[4,256,256]{2,1,0:T(8,128)(2,1)} %get-tuple-element.35), channel_id=1, source_target_pairs={{0,2},{2,0},{1,3},{3,1},{4,6},{6,4},{5,7},{7,5},{8,10},{10,8},{9,1... | collective-permute-start | bytes 1572872 | tf_op jit(solution)/shard_map/ppermute | solution.py:19
  9.5 5.3 %collective-permute-start = (bf16[1,128,1024]{2,1,0:T(8,128)(2,1)}, bf16[1,128,1024]{2,1,0:T(8,128)(2,1)}, u32[]{:S(2)}, u32[]{:S(2)}) collective-permute-start(bf16[1,128,1024]{2,1,0:T(8,128)(2,1)} %get-tuple-element.71), channel_id=1, source_target_pairs={{0,2},{1,3},{2,4},{3,5},{4,6},{5,7},{6,8},{7,9},{8,10},{9,11},{10,... | collective-permute-start | bytes 786440 | tf_op jit(solution)/shard_map/ppermute | solution.py:25
  17.5 1.6 %shard_map.104 = (bf16[512,512]{1,0:T(8,128)(2,1)S(1)}, f32[512,512]{1,0:T(8,128)S(1)}) custom-call(bf16[512,1024]{1,0:T(8,128)(2,1)S(1)} %bitcast.109, bf16[512,1024]{1,0:T(8,128)(2,1)S(1)} %bitcast.114), custom_call_target="tpu_custom_call" | custom-call | flops 536870912 | bytes 3145728 | tf_op jit(solution)/shard_map/pallas_call | solution.py:82
  23.8 5.0 %collective-permute-done = bf16[1,128,1024]{2,1,0:T(8,128)(2,1)} collective-permute-done((bf16[1,128,1024]{2,1,0:T(8,128)(2,1)}, bf16[1,128,1024]{2,1,0:T(8,128)(2,1)}, u32[]{:S(2)}, u32[]{:S(2)}) %collective-permute-start) | collective-permute-done | bytes 262176 | tf_op jit(solution)/shard_map/ppermute | solution.py:25
  29.7 1.8 %maximum_select_fusion = bf16[2,4,2,128,256]{4,3,2,1,0:T(8,128)(2,1)S(1)} fusion(bf16[1,4,2,128,256]{4,3,2,1,0:T(8,128)(2,1)} %bitcast.13, bf16[1,4,2,128,256]{4,3,2,1,0:T(8,128)(2,1)} %bitcast.130, pred[]{:T(512)S(6)} %eq.34), kind=kLoop, calls=%fused_computation.2 | loop fusion | flops 1572864 | bytes 2097153 | tf_op jit(solution)/shard_map/jit(_where)/select_n | solution.py:104
  33.4 2.6 %collective-permute-start.8 = (bf16[2,2,64,512]{3,2,1,0:T(8,128)(2,1)S(1)}, bf16[2,2,64,512]{3,2,1,0:T(8,128)(2,1)S(1)}, u32[]{:S(2)}, u32[]{:S(2)}) collective-permute-start(bf16[2,2,64,512]{3,2,1,0:T(8,128)(2,1)S(1)} %fusion.1), channel_id=1, source_target_pairs={{0,4},{4,0},{1,5},{5,1},{2,6},{6,2},{3,7},{7,3},{8,12},{12,8},{9,1... | collective-permute-start | bytes 786440 | tf_op jit(solution)/shard_map/ppermute | solution.py:19
  37.3 5.7 %collective-permute-done.8 = bf16[2,2,64,512]{3,2,1,0:T(8,128)(2,1)S(1)} collective-permute-done((bf16[2,2,64,512]{3,2,1,0:T(8,128)(2,1)S(1)}, bf16[2,2,64,512]{3,2,1,0:T(8,128)(2,1)S(1)}, u32[]{:S(2)}, u32[]{:S(2)}) %collective-permute-start.8) | collective-permute-done | bytes 262176 | tf_op jit(solution)/shard_map/ppermute | solution.py:19
  43.1 5.0 %collective-permute-done.6 = bf16[2,2,64,512]{3,2,1,0:T(8,128)(2,1)S(1)} collective-permute-done((bf16[2,2,64,512]{3,2,1,0:T(8,128)(2,1)S(1)}, bf16[2,2,64,512]{3,2,1,0:T(8,128)(2,1)S(1)}, u32[]{:S(2)}, u32[]{:S(2)}) %collective-permute-start.6) | collective-permute-done | bytes 262176 | tf_op jit(solution)/shard_map/ppermute | solution.py:19
  48.4 10.8 %shard_map.102 = (bf16[512,1024]{1,0:T(8,128)(2,1)S(1)}, f32[1024,288]{1,0:T(8,128)S(1)}) custom-call(bf16[512,1024]{1,0:T(8,128)(2,1)S(1)} %copy-done.10, bf16[128,1024]{1,0:T(8,128)(2,1)} %bitcast.5.top_ref, bf16[128,1024]{1,0:T(8,128)(2,1)S(1)} %bitcast.128, f32[6,1024]{1,0:T(8,128)S(1)} %get-tuple-element.73.left_ref, ...), custom_call_target="tpu_custom_call" | custom-call | flops 12079595520 | bytes 4194304 | tf_op jit(solution)/shard_map/pallas_call | solution.py:205
  59.2 1.6 %shard_map.106 = (bf16[512,512]{1,0:T(8,128)(2,1)S(1)}, f32[512,512]{1,0:T(8,128)S(1)}) custom-call(bf16[512,1024]{1,0:T(8,128)(2,1)S(1)} %bitcast.110, bf16[512,1024]{1,0:T(8,128)(2,1)S(1)} %get-tuple-element.38.columns_ref), custom_call_target="tpu_custom_call" | custom-call | flops 536870912 | bytes 3145728 | tf_op jit(solution)/shard_map/pallas_call | solution.py:82
  60.8 1.6 %shard_map.103 = (bf16[512,512]{1,0:T(8,128)(2,1)S(1)}, f32[512,512]{1,0:T(8,128)S(1)}) custom-call(bf16[512,1024]{1,0:T(8,128)(2,1)S(1)} %bitcast.111, bf16[512,1024]{1,0:T(8,128)(2,1)S(1)} %get-tuple-element.38.columns_ref), custom_call_target="tpu_custom_call" | custom-call | flops 536870912 | bytes 3145728 | tf_op jit(solution)/shard_map/pallas_call | solution.py:82
  63.4 2.8 %collective-permute-start.10 = (bf16[2,64,512]{2,1,0:T(8,128)(2,1)S(1)}, bf16[2,64,512]{2,1,0:T(8,128)(2,1)S(1)}, u32[]{:S(2)}, u32[]{:S(2)}) collective-permute-start(bf16[2,64,512]{2,1,0:T(8,128)(2,1)S(1)} %fusion.6), channel_id=1, source_target_pairs={{0,8},{8,0},{1,9},{9,1},{2,10},{10,2},{3,11},{11,3},{4,12},{12,4},... | collective-permute-start | bytes 393224 | tf_op jit(solution)/shard_map/ppermute | solution.py:19
  66.4 2.3 %add_convert_fusion = bf16[512,1024]{1,0:T(8,128)(2,1)} fusion(bf16[512,1024]{1,0:T(8,128)(2,1)S(1)} %bitcast.115, bf16[512,1024]{1,0:T(8,128)(2,1)S(1)} %get-tuple-element.38.columns_ref, bf16[1024,1024]{1,0:T(8,128)(2,1)S(1)} %copy-done.11), kind=kOutput, calls=%fused_computation | convolution fusion | flops 1075314688 | bytes 5242880 | tf_op jit(solution)/shard_map/dot_general | solution.py:314
  68.7 7.5 %collective-permute-done.10 = bf16[2,64,512]{2,1,0:T(8,128)(2,1)S(1)} collective-permute-done((bf16[2,64,512]{2,1,0:T(8,128)(2,1)S(1)}, bf16[2,64,512]{2,1,0:T(8,128)(2,1)S(1)}, u32[]{:S(2)}, u32[]{:S(2)}) %collective-permute-start.10) | collective-permute-done | bytes 131104 | tf_op jit(solution)/shard_map/ppermute | solution.py:19
  76.3 2.5 %collective-permute-done.9 = bf16[2,64,512]{2,1,0:T(8,128)(2,1)S(1)} collective-permute-done((bf16[2,64,512]{2,1,0:T(8,128)(2,1)S(1)}, bf16[2,64,512]{2,1,0:T(8,128)(2,1)S(1)}, u32[]{:S(2)}, u32[]{:S(2)}) %collective-permute-start.9) | collective-permute-done | bytes 131104 | tf_op jit(solution)/shard_map/ppermute | solution.py:19
  79.3 1.7 %collective-permute-start.15 = (bf16[64,512]{1,0:T(8,128)(2,1)S(1)}, bf16[64,512]{1,0:T(8,128)(2,1)S(1)}, u32[]{:S(2)}, u32[]{:S(2)}) collective-permute-start(bf16[64,512]{1,0:T(8,128)(2,1)S(1)} %fusion.11), channel_id=1, source_target_pairs={{0,2},{2,0},{1,3},{3,1},{4,6},{6,4},{5,7},{7,5},{8,10},{10,8},{9,1... | collective-permute-start | bytes 196616 | tf_op jit(solution)/shard_map/ppermute | solution.py:19
  83.7 1.7 %collective-permute-start.16 = (bf16[2,2,64,512]{3,2,0,1:T(8,128)(2,1)S(1)}, bf16[2,2,64,512]{3,2,0,1:T(8,128)(2,1)S(1)}, u32[]{:S(2)}, u32[]{:S(2)}) collective-permute-start(bf16[2,2,64,512]{3,2,0,1:T(8,128)(2,1)S(1)} %fusion.2), channel_id=1, source_target_pairs={{0,2},{2,0},{1,3},{3,1},{4,6},{6,4},{5,7},{7,5},{8,10},{10,8},{9,1... | collective-permute-start | bytes 786440 | tf_op jit(solution)/shard_map/ppermute | solution.py:19
  85.6 3.7 %collective-permute-done.18 = bf16[2,2,64,288]{3,2,1,0:T(8,128)(2,1)S(1)} collective-permute-done((bf16[2,2,64,288]{3,2,1,0:T(8,128)(2,1)S(1)}, bf16[2,2,64,288]{3,2,1,0:T(8,128)(2,1)S(1)}, u32[]{:S(2)}, u32[]{:S(2)}) %collective-permute-start.18) | collective-permute-done | bytes 147488 | tf_op jit(solution)/shard_map/ppermute | solution.py:19
  89.4 3.8 %collective-permute-done.17 = bf16[2,2,64,512]{3,2,1,0:T(8,128)(2,1)S(1)} collective-permute-done((bf16[2,2,64,512]{3,2,1,0:T(8,128)(2,1)S(1)}, bf16[2,2,64,512]{3,2,1,0:T(8,128)(2,1)S(1)}, u32[]{:S(2)}, u32[]{:S(2)}) %collective-permute-start.17) | collective-permute-done | bytes 262176 | tf_op jit(solution)/shard_map/ppermute | solution.py:19
  93.4 2.7 %collective-permute-start.21 = (bf16[2,64,288]{2,1,0:T(8,128)(2,1)S(1)}, bf16[2,64,288]{2,1,0:T(8,128)(2,1)S(1)}, u32[]{:S(2)}, u32[]{:S(2)}) collective-permute-start(bf16[2,64,288]{2,1,0:T(8,128)(2,1)S(1)} %fusion.9), channel_id=1, source_target_pairs={{0,8},{8,0},{1,9},{9,1},{2,10},{10,2},{3,11},{11,3},{4,12},{12,4},... | collective-permute-start | bytes 221192 | tf_op jit(solution)/shard_map/ppermute | solution.py:19
  98.0 4.5 %collective-permute-done.21 = bf16[2,64,288]{2,1,0:T(8,128)(2,1)S(1)} collective-permute-done((bf16[2,64,288]{2,1,0:T(8,128)(2,1)S(1)}, bf16[2,64,288]{2,1,0:T(8,128)(2,1)S(1)}, u32[]{:S(2)}, u32[]{:S(2)}) %collective-permute-start.21) | collective-permute-done | bytes 73760 | tf_op jit(solution)/shard_map/ppermute | solution.py:19
  102.5 3.2 %collective-permute-done.20 = bf16[2,64,512]{2,1,0:T(8,128)(2,1)S(1)} collective-permute-done((bf16[2,64,512]{2,1,0:T(8,128)(2,1)S(1)}, bf16[2,64,512]{2,1,0:T(8,128)(2,1)S(1)}, u32[]{:S(2)}, u32[]{:S(2)}) %collective-permute-start.20) | collective-permute-done | bytes 131104 | tf_op jit(solution)/shard_map/ppermute | solution.py:19
  110.6 2.1 %collective-permute-done.23 = bf16[64,512]{1,0:T(8,128)(2,1)S(1)} collective-permute-done((bf16[64,512]{1,0:T(8,128)(2,1)S(1)}, bf16[64,512]{1,0:T(8,128)(2,1)S(1)}, u32[]{:S(2)}, u32[]{:S(2)}) %collective-permute-start.23) | collective-permute-done | bytes 65568 | tf_op jit(solution)/shard_map/ppermute | solution.py:19
  (112 shorter events, 27.5 us)
Async XLA Ops:
  3.1 26.5 %collective-permute-start.3 = (bf16[4,256,256]{2,1,0:T(8,128)(2,1)}, bf16[4,256,256]{2,1,0:T(8,128)(2,1)}, u32[]{:S(2)}, u32[]{:S(2)}) collective-permute-start(bf16[4,256,256]{2,1,0:T(8,128)(2,1)} %get-tuple-element.35), channel_id=1, source_target_pairs={{0,2},{2,0},{1,3},{3,1},{4,6},{6,4},{5,7},{7,5},{8,10},{10,8},{9,1... | collective-permute-start | bytes 1572872 | tf_op jit(solution)/shard_map/ppermute | solution.py:19
  8.2 15.6 %collective-permute-start.1 = (bf16[1,128,1024]{2,1,0:T(8,128)(2,1)}, bf16[1,128,1024]{2,1,0:T(8,128)(2,1)S(1)}, u32[]{:S(2)}, u32[]{:S(2)}) collective-permute-start(bf16[1,128,1024]{2,1,0:T(8,128)(2,1)} %get-tuple-element.70), channel_id=1, source_target_pairs={{2,0},{3,1},{4,2},{5,3},{6,4},{7,5},{8,6},{9,7},{10,8},{11,9},{12,... | collective-permute-start | bytes 786440 | tf_op jit(solution)/shard_map/ppermute | solution.py:25
  9.5 19.3 %collective-permute-start = (bf16[1,128,1024]{2,1,0:T(8,128)(2,1)}, bf16[1,128,1024]{2,1,0:T(8,128)(2,1)}, u32[]{:S(2)}, u32[]{:S(2)}) collective-permute-start(bf16[1,128,1024]{2,1,0:T(8,128)(2,1)} %get-tuple-element.71), channel_id=1, source_target_pairs={{0,2},{1,3},{2,4},{3,5},{4,6},{5,7},{6,8},{7,9},{8,10},{9,11},{10,... | collective-permute-start | bytes 786440 | tf_op jit(solution)/shard_map/ppermute | solution.py:25
  17.5 14.6 %collective-permute-start.7 = (bf16[2,2,2,64,512]{4,3,2,0,1:T(8,128)(2,1)}, bf16[2,2,2,64,512]{4,3,2,0,1:T(8,128)(2,1)}, u32[]{:S(2)}, u32[]{:S(2)}) collective-permute-start(bf16[2,2,2,64,512]{4,3,2,0,1:T(8,128)(2,1)} %copy.27), channel_id=1, source_target_pairs={{0,1},{1,0},{2,3},{3,2},{4,5},{5,4},{6,7},{7,6},{8,9},{9,8},{10,11... | collective-permute-start | bytes 1572872 | tf_op jit(solution)/shard_map/ppermute | solution.py:19
  20.9 15.0 %collective-permute-start.5 = (bf16[2,2,2,64,512]{4,3,2,0,1:T(8,128)(2,1)}, bf16[2,2,2,64,512]{4,3,2,0,1:T(8,128)(2,1)}, u32[]{:S(2)}, u32[]{:S(2)}) collective-permute-start(bf16[2,2,2,64,512]{4,3,2,0,1:T(8,128)(2,1)} %copy.25), channel_id=1, source_target_pairs={{0,1},{1,0},{2,3},{3,2},{4,5},{5,4},{6,7},{7,6},{8,9},{9,8},{10,11... | collective-permute-start | bytes 1572872 | tf_op jit(solution)/shard_map/ppermute | solution.py:19
  29.6 7.8 %collective-permute-start.2 = (bf16[6,1024]{1,0:T(8,128)(2,1)S(1)}, bf16[6,1024]{1,0:T(8,128)(2,1)S(1)}, u32[]{:S(2)}, u32[]{:S(2)}) collective-permute-start(bf16[6,1024]{1,0:T(8,128)(2,1)S(1)} %pad_maximum_fusion.2), channel_id=1, source_target_pairs={{0,1},{1,0},{2,3},{3,2},{4,5},{5,4},{6,7},{7,6},{8,9},{9,8},{10,11... | collective-permute-start | bytes 36872 | tf_op jit(solution)/shard_map/ppermute | solution.py:19
  31.5 16.6 %collective-permute-start.4 = (bf16[2,4,128,256]{3,2,1,0:T(8,128)(2,1)S(1)}, bf16[2,4,128,256]{3,2,1,0:T(8,128)(2,1)S(1)}, u32[]{:S(2)}, u32[]{:S(2)}) collective-permute-start(bf16[2,4,128,256]{3,2,1,0:T(8,128)(2,1)S(1)} %get-tuple-element.65), channel_id=1, source_target_pairs={{0,1},{1,0},{2,3},{3,2},{4,5},{5,4},{6,7},{7,6},{8,9},{9,8},{10,11... | collective-permute-start | bytes 1572872 | tf_op jit(solution)/shard_map/ppermute | solution.py:19
  33.4 9.7 %collective-permute-start.8 = (bf16[2,2,64,512]{3,2,1,0:T(8,128)(2,1)S(1)}, bf16[2,2,64,512]{3,2,1,0:T(8,128)(2,1)S(1)}, u32[]{:S(2)}, u32[]{:S(2)}) collective-permute-start(bf16[2,2,64,512]{3,2,1,0:T(8,128)(2,1)S(1)} %fusion.1), channel_id=1, source_target_pairs={{0,4},{4,0},{1,5},{5,1},{2,6},{6,2},{3,7},{7,3},{8,12},{12,8},{9,1... | collective-permute-start | bytes 786440 | tf_op jit(solution)/shard_map/ppermute | solution.py:19
  37.2 10.9 %collective-permute-start.6 = (bf16[2,2,64,512]{3,2,1,0:T(8,128)(2,1)S(1)}, bf16[2,2,64,512]{3,2,1,0:T(8,128)(2,1)S(1)}, u32[]{:S(2)}, u32[]{:S(2)}) collective-permute-start(bf16[2,2,64,512]{3,2,1,0:T(8,128)(2,1)S(1)} %fusion), channel_id=1, source_target_pairs={{0,4},{4,0},{1,5},{5,1},{2,6},{6,2},{3,7},{7,3},{8,12},{12,8},{9,1... | collective-permute-start | bytes 786440 | tf_op jit(solution)/shard_map/ppermute | solution.py:19
  62.5 16.3 %collective-permute-start.13 = (bf16[2,2,2,64,288]{4,3,2,1,0:T(8,128)(2,1)S(1)}, bf16[2,2,2,64,288]{4,3,2,1,0:T(8,128)(2,1)S(1)}, u32[]{:S(2)}, u32[]{:S(2)}) collective-permute-start(bf16[2,2,2,64,288]{4,3,2,1,0:T(8,128)(2,1)S(1)} %bitcast.133), channel_id=1, source_target_pairs={{0,1},{1,0},{2,3},{3,2},{4,5},{5,4},{6,7},{7,6},{8,9},{9,8},{10,11... | collective-permute-start | bytes 884744 | tf_op jit(solution)/shard_map/ppermute | solution.py:19
  62.6 16.3 %collective-permute-start.11 = (bf16[2,2,2,64,512]{4,3,0,1,2:T(8,128)(2,1)S(1)}, bf16[2,2,2,64,512]{4,3,0,1,2:T(8,128)(2,1)S(1)}, u32[]{:S(2)}, u32[]{:S(2)}) collective-permute-start(bf16[2,2,2,64,512]{4,3,0,1,2:T(8,128)(2,1)S(1)} %copy.29), channel_id=1, source_target_pairs={{0,1},{1,0},{2,3},{3,2},{4,5},{5,4},{6,7},{7,6},{8,9},{9,8},{10,11... | collective-permute-start | bytes 1572872 | tf_op jit(solution)/shard_map/ppermute | solution.py:19
  63.2 15.9 %collective-permute-start.12 = (bf16[2,2,2,64,512]{4,3,2,0,1:T(8,128)(2,1)S(1)}, bf16[2,2,2,64,512]{4,3,2,0,1:T(8,128)(2,1)S(1)}, u32[]{:S(2)}, u32[]{:S(2)}) collective-permute-start(bf16[2,2,2,64,512]{4,3,2,0,1:T(8,128)(2,1)S(1)} %copy.31), channel_id=1, source_target_pairs={{0,1},{1,0},{2,3},{3,2},{4,5},{5,4},{6,7},{7,6},{8,9},{9,8},{10,11... | collective-permute-start | bytes 1572872 | tf_op jit(solution)/shard_map/ppermute | solution.py:19
  63.4 12.9 %collective-permute-start.10 = (bf16[2,64,512]{2,1,0:T(8,128)(2,1)S(1)}, bf16[2,64,512]{2,1,0:T(8,128)(2,1)S(1)}, u32[]{:S(2)}, u32[]{:S(2)}) collective-permute-start(bf16[2,64,512]{2,1,0:T(8,128)(2,1)S(1)} %fusion.6), channel_id=1, source_target_pairs={{0,8},{8,0},{1,9},{9,1},{2,10},{10,2},{3,11},{11,3},{4,12},{12,4},... | collective-permute-start | bytes 393224 | tf_op jit(solution)/shard_map/ppermute | solution.py:19
  66.2 12.6 %collective-permute-start.9 = (bf16[2,64,512]{2,1,0:T(8,128)(2,1)S(1)}, bf16[2,64,512]{2,1,0:T(8,128)(2,1)S(1)}, u32[]{:S(2)}, u32[]{:S(2)}) collective-permute-start(bf16[2,64,512]{2,1,0:T(8,128)(2,1)S(1)} %fusion.5), channel_id=1, source_target_pairs={{0,8},{8,0},{1,9},{9,1},{2,10},{10,2},{3,11},{11,3},{4,12},{12,4},... | collective-permute-start | bytes 393224 | tf_op jit(solution)/shard_map/ppermute | solution.py:19
  79.3 6.0 %collective-permute-start.15 = (bf16[64,512]{1,0:T(8,128)(2,1)S(1)}, bf16[64,512]{1,0:T(8,128)(2,1)S(1)}, u32[]{:S(2)}, u32[]{:S(2)}) collective-permute-start(bf16[64,512]{1,0:T(8,128)(2,1)S(1)} %fusion.11), channel_id=1, source_target_pairs={{0,2},{2,0},{1,3},{3,1},{4,6},{6,4},{5,7},{7,5},{8,10},{10,8},{9,1... | collective-permute-start | bytes 196616 | tf_op jit(solution)/shard_map/ppermute | solution.py:19
  81.0 4.6 %collective-permute-start.14 = (bf16[64,512]{1,0:T(8,128)(2,1)S(1)}, bf16[64,512]{1,0:T(8,128)(2,1)S(1)}, u32[]{:S(2)}, u32[]{:S(2)}) collective-permute-start(bf16[64,512]{1,0:T(8,128)(2,1)S(1)} %fusion.10), channel_id=1, source_target_pairs={{0,2},{2,0},{1,3},{3,1},{4,6},{6,4},{5,7},{7,5},{8,10},{10,8},{9,1... | collective-permute-start | bytes 196616 | tf_op jit(solution)/shard_map/ppermute | solution.py:19
  81.5 7.9 %collective-permute-start.18 = (bf16[2,2,64,288]{3,2,1,0:T(8,128)(2,1)S(1)}, bf16[2,2,64,288]{3,2,1,0:T(8,128)(2,1)S(1)}, u32[]{:S(2)}, u32[]{:S(2)}) collective-permute-start(bf16[2,2,64,288]{3,2,1,0:T(8,128)(2,1)S(1)} %fusion.4), channel_id=1, source_target_pairs={{0,4},{4,0},{1,5},{5,1},{2,6},{6,2},{3,7},{7,3},{8,12},{12,8},{9,1... | collective-permute-start | bytes 442376 | tf_op jit(solution)/shard_map/ppermute | solution.py:19
  82.3 10.9 %collective-permute-start.17 = (bf16[2,2,64,512]{3,2,1,0:T(8,128)(2,1)S(1)}, bf16[2,2,64,512]{3,2,1,0:T(8,128)(2,1)S(1)}, u32[]{:S(2)}, u32[]{:S(2)}) collective-permute-start(bf16[2,2,64,512]{3,2,1,0:T(8,128)(2,1)S(1)} %fusion.3), channel_id=1, source_target_pairs={{0,4},{4,0},{1,5},{5,1},{2,6},{6,2},{3,7},{7,3},{8,12},{12,8},{9,1... | collective-permute-start | bytes 786440 | tf_op jit(solution)/shard_map/ppermute | solution.py:19
  83.7 9.6 %collective-permute-start.16 = (bf16[2,2,64,512]{3,2,0,1:T(8,128)(2,1)S(1)}, bf16[2,2,64,512]{3,2,0,1:T(8,128)(2,1)S(1)}, u32[]{:S(2)}, u32[]{:S(2)}) collective-permute-start(bf16[2,2,64,512]{3,2,0,1:T(8,128)(2,1)S(1)} %fusion.2), channel_id=1, source_target_pairs={{0,2},{2,0},{1,3},{3,1},{4,6},{6,4},{5,7},{7,5},{8,10},{10,8},{9,1... | collective-permute-start | bytes 786440 | tf_op jit(solution)/shard_map/ppermute | solution.py:19
  93.4 9.1 %collective-permute-start.21 = (bf16[2,64,288]{2,1,0:T(8,128)(2,1)S(1)}, bf16[2,64,288]{2,1,0:T(8,128)(2,1)S(1)}, u32[]{:S(2)}, u32[]{:S(2)}) collective-permute-start(bf16[2,64,288]{2,1,0:T(8,128)(2,1)S(1)} %fusion.9), channel_id=1, source_target_pairs={{0,8},{8,0},{1,9},{9,1},{2,10},{10,2},{3,11},{11,3},{4,12},{12,4},... | collective-permute-start | bytes 221192 | tf_op jit(solution)/shard_map/ppermute | solution.py:19
  96.1 9.6 %collective-permute-start.20 = (bf16[2,64,512]{2,1,0:T(8,128)(2,1)S(1)}, bf16[2,64,512]{2,1,0:T(8,128)(2,1)S(1)}, u32[]{:S(2)}, u32[]{:S(2)}) collective-permute-start(bf16[2,64,512]{2,1,0:T(8,128)(2,1)S(1)} %fusion.8), channel_id=1, source_target_pairs={{0,8},{8,0},{1,9},{9,1},{2,10},{10,2},{3,11},{11,3},{4,12},{12,4},... | collective-permute-start | bytes 393224 | tf_op jit(solution)/shard_map/ppermute | solution.py:19
  96.5 9.2 %collective-permute-start.19 = (bf16[2,64,512]{2,1,0:T(8,128)(2,1)S(1)}, bf16[2,64,512]{2,1,0:T(8,128)(2,1)S(1)}, u32[]{:S(2)}, u32[]{:S(2)}) collective-permute-start(bf16[2,64,512]{2,1,0:T(8,128)(2,1)S(1)} %fusion.7), channel_id=1, source_target_pairs={{0,4},{4,0},{1,5},{5,1},{2,6},{6,2},{3,7},{7,3},{8,12},{12,8},{9,1... | collective-permute-start | bytes 393224 | tf_op jit(solution)/shard_map/ppermute | solution.py:19
  106.8 5.9 %collective-permute-start.23 = (bf16[64,512]{1,0:T(8,128)(2,1)S(1)}, bf16[64,512]{1,0:T(8,128)(2,1)S(1)}, u32[]{:S(2)}, u32[]{:S(2)}) collective-permute-start(bf16[64,512]{1,0:T(8,128)(2,1)S(1)} %fusion.12), channel_id=1, source_target_pairs={{0,8},{8,0},{1,9},{9,1},{2,10},{10,2},{3,11},{11,3},{4,12},{12,4},... | collective-permute-start | bytes 196616 | tf_op jit(solution)/shard_map/ppermute | solution.py:19
  106.8 5.9 %collective-permute-start.24 = (bf16[64,512]{1,0:T(8,128)(2,1)S(1)}, bf16[64,512]{1,0:T(8,128)(2,1)S(1)}, u32[]{:S(2)}, u32[]{:S(2)}) collective-permute-start(bf16[64,512]{1,0:T(8,128)(2,1)S(1)} %fusion.13), channel_id=1, source_target_pairs={{0,2},{2,0},{1,3},{3,1},{4,6},{6,4},{5,7},{7,5},{8,10},{10,8},{9,1... | collective-permute-start | bytes 196616 | tf_op jit(solution)/shard_map/ppermute | solution.py:19
  (13 other events, 73.2 us)

commit v5 on v4

--- a/solution.py
+++ b/solution.py
@@ -280,27 +280,25 @@
         normalizer,
     )
 
-    high_first = list(range(2, bits)) + [1]
     low_first = list(range(1, bits))
+    high_first = [2, 1] + list(range(3, bits))
     third = []
     third_left = []
     for at in (0, 1):
         piece = halve_start(wgrad_half(third_rows, grad_rows, at, unit, normalizer), bits)
-        left = list(range(1, bits))[::-1]
-        third.append(halve_round(piece, left, high_first[0]))
-        third_left.append(left)
+        third.append(piece)
+        third_left.append(list(range(1, bits))[::-1])
     first_terms = [wgrad_half(input_rows, first_rows, at, unit, normalizer) for at in (0, 1)]
     group_pair = split_term(local_term, unit)
-    third[0], third[1], _ = lax.optimization_barrier((third[0], third[1], first_terms[0][0]))
+    third[0], third[1], _ = lax.optimization_barrier((third[0], third[1], first_rows))
     last = [halve_start(pair, bits) for pair in first_terms + [group_pair]]
     last_left = [list(range(1, bits))[::-1] for _ in last]
-    last_order = [low_first, high_first, high_first]
+    last_order = [low_first, high_first, low_first]
     for at in range(len(high_first)):
-        if at + 1 < len(high_first):
-            third = [
-                halve_round(piece, left, high_first[at + 1])
-                for piece, left in zip(third, third_left)
-            ]
+        third = [
+            halve_round(piece, left, order[at])
+            for piece, left, order in zip(third, third_left, last_order)
+        ]
         tied = lax.optimization_barrier((*third, *last))
         third, last = list(tied[:2]), list(tied[2:])
         last = [

time: 114 us -> 105 us (0.921)
  waiting for transfers between devices: 44.8 us -> 35.8 us
  starting transfers between devices: 30 us -> 28.1 us
  local copies, waits for them, and re-layouts: 8.38 us -> 10.2 us
    ppermute x23, waiting for transfers between devices: 39.1 us -> 22.2 us  [partner(): return lax.ppermute(block, axis, route)]
    ppermute x2, waiting for transfers between devices: 5.71 us -> 13.6 us  [from_behind(): return lax.ppermute(array, axis, pairs)]
    ppermute x2, starting transfers between devices: 6.53 us -> 3.38 us  [from_behind(): return lax.ppermute(array, axis, pairs)]
    unnamed x25 -> x27, local copies, waits for them, and re-layouts: 2.68 us -> 4.68 us
    ppermute x23, starting transfers between devices: 23.4 us -> 24.7 us  [partner(): return lax.ppermute(block, axis, route)]
  transfers between devices with their start and end apart: 25 -> 25, of which waited for: 13 -> 8; matrix products, arithmetic and copies ran while one was open for 13% -> 15% of each run, Pallas kernels for 3% -> 3%
where the time goes in v5:
time: 105 us
  waiting for transfers between devices  35.8 us (34%)
  starting transfers between devices  28.1 us (27%)
  Pallas kernels  17.2 us (16%)
  local copies, waits for them, and re-layouts  10.2 us (10%)
  other arithmetic  8.46 us (8%)
  matrix products  3.54 us (3%)
  between operations  1.34 us (1%)
    ppermute x23, starting transfers between devices, partner(): return lax.ppermute(block, axis, route)  24.7 us
    ppermute x23, waiting for transfers between devices, partner(): return lax.ppermute(block, axis, route)  22.2 us
    ppermute x2, waiting for transfers between devices, from_behind(): return lax.ppermute(array, axis, pairs)  13.6 us
    pallas_call x1, Pallas kernels, group_backward(): pl.pallas_call(functools.partial(group_kernel, tile_rows, width, taps //...  10.8 us
    pallas_call x4, Pallas kernels, wgrad_half(): pl.pallas_call(functools.partial(wgrad_kernel, unit, normalizer), grid=(c...  6.35 us
    unnamed x27, local copies, waits for them, and re-layouts  4.68 us
    ppermute x2, starting transfers between devices, from_behind(): return lax.ppermute(array, axis, pairs)  3.38 us
    add x5, other arithmetic, halve_start(): return shards_view(kept, bits - 1) + received.astype(jnp.float32)  3.07 us
  transfers between devices with their start and end apart: 25, of which 8 were waited for; matrix products, arithmetic and copies ran while one was open for 15% of the time, Pallas kernels for 3%

profile of v5, /device:TPU:0, one launch (start us, length us, event | category | flops | bytes accessed | tf_op | source)
XLA Modules:
  0.0 104.6 jit_solution(3179433569602962747)
XLA Ops:
  0.7 2.4 %constant_dynamic-slice_fusion.1 = (bf16[1,4,256,256]{3,2,1,0:T(8,128)(2,1)}, bf16[4,256,256]{2,1,0:T(8,128)(2,1)}) fusion(bf16[2,4,256,256]{3,2,1,0:T(8,128)(2,1)} %bitcast.131, s32[]{:T(128)S(6)} %select_n.235, s32[]{:T(128)S(6)} %select_n.218), kind=kLoop, calls=%fused_computation.66 | loop fusion | bytes 2097160 | tf_op jit(solution)/shard_map/jit(dynamic_index_in_dim)/dynamic_slice | solution.py:249
  3.1 2.9 %collective-permute-start.3 = (bf16[4,256,256]{2,1,0:T(8,128)(2,1)}, bf16[4,256,256]{2,1,0:T(8,128)(2,1)}, u32[]{:S(2)}, u32[]{:S(2)}) collective-permute-start(bf16[4,256,256]{2,1,0:T(8,128)(2,1)} %get-tuple-element.35), channel_id=1, source_target_pairs={{0,2},{2,0},{1,3},{3,1},{4,6},{6,4},{5,7},{7,5},{8,10},{10,8},{9,1... | collective-permute-start | bytes 1572872 | tf_op jit(solution)/shard_map/ppermute | solution.py:19
  8.2 2.1 %collective-permute-start = (bf16[1,128,1024]{2,1,0:T(8,128)(2,1)}, bf16[1,128,1024]{2,1,0:T(8,128)(2,1)S(1)}, u32[]{:S(2)}, u32[]{:S(2)}) collective-permute-start(bf16[1,128,1024]{2,1,0:T(8,128)(2,1)} %get-tuple-element.71), channel_id=1, source_target_pairs={{0,2},{1,3},{2,4},{3,5},{4,6},{5,7},{6,8},{7,9},{8,10},{9,11},{10,... | collective-permute-start | bytes 786440 | tf_op jit(solution)/shard_map/ppermute | solution.py:25
  11.6 1.6 %shard_map.105 = (bf16[512,512]{1,0:T(8,128)(2,1)S(1)}, f32[512,512]{1,0:T(8,128)S(1)}) custom-call(bf16[512,1024]{1,0:T(8,128)(2,1)S(1)} %bitcast.108, bf16[512,1024]{1,0:T(8,128)(2,1)S(1)} %bitcast.113), custom_call_target="tpu_custom_call" | custom-call | flops 536870912 | bytes 3145728 | tf_op jit(solution)/shard_map/pallas_call | solution.py:82
  15.2 13.6 %collective-permute-done = bf16[1,128,1024]{2,1,0:T(8,128)(2,1)S(1)} collective-permute-done((bf16[1,128,1024]{2,1,0:T(8,128)(2,1)}, bf16[1,128,1024]{2,1,0:T(8,128)(2,1)S(1)}, u32[]{:S(2)}, u32[]{:S(2)}) %collective-permute-start) | collective-permute-done | bytes 262176 | tf_op jit(solution)/shard_map/ppermute | solution.py:25
  30.9 1.6 %shard_map.104 = (bf16[512,512]{1,0:T(8,128)(2,1)S(1)}, f32[512,512]{1,0:T(8,128)S(1)}) custom-call(bf16[512,1024]{1,0:T(8,128)(2,1)S(1)} %bitcast.109, bf16[512,1024]{1,0:T(8,128)(2,1)S(1)} %bitcast.114), custom_call_target="tpu_custom_call" | custom-call | flops 536870912 | bytes 3145728 | tf_op jit(solution)/shard_map/pallas_call | solution.py:82
  36.3 1.8 %maximum_select_fusion = bf16[2,4,2,128,256]{4,3,2,1,0:T(8,128)(2,1)S(1)} fusion(bf16[1,4,2,128,256]{4,3,2,1,0:T(8,128)(2,1)} %bitcast.13, bf16[1,4,2,128,256]{4,3,2,1,0:T(8,128)(2,1)} %bitcast.130, pred[]{:T(512)S(6)} %eq.34), kind=kLoop, calls=%fused_computation.2 | loop fusion | flops 1572864 | bytes 2097153 | tf_op jit(solution)/shard_map/jit(_where)/select_n | solution.py:104
  41.2 10.8 %shard_map.102 = (bf16[512,1024]{1,0:T(8,128)(2,1)S(1)}, f32[1024,288]{1,0:T(8,128)S(1)}) custom-call(bf16[512,1024]{1,0:T(8,128)(2,1)S(1)} %copy-done.11, bf16[128,1024]{1,0:T(8,128)(2,1)S(1)} %bitcast.128, bf16[128,1024]{1,0:T(8,128)(2,1)} %bitcast.7.bottom_ref, f32[6,1024]{1,0:T(8,128)S(1)} %get-tuple-element.73.left_ref, ...), custom_call_target="tpu_custom_call" | custom-call | flops 12079595520 | bytes 4194304 | tf_op jit(solution)/shard_map/pallas_call | solution.py:205
  52.0 1.6 %shard_map.103 = (bf16[512,512]{1,0:T(8,128)(2,1)S(1)}, f32[512,512]{1,0:T(8,128)S(1)}) custom-call(bf16[512,1024]{1,0:T(8,128)(2,1)S(1)} %bitcast.110, bf16[512,1024]{1,0:T(8,128)(2,1)S(1)} %get-tuple-element.38.columns_ref), custom_call_target="tpu_custom_call" | custom-call | flops 536870912 | bytes 3145728 | tf_op jit(solution)/shard_map/pallas_call | solution.py:82
  53.6 1.6 %shard_map.106 = (bf16[512,512]{1,0:T(8,128)(2,1)S(1)}, f32[512,512]{1,0:T(8,128)S(1)}) custom-call(bf16[512,1024]{1,0:T(8,128)(2,1)S(1)} %bitcast.111, bf16[512,1024]{1,0:T(8,128)(2,1)S(1)} %get-tuple-element.38.columns_ref), custom_call_target="tpu_custom_call" | custom-call | flops 536870912 | bytes 3145728 | tf_op jit(solution)/shard_map/pallas_call | solution.py:82
  56.5 2.6 %collective-permute-start.8 = (bf16[2,2,64,512]{3,2,0,1:T(8,128)(2,1)S(1)}, bf16[2,2,64,512]{3,2,0,1:T(8,128)(2,1)S(1)}, u32[]{:S(2)}, u32[]{:S(2)}) collective-permute-start(bf16[2,2,64,512]{3,2,0,1:T(8,128)(2,1)S(1)} %fusion.1), channel_id=1, source_target_pairs={{0,4},{4,0},{1,5},{5,1},{2,6},{6,2},{3,7},{7,3},{8,12},{12,8},{9,1... | collective-permute-start | bytes 786440 | tf_op jit(solution)/shard_map/ppermute | solution.py:19
  59.1 1.5 %collective-permute-start.7 = (bf16[2,2,64,512]{3,2,0,1:T(8,128)(2,1)S(1)}, bf16[2,2,64,512]{3,2,0,1:T(8,128)(2,1)S(1)}, u32[]{:S(2)}, u32[]{:S(2)}) collective-permute-start(bf16[2,2,64,512]{3,2,0,1:T(8,128)(2,1)S(1)} %fusion), channel_id=1, source_target_pairs={{0,2},{2,0},{1,3},{3,1},{4,6},{6,4},{5,7},{7,5},{8,10},{10,8},{9,1... | collective-permute-start | bytes 786440 | tf_op jit(solution)/shard_map/ppermute | solution.py:19
  60.6 2.3 %add_convert_fusion = bf16[512,1024]{1,0:T(8,128)(2,1)} fusion(bf16[512,1024]{1,0:T(8,128)(2,1)S(1)} %bitcast.115, bf16[512,1024]{1,0:T(8,128)(2,1)S(1)} %get-tuple-element.38.columns_ref, bf16[1024,1024]{1,0:T(8,128)(2,1)S(1)} %copy-done.12), kind=kOutput, calls=%fused_computation | convolution fusion | flops 1075314688 | bytes 5242880 | tf_op jit(solution)/shard_map/dot_general | solution.py:312
  62.9 4.3 %collective-permute-done.7 = bf16[2,2,64,512]{3,2,0,1:T(8,128)(2,1)S(1)} collective-permute-done((bf16[2,2,64,512]{3,2,0,1:T(8,128)(2,1)S(1)}, bf16[2,2,64,512]{3,2,0,1:T(8,128)(2,1)S(1)}, u32[]{:S(2)}, u32[]{:S(2)}) %collective-permute-start.7) | collective-permute-done | bytes 262176 | tf_op jit(solution)/shard_map/ppermute | solution.py:19
  70.6 1.6 %collective-permute-start.14 = (bf16[2,2,64,512]{3,2,0,1:T(8,128)(2,1)S(1)}, bf16[2,2,64,512]{3,2,0,1:T(8,128)(2,1)S(1)}, u32[]{:S(2)}, u32[]{:S(2)}) collective-permute-start(bf16[2,2,64,512]{3,2,0,1:T(8,128)(2,1)S(1)} %fusion.2), channel_id=1, source_target_pairs={{0,2},{2,0},{1,3},{3,1},{4,6},{6,4},{5,7},{7,5},{8,10},{10,8},{9,1... | collective-permute-start | bytes 786440 | tf_op jit(solution)/shard_map/ppermute | solution.py:19
  72.2 1.6 %collective-permute-start.12 = (bf16[2,64,512]{2,1,0:T(8,128)(2,1)S(1)}, bf16[2,64,512]{2,1,0:T(8,128)(2,1)S(1)}, u32[]{:S(2)}, u32[]{:S(2)}) collective-permute-start(bf16[2,64,512]{2,1,0:T(8,128)(2,1)S(1)} %fusion.5), channel_id=1, source_target_pairs={{0,4},{4,0},{1,5},{5,1},{2,6},{6,2},{3,7},{7,3},{8,12},{12,8},{9,1... | collective-permute-start | bytes 393224 | tf_op jit(solution)/shard_map/ppermute | solution.py:19
  73.9 4.8 %collective-permute-done.13 = bf16[2,64,512]{2,1,0:T(8,128)(2,1)S(1)} collective-permute-done((bf16[2,64,512]{2,1,0:T(8,128)(2,1)S(1)}, bf16[2,64,512]{2,1,0:T(8,128)(2,1)S(1)}, u32[]{:S(2)}, u32[]{:S(2)}) %collective-permute-start.13) | collective-permute-done | bytes 131104 | tf_op jit(solution)/shard_map/ppermute | solution.py:19
  79.4 2.8 %collective-permute-done.14 = bf16[2,2,64,512]{3,2,0,1:T(8,128)(2,1)S(1)} collective-permute-done((bf16[2,2,64,512]{3,2,0,1:T(8,128)(2,1)S(1)}, bf16[2,2,64,512]{3,2,0,1:T(8,128)(2,1)S(1)}, u32[]{:S(2)}, u32[]{:S(2)}) %collective-permute-start.14) | collective-permute-done | bytes 262176 | tf_op jit(solution)/shard_map/ppermute | solution.py:19
  84.4 1.6 %collective-permute-start.19 = (bf16[2,64,512]{2,1,0:T(8,128)(2,1)S(1)}, bf16[2,64,512]{2,1,0:T(8,128)(2,1)S(1)}, u32[]{:S(2)}, u32[]{:S(2)}) collective-permute-start(bf16[2,64,512]{2,1,0:T(8,128)(2,1)S(1)} %fusion.7), channel_id=1, source_target_pairs={{0,4},{4,0},{1,5},{5,1},{2,6},{6,2},{3,7},{7,3},{8,12},{12,8},{9,1... | collective-permute-start | bytes 393224 | tf_op jit(solution)/shard_map/ppermute | solution.py:19
  86.0 1.8 %collective-permute-start.18 = (bf16[64,512]{1,0:T(8,128)(2,1)S(1)}, bf16[64,512]{1,0:T(8,128)(2,1)S(1)}, u32[]{:S(2)}, u32[]{:S(2)}) collective-permute-start(bf16[64,512]{1,0:T(8,128)(2,1)S(1)} %fusion.11), channel_id=1, source_target_pairs={{0,8},{8,0},{1,9},{9,1},{2,10},{10,2},{3,11},{11,3},{4,12},{12,4},... | collective-permute-start | bytes 196616 | tf_op jit(solution)/shard_map/ppermute | solution.py:19
  89.1 2.2 %collective-permute-done.18 = bf16[64,512]{1,0:T(8,128)(2,1)S(1)} collective-permute-done((bf16[64,512]{1,0:T(8,128)(2,1)S(1)}, bf16[64,512]{1,0:T(8,128)(2,1)S(1)}, u32[]{:S(2)}, u32[]{:S(2)}) %collective-permute-start.18) | collective-permute-done | bytes 65568 | tf_op jit(solution)/shard_map/ppermute | solution.py:19
  91.3 2.6 %collective-permute-done.17 = bf16[64,512]{1,0:T(8,128)(2,1)S(1)} collective-permute-done((bf16[64,512]{1,0:T(8,128)(2,1)S(1)}, bf16[64,512]{1,0:T(8,128)(2,1)S(1)}, u32[]{:S(2)}, u32[]{:S(2)}) %collective-permute-start.17) | collective-permute-done | bytes 65568 | tf_op jit(solution)/shard_map/ppermute | solution.py:19
  94.5 2.6 %collective-permute-start.24 = (bf16[64,512]{1,0:T(8,128)(2,1)S(1)}, bf16[64,512]{1,0:T(8,128)(2,1)S(1)}, u32[]{:S(2)}, u32[]{:S(2)}) collective-permute-start(bf16[64,512]{1,0:T(8,128)(2,1)S(1)} %fusion.13), channel_id=1, source_target_pairs={{0,8},{8,0},{1,9},{9,1},{2,10},{10,2},{3,11},{11,3},{4,12},{12,4},... | collective-permute-start | bytes 196616 | tf_op jit(solution)/shard_map/ppermute | solution.py:19
  98.3 4.9 %collective-permute-done.22 = bf16[64,288]{1,0:T(8,128)(2,1)S(1)} collective-permute-done((bf16[64,288]{1,0:T(8,128)(2,1)S(1)}, bf16[64,288]{1,0:T(8,128)(2,1)S(1)}, u32[]{:S(2)}, u32[]{:S(2)}) %collective-permute-start.22) | collective-permute-done | bytes 36896 | tf_op jit(solution)/shard_map/ppermute | solution.py:19
  (114 shorter events, 26.0 us)
Async XLA Ops:
  3.1 33.2 %collective-permute-start.3 = (bf16[4,256,256]{2,1,0:T(8,128)(2,1)}, bf16[4,256,256]{2,1,0:T(8,128)(2,1)}, u32[]{:S(2)}, u32[]{:S(2)}) collective-permute-start(bf16[4,256,256]{2,1,0:T(8,128)(2,1)} %get-tuple-element.35), channel_id=1, source_target_pairs={{0,2},{2,0},{1,3},{3,1},{4,6},{6,4},{5,7},{7,5},{8,10},{10,8},{9,1... | collective-permute-start | bytes 1572872 | tf_op jit(solution)/shard_map/ppermute | solution.py:19
  8.2 20.6 %collective-permute-start = (bf16[1,128,1024]{2,1,0:T(8,128)(2,1)}, bf16[1,128,1024]{2,1,0:T(8,128)(2,1)S(1)}, u32[]{:S(2)}, u32[]{:S(2)}) collective-permute-start(bf16[1,128,1024]{2,1,0:T(8,128)(2,1)} %get-tuple-element.71), channel_id=1, source_target_pairs={{0,2},{1,3},{2,4},{3,5},{4,6},{5,7},{6,8},{7,9},{8,10},{9,11},{10,... | collective-permute-start | bytes 786440 | tf_op jit(solution)/shard_map/ppermute | solution.py:25
  10.3 18.5 %collective-permute-start.1 = (bf16[1,128,1024]{2,1,0:T(8,128)(2,1)}, bf16[1,128,1024]{2,1,0:T(8,128)(2,1)}, u32[]{:S(2)}, u32[]{:S(2)}) collective-permute-start(bf16[1,128,1024]{2,1,0:T(8,128)(2,1)} %get-tuple-element.70), channel_id=1, source_target_pairs={{2,0},{3,1},{4,2},{5,3},{6,4},{7,5},{8,6},{9,7},{10,8},{11,9},{12,... | collective-permute-start | bytes 786440 | tf_op jit(solution)/shard_map/ppermute | solution.py:25
  15.1 23.2 %collective-permute-start.6 = (bf16[2,2,2,64,512]{4,3,0,2,1:T(8,128)(2,1)}, bf16[2,2,2,64,512]{4,3,0,2,1:T(8,128)(2,1)}, u32[]{:S(2)}, u32[]{:S(2)}) collective-permute-start(bf16[2,2,2,64,512]{4,3,0,2,1:T(8,128)(2,1)} %copy.27), channel_id=1, source_target_pairs={{0,1},{1,0},{2,3},{3,2},{4,5},{5,4},{6,7},{7,6},{8,9},{9,8},{10,11... | collective-permute-start | bytes 1572872 | tf_op jit(solution)/shard_map/ppermute | solution.py:19
  29.6 6.7 %collective-permute-start.2 = (bf16[6,1024]{1,0:T(8,128)(2,1)S(1)}, bf16[6,1024]{1,0:T(8,128)(2,1)S(1)}, u32[]{:S(2)}, u32[]{:S(2)}) collective-permute-start(bf16[6,1024]{1,0:T(8,128)(2,1)S(1)} %pad_maximum_fusion.2), channel_id=1, source_target_pairs={{0,1},{1,0},{2,3},{3,2},{4,5},{5,4},{6,7},{7,6},{8,9},{9,8},{10,11... | collective-permute-start | bytes 36872 | tf_op jit(solution)/shard_map/ppermute | solution.py:19
  34.3 5.3 %collective-permute-start.5 = (bf16[2,2,2,64,512]{4,3,0,1,2:T(8,128)(2,1)}, bf16[2,2,2,64,512]{4,3,0,1,2:T(8,128)(2,1)}, u32[]{:S(2)}, u32[]{:S(2)}) collective-permute-start(bf16[2,2,2,64,512]{4,3,0,1,2:T(8,128)(2,1)} %copy.25), channel_id=1, source_target_pairs={{0,1},{1,0},{2,3},{3,2},{4,5},{5,4},{6,7},{7,6},{8,9},{9,8},{10,11... | collective-permute-start | bytes 1572872 | tf_op jit(solution)/shard_map/ppermute | solution.py:19
  55.3 12.3 %collective-permute-start.10 = (bf16[2,2,2,64,512]{4,3,0,2,1:T(8,128)(2,1)S(1)}, bf16[2,2,2,64,512]{4,3,0,2,1:T(8,128)(2,1)S(1)}, u32[]{:S(2)}, u32[]{:S(2)}) collective-permute-start(bf16[2,2,2,64,512]{4,3,0,2,1:T(8,128)(2,1)S(1)} %copy.31), channel_id=1, source_target_pairs={{0,1},{1,0},{2,3},{3,2},{4,5},{5,4},{6,7},{7,6},{8,9},{9,8},{10,11... | collective-permute-start | bytes 1572872 | tf_op jit(solution)/shard_map/ppermute | solution.py:19
  55.8 12.0 %collective-permute-start.9 = (bf16[2,2,2,64,512]{4,3,0,1,2:T(8,128)(2,1)S(1)}, bf16[2,2,2,64,512]{4,3,0,1,2:T(8,128)(2,1)S(1)}, u32[]{:S(2)}, u32[]{:S(2)}) collective-permute-start(bf16[2,2,2,64,512]{4,3,0,1,2:T(8,128)(2,1)S(1)} %copy.29), channel_id=1, source_target_pairs={{0,1},{1,0},{2,3},{3,2},{4,5},{5,4},{6,7},{7,6},{8,9},{9,8},{10,11... | collective-permute-start | bytes 1572872 | tf_op jit(solution)/shard_map/ppermute | solution.py:19
  56.0 11.4 %collective-permute-start.11 = (bf16[2,2,2,64,288]{4,3,2,1,0:T(8,128)(2,1)S(1)}, bf16[2,2,2,64,288]{4,3,2,1,0:T(8,128)(2,1)S(1)}, u32[]{:S(2)}, u32[]{:S(2)}) collective-permute-start(bf16[2,2,2,64,288]{4,3,2,1,0:T(8,128)(2,1)S(1)} %bitcast.133), channel_id=1, source_target_pairs={{0,1},{1,0},{2,3},{3,2},{4,5},{5,4},{6,7},{7,6},{8,9},{9,8},{10,11... | collective-permute-start | bytes 884744 | tf_op jit(solution)/shard_map/ppermute | solution.py:19
  56.5 10.8 %collective-permute-start.8 = (bf16[2,2,64,512]{3,2,0,1:T(8,128)(2,1)S(1)}, bf16[2,2,64,512]{3,2,0,1:T(8,128)(2,1)S(1)}, u32[]{:S(2)}, u32[]{:S(2)}) collective-permute-start(bf16[2,2,64,512]{3,2,0,1:T(8,128)(2,1)S(1)} %fusion.1), channel_id=1, source_target_pairs={{0,4},{4,0},{1,5},{5,1},{2,6},{6,2},{3,7},{7,3},{8,12},{12,8},{9,1... | collective-permute-start | bytes 786440 | tf_op jit(solution)/shard_map/ppermute | solution.py:19
  59.1 8.1 %collective-permute-start.7 = (bf16[2,2,64,512]{3,2,0,1:T(8,128)(2,1)S(1)}, bf16[2,2,64,512]{3,2,0,1:T(8,128)(2,1)S(1)}, u32[]{:S(2)}, u32[]{:S(2)}) collective-permute-start(bf16[2,2,64,512]{3,2,0,1:T(8,128)(2,1)S(1)} %fusion), channel_id=1, source_target_pairs={{0,2},{2,0},{1,3},{3,1},{4,6},{6,4},{5,7},{7,5},{8,10},{10,8},{9,1... | collective-permute-start | bytes 786440 | tf_op jit(solution)/shard_map/ppermute | solution.py:19
  68.0 11.3 %collective-permute-start.16 = (bf16[2,2,64,288]{3,2,1,0:T(8,128)(2,1)S(1)}, bf16[2,2,64,288]{3,2,1,0:T(8,128)(2,1)S(1)}, u32[]{:S(2)}, u32[]{:S(2)}) collective-permute-start(bf16[2,2,64,288]{3,2,1,0:T(8,128)(2,1)S(1)} %fusion.4), channel_id=1, source_target_pairs={{0,2},{2,0},{1,3},{3,1},{4,6},{6,4},{5,7},{7,5},{8,10},{10,8},{9,1... | collective-permute-start | bytes 442376 | tf_op jit(solution)/shard_map/ppermute | solution.py:19
  69.5 9.9 %collective-permute-start.15 = (bf16[2,2,64,512]{3,2,0,1:T(8,128)(2,1)S(1)}, bf16[2,2,64,512]{3,2,0,1:T(8,128)(2,1)S(1)}, u32[]{:S(2)}, u32[]{:S(2)}) collective-permute-start(bf16[2,2,64,512]{3,2,0,1:T(8,128)(2,1)S(1)} %fusion.3), channel_id=1, source_target_pairs={{0,4},{4,0},{1,5},{5,1},{2,6},{6,2},{3,7},{7,3},{8,12},{12,8},{9,1... | collective-permute-start | bytes 786440 | tf_op jit(solution)/shard_map/ppermute | solution.py:19
  70.0 8.7 %collective-permute-start.13 = (bf16[2,64,512]{2,1,0:T(8,128)(2,1)S(1)}, bf16[2,64,512]{2,1,0:T(8,128)(2,1)S(1)}, u32[]{:S(2)}, u32[]{:S(2)}) collective-permute-start(bf16[2,64,512]{2,1,0:T(8,128)(2,1)S(1)} %fusion.6), channel_id=1, source_target_pairs={{0,2},{2,0},{1,3},{3,1},{4,6},{6,4},{5,7},{7,5},{8,10},{10,8},{9,1... | collective-permute-start | bytes 393224 | tf_op jit(solution)/shard_map/ppermute | solution.py:19
  70.6 11.7 %collective-permute-start.14 = (bf16[2,2,64,512]{3,2,0,1:T(8,128)(2,1)S(1)}, bf16[2,2,64,512]{3,2,0,1:T(8,128)(2,1)S(1)}, u32[]{:S(2)}, u32[]{:S(2)}) collective-permute-start(bf16[2,2,64,512]{3,2,0,1:T(8,128)(2,1)S(1)} %fusion.2), channel_id=1, source_target_pairs={{0,2},{2,0},{1,3},{3,1},{4,6},{6,4},{5,7},{7,5},{8,10},{10,8},{9,1... | collective-permute-start | bytes 786440 | tf_op jit(solution)/shard_map/ppermute | solution.py:19
  72.2 7.0 %collective-permute-start.12 = (bf16[2,64,512]{2,1,0:T(8,128)(2,1)S(1)}, bf16[2,64,512]{2,1,0:T(8,128)(2,1)S(1)}, u32[]{:S(2)}, u32[]{:S(2)}) collective-permute-start(bf16[2,64,512]{2,1,0:T(8,128)(2,1)S(1)} %fusion.5), channel_id=1, source_target_pairs={{0,4},{4,0},{1,5},{5,1},{2,6},{6,2},{3,7},{7,3},{8,12},{12,8},{9,1... | collective-permute-start | bytes 393224 | tf_op jit(solution)/shard_map/ppermute | solution.py:19
  82.3 11.6 %collective-permute-start.21 = (bf16[2,64,288]{2,1,0:T(8,128)(2,1)S(1)}, bf16[2,64,288]{2,1,0:T(8,128)(2,1)S(1)}, u32[]{:S(2)}, u32[]{:S(2)}) collective-permute-start(bf16[2,64,288]{2,1,0:T(8,128)(2,1)S(1)} %fusion.9), channel_id=1, source_target_pairs={{0,4},{4,0},{1,5},{5,1},{2,6},{6,2},{3,7},{7,3},{8,12},{12,8},{9,1... | collective-permute-start | bytes 221192 | tf_op jit(solution)/shard_map/ppermute | solution.py:19
  83.1 10.9 %collective-permute-start.20 = (bf16[2,64,512]{2,1,0:T(8,128)(2,1)S(1)}, bf16[2,64,512]{2,1,0:T(8,128)(2,1)S(1)}, u32[]{:S(2)}, u32[]{:S(2)}) collective-permute-start(bf16[2,64,512]{2,1,0:T(8,128)(2,1)S(1)} %fusion.8), channel_id=1, source_target_pairs={{0,2},{2,0},{1,3},{3,1},{4,6},{6,4},{5,7},{7,5},{8,10},{10,8},{9,1... | collective-permute-start | bytes 393224 | tf_op jit(solution)/shard_map/ppermute | solution.py:19
  84.4 9.7 %collective-permute-start.19 = (bf16[2,64,512]{2,1,0:T(8,128)(2,1)S(1)}, bf16[2,64,512]{2,1,0:T(8,128)(2,1)S(1)}, u32[]{:S(2)}, u32[]{:S(2)}) collective-permute-start(bf16[2,64,512]{2,1,0:T(8,128)(2,1)S(1)} %fusion.7), channel_id=1, source_target_pairs={{0,4},{4,0},{1,5},{5,1},{2,6},{6,2},{3,7},{7,3},{8,12},{12,8},{9,1... | collective-permute-start | bytes 393224 | tf_op jit(solution)/shard_map/ppermute | solution.py:19
  86.0 5.3 %collective-permute-start.18 = (bf16[64,512]{1,0:T(8,128)(2,1)S(1)}, bf16[64,512]{1,0:T(8,128)(2,1)S(1)}, u32[]{:S(2)}, u32[]{:S(2)}) collective-permute-start(bf16[64,512]{1,0:T(8,128)(2,1)S(1)} %fusion.11), channel_id=1, source_target_pairs={{0,8},{8,0},{1,9},{9,1},{2,10},{10,2},{3,11},{11,3},{4,12},{12,4},... | collective-permute-start | bytes 196616 | tf_op jit(solution)/shard_map/ppermute | solution.py:19
  87.9 6.0 %collective-permute-start.17 = (bf16[64,512]{1,0:T(8,128)(2,1)S(1)}, bf16[64,512]{1,0:T(8,128)(2,1)S(1)}, u32[]{:S(2)}, u32[]{:S(2)}) collective-permute-start(bf16[64,512]{1,0:T(8,128)(2,1)S(1)} %fusion.10), channel_id=1, source_target_pairs={{0,8},{8,0},{1,9},{9,1},{2,10},{10,2},{3,11},{11,3},{4,12},{12,4},... | collective-permute-start | bytes 196616 | tf_op jit(solution)/shard_map/ppermute | solution.py:19
  94.1 9.7 %collective-permute-start.23 = (bf16[64,512]{1,0:T(8,128)(2,1)S(1)}, bf16[64,512]{1,0:T(8,128)(2,1)S(1)}, u32[]{:S(2)}, u32[]{:S(2)}) collective-permute-start(bf16[64,512]{1,0:T(8,128)(2,1)S(1)} %fusion.12), channel_id=1, source_target_pairs={{0,8},{8,0},{1,9},{9,1},{2,10},{10,2},{3,11},{11,3},{4,12},{12,4},... | collective-permute-start | bytes 196616 | tf_op jit(solution)/shard_map/ppermute | solution.py:19
  94.5 9.3 %collective-permute-start.24 = (bf16[64,512]{1,0:T(8,128)(2,1)S(1)}, bf16[64,512]{1,0:T(8,128)(2,1)S(1)}, u32[]{:S(2)}, u32[]{:S(2)}) collective-permute-start(bf16[64,512]{1,0:T(8,128)(2,1)S(1)} %fusion.13), channel_id=1, source_target_pairs={{0,8},{8,0},{1,9},{9,1},{2,10},{10,2},{3,11},{11,3},{4,12},{12,4},... | collective-permute-start | bytes 196616 | tf_op jit(solution)/shard_map/ppermute | solution.py:19
  97.2 6.0 %collective-permute-start.22 = (bf16[64,288]{1,0:T(8,128)(2,1)S(1)}, bf16[64,288]{1,0:T(8,128)(2,1)S(1)}, u32[]{:S(2)}, u32[]{:S(2)}) collective-permute-start(bf16[64,288]{1,0:T(8,128)(2,1)S(1)} %fusion.14), channel_id=1, source_target_pairs={{0,8},{8,0},{1,9},{9,1},{2,10},{10,2},{3,11},{11,3},{4,12},{12,4},... | collective-permute-start | bytes 110600 | tf_op jit(solution)/shard_map/ppermute | solution.py:19
  (14 other events, 56.6 us)

commit v6 on v5

--- a/solution.py
+++ b/solution.py
@@ -299,8 +299,9 @@
             halve_round(piece, left, order[at])
             for piece, left, order in zip(third, third_left, last_order)
         ]
-        tied = lax.optimization_barrier((*third, *last))
-        third, last = list(tied[:2]), list(tied[2:])
+        if at + 1 < len(high_first):
+            tied = lax.optimization_barrier((*third, *last))
+            third, last = list(tied[:2]), list(tied[2:])
         last = [
             halve_round(piece, left, order[at])
             for piece, left, order in zip(last, last_left, last_order)

time: 105 us -> 107 us (1.019)
  waiting for transfers between devices: 35.8 us -> 37.3 us
    ppermute x23, waiting for transfers between devices: 22.2 us -> 23.7 us  [partner(): return lax.ppermute(block, axis, route)]
  transfers between devices with their start and end apart: 25 -> 25, of which waited for: 8 -> 10; matrix products, arithmetic and copies ran while one was open for 15% -> 14% of each run, Pallas kernels for 3% -> 3%
where the time goes in v6:
time: 107 us
  waiting for transfers between devices  37.3 us (35%)
  starting transfers between devices  28.9 us (27%)
  Pallas kernels  17.2 us (16%)
  local copies, waits for them, and re-layouts  10.3 us (10%)
  other arithmetic  8.45 us (8%)
  matrix products  3.54 us (3%)
  between operations  1.32 us (1%)
    ppermute x23, starting transfers between devices, partner(): return lax.ppermute(block, axis, route)  25.5 us
    ppermute x23, waiting for transfers between devices, partner(): return lax.ppermute(block, axis, route)  23.7 us
    ppermute x2, waiting for transfers between devices, from_behind(): return lax.ppermute(array, axis, pairs)  13.6 us
    pallas_call x1, Pallas kernels, group_backward(): pl.pallas_call(functools.partial(group_kernel, tile_rows, width, taps //...  10.8 us
    pallas_call x4, Pallas kernels, wgrad_half(): pl.pallas_call(functools.partial(wgrad_kernel, unit, normalizer), grid=(c...  6.35 us
    unnamed x27, local copies, waits for them, and re-layouts  4.68 us
    ppermute x2, starting transfers between devices, from_behind(): return lax.ppermute(array, axis, pairs)  3.38 us
    add x5, other arithmetic, halve_start(): return shards_view(kept, bits - 1) + received.astype(jnp.float32)  3.07 us
  transfers between devices with their start and end apart: 25, of which 10 were waited for; matrix products, arithmetic and copies ran while one was open for 14% of the time, Pallas kernels for 3%

profile of v6, /device:TPU:0, one launch (start us, length us, event | category | flops | bytes accessed | tf_op | source)
XLA Modules:
  0.0 106.9 jit_solution(2607766457358230238)
XLA Ops:
  0.7 2.4 %constant_dynamic-slice_fusion.1 = (bf16[1,4,256,256]{3,2,1,0:T(8,128)(2,1)}, bf16[4,256,256]{2,1,0:T(8,128)(2,1)}) fusion(bf16[2,4,256,256]{3,2,1,0:T(8,128)(2,1)} %bitcast.131, s32[]{:T(128)S(6)} %select_n.235, s32[]{:T(128)S(6)} %select_n.218), kind=kLoop, calls=%fused_computation.66 | loop fusion | bytes 2097160 | tf_op jit(solution)/shard_map/jit(dynamic_index_in_dim)/dynamic_slice | solution.py:249
  3.1 2.9 %collective-permute-start.3 = (bf16[4,256,256]{2,1,0:T(8,128)(2,1)}, bf16[4,256,256]{2,1,0:T(8,128)(2,1)}, u32[]{:S(2)}, u32[]{:S(2)}) collective-permute-start(bf16[4,256,256]{2,1,0:T(8,128)(2,1)} %get-tuple-element.30), channel_id=1, source_target_pairs={{0,2},{2,0},{1,3},{3,1},{4,6},{6,4},{5,7},{7,5},{8,10},{10,8},{9,1... | collective-permute-start | bytes 1572872 | tf_op jit(solution)/shard_map/ppermute | solution.py:19
  8.2 2.1 %collective-permute-start = (bf16[1,128,1024]{2,1,0:T(8,128)(2,1)}, bf16[1,128,1024]{2,1,0:T(8,128)(2,1)S(1)}, u32[]{:S(2)}, u32[]{:S(2)}) collective-permute-start(bf16[1,128,1024]{2,1,0:T(8,128)(2,1)} %get-tuple-element.61), channel_id=1, source_target_pairs={{0,2},{1,3},{2,4},{3,5},{4,6},{5,7},{6,8},{7,9},{8,10},{9,11},{10,... | collective-permute-start | bytes 786440 | tf_op jit(solution)/shard_map/ppermute | solution.py:25
  11.6 1.6 %shard_map.105 = (bf16[512,512]{1,0:T(8,128)(2,1)S(1)}, f32[512,512]{1,0:T(8,128)S(1)}) custom-call(bf16[512,1024]{1,0:T(8,128)(2,1)S(1)} %bitcast.108, bf16[512,1024]{1,0:T(8,128)(2,1)S(1)} %bitcast.113), custom_call_target="tpu_custom_call" | custom-call | flops 536870912 | bytes 3145728 | tf_op jit(solution)/shard_map/pallas_call | solution.py:82
  15.2 13.6 %collective-permute-done = bf16[1,128,1024]{2,1,0:T(8,128)(2,1)S(1)} collective-permute-done((bf16[1,128,1024]{2,1,0:T(8,128)(2,1)}, bf16[1,128,1024]{2,1,0:T(8,128)(2,1)S(1)}, u32[]{:S(2)}, u32[]{:S(2)}) %collective-permute-start) | collective-permute-done | bytes 262176 | tf_op jit(solution)/shard_map/ppermute | solution.py:25
  36.3 1.8 %maximum_select_fusion = bf16[2,4,2,128,256]{4,3,2,1,0:T(8,128)(2,1)S(1)} fusion(bf16[1,4,2,128,256]{4,3,2,1,0:T(8,128)(2,1)} %bitcast.13, bf16[1,4,2,128,256]{4,3,2,1,0:T(8,128)(2,1)} %bitcast.130, pred[]{:T(512)S(6)} %eq.34), kind=kLoop, calls=%fused_computation.2 | loop fusion | flops 1572864 | bytes 2097153 | tf_op jit(solution)/shard_map/jit(_where)/select_n | solution.py:104
  41.2 10.8 %shard_map.102 = (bf16[512,1024]{1,0:T(8,128)(2,1)S(1)}, f32[1024,288]{1,0:T(8,128)S(1)}) custom-call(bf16[512,1024]{1,0:T(8,128)(2,1)S(1)} %copy-done.11, bf16[128,1024]{1,0:T(8,128)(2,1)S(1)} %bitcast.128, bf16[128,1024]{1,0:T(8,128)(2,1)} %bitcast.7.bottom_ref, f32[6,1024]{1,0:T(8,128)S(1)} %get-tuple-element.63.left_ref, ...), custom_call_target="tpu_custom_call" | custom-call | flops 12079595520 | bytes 4194304 | tf_op jit(solution)/shard_map/pallas_call | solution.py:205
  52.0 1.6 %shard_map.103 = (bf16[512,512]{1,0:T(8,128)(2,1)S(1)}, f32[512,512]{1,0:T(8,128)S(1)}) custom-call(bf16[512,1024]{1,0:T(8,128)(2,1)S(1)} %bitcast.110, bf16[512,1024]{1,0:T(8,128)(2,1)S(1)} %get-tuple-element.33.columns_ref), custom_call_target="tpu_custom_call" | custom-call | flops 536870912 | bytes 3145728 | tf_op jit(solution)/shard_map/pallas_call | solution.py:82
  53.6 1.6 %shard_map.106 = (bf16[512,512]{1,0:T(8,128)(2,1)S(1)}, f32[512,512]{1,0:T(8,128)S(1)}) custom-call(bf16[512,1024]{1,0:T(8,128)(2,1)S(1)} %bitcast.111, bf16[512,1024]{1,0:T(8,128)(2,1)S(1)} %get-tuple-element.33.columns_ref), custom_call_target="tpu_custom_call" | custom-call | flops 536870912 | bytes 3145728 | tf_op jit(solution)/shard_map/pallas_call | solution.py:82
  56.5 2.6 %collective-permute-start.8 = (bf16[2,2,64,512]{3,2,0,1:T(8,128)(2,1)S(1)}, bf16[2,2,64,512]{3,2,0,1:T(8,128)(2,1)S(1)}, u32[]{:S(2)}, u32[]{:S(2)}) collective-permute-start(bf16[2,2,64,512]{3,2,0,1:T(8,128)(2,1)S(1)} %fusion.1), channel_id=1, source_target_pairs={{0,4},{4,0},{1,5},{5,1},{2,6},{6,2},{3,7},{7,3},{8,12},{12,8},{9,1... | collective-permute-start | bytes 786440 | tf_op jit(solution)/shard_map/ppermute | solution.py:19
  60.6 2.3 %add_convert_fusion = bf16[512,1024]{1,0:T(8,128)(2,1)} fusion(bf16[512,1024]{1,0:T(8,128)(2,1)S(1)} %bitcast.115, bf16[512,1024]{1,0:T(8,128)(2,1)S(1)} %get-tuple-element.33.columns_ref, bf16[1024,1024]{1,0:T(8,128)(2,1)S(1)} %copy-done.12), kind=kOutput, calls=%fused_computation | convolution fusion | flops 1075314688 | bytes 5242880 | tf_op jit(solution)/shard_map/dot_general | solution.py:313
  62.9 4.3 %collective-permute-done.7 = bf16[2,2,64,512]{3,2,0,1:T(8,128)(2,1)S(1)} collective-permute-done((bf16[2,2,64,512]{3,2,0,1:T(8,128)(2,1)S(1)}, bf16[2,2,64,512]{3,2,0,1:T(8,128)(2,1)S(1)}, u32[]{:S(2)}, u32[]{:S(2)}) %collective-permute-start.7) | collective-permute-done | bytes 262176 | tf_op jit(solution)/shard_map/ppermute | solution.py:19
  70.6 1.6 %collective-permute-start.14 = (bf16[2,2,64,512]{3,2,0,1:T(8,128)(2,1)S(1)}, bf16[2,2,64,512]{3,2,0,1:T(8,128)(2,1)S(1)}, u32[]{:S(2)}, u32[]{:S(2)}) collective-permute-start(bf16[2,2,64,512]{3,2,0,1:T(8,128)(2,1)S(1)} %fusion.2), channel_id=1, source_target_pairs={{0,2},{2,0},{1,3},{3,1},{4,6},{6,4},{5,7},{7,5},{8,10},{10,8},{9,1... | collective-permute-start | bytes 786440 | tf_op jit(solution)/shard_map/ppermute | solution.py:19
  72.2 1.6 %collective-permute-start.12 = (bf16[2,64,512]{2,1,0:T(8,128)(2,1)S(1)}, bf16[2,64,512]{2,1,0:T(8,128)(2,1)S(1)}, u32[]{:S(2)}, u32[]{:S(2)}) collective-permute-start(bf16[2,64,512]{2,1,0:T(8,128)(2,1)S(1)} %fusion.5), channel_id=1, source_target_pairs={{0,4},{4,0},{1,5},{5,1},{2,6},{6,2},{3,7},{7,3},{8,12},{12,8},{9,1... | collective-permute-start | bytes 393224 | tf_op jit(solution)/shard_map/ppermute | solution.py:19
  73.9 4.8 %collective-permute-done.13 = bf16[2,64,512]{2,1,0:T(8,128)(2,1)S(1)} collective-permute-done((bf16[2,64,512]{2,1,0:T(8,128)(2,1)S(1)}, bf16[2,64,512]{2,1,0:T(8,128)(2,1)S(1)}, u32[]{:S(2)}, u32[]{:S(2)}) %collective-permute-start.13) | collective-permute-done | bytes 131104 | tf_op jit(solution)/shard_map/ppermute | solution.py:19
  79.4 2.8 %collective-permute-done.14 = bf16[2,2,64,512]{3,2,0,1:T(8,128)(2,1)S(1)} collective-permute-done((bf16[2,2,64,512]{3,2,0,1:T(8,128)(2,1)S(1)}, bf16[2,2,64,512]{3,2,0,1:T(8,128)(2,1)S(1)}, u32[]{:S(2)}, u32[]{:S(2)}) %collective-permute-start.14) | collective-permute-done | bytes 262176 | tf_op jit(solution)/shard_map/ppermute | solution.py:19
  84.4 1.6 %collective-permute-start.19 = (bf16[2,64,288]{2,1,0:T(8,128)(2,1)S(1)}, bf16[2,64,288]{2,1,0:T(8,128)(2,1)S(1)}, u32[]{:S(2)}, u32[]{:S(2)}) collective-permute-start(bf16[2,64,288]{2,1,0:T(8,128)(2,1)S(1)} %fusion.9), channel_id=1, source_target_pairs={{0,4},{4,0},{1,5},{5,1},{2,6},{6,2},{3,7},{7,3},{8,12},{12,8},{9,1... | collective-permute-start | bytes 221192 | tf_op jit(solution)/shard_map/ppermute | solution.py:19
  86.0 1.8 %collective-permute-start.17 = (bf16[64,512]{1,0:T(8,128)(2,1)S(1)}, bf16[64,512]{1,0:T(8,128)(2,1)S(1)}, u32[]{:S(2)}, u32[]{:S(2)}) collective-permute-start(bf16[64,512]{1,0:T(8,128)(2,1)S(1)} %fusion.10), channel_id=1, source_target_pairs={{0,8},{8,0},{1,9},{9,1},{2,10},{10,2},{3,11},{11,3},{4,12},{12,4},... | collective-permute-start | bytes 196616 | tf_op jit(solution)/shard_map/ppermute | solution.py:19
  89.1 2.2 %collective-permute-done.17 = bf16[64,512]{1,0:T(8,128)(2,1)S(1)} collective-permute-done((bf16[64,512]{1,0:T(8,128)(2,1)S(1)}, bf16[64,512]{1,0:T(8,128)(2,1)S(1)}, u32[]{:S(2)}, u32[]{:S(2)}) %collective-permute-start.17) | collective-permute-done | bytes 65568 | tf_op jit(solution)/shard_map/ppermute | solution.py:19
  91.3 1.9 %collective-permute-done.18 = bf16[64,512]{1,0:T(8,128)(2,1)S(1)} collective-permute-done((bf16[64,512]{1,0:T(8,128)(2,1)S(1)}, bf16[64,512]{1,0:T(8,128)(2,1)S(1)}, u32[]{:S(2)}, u32[]{:S(2)}) %collective-permute-start.18) | collective-permute-done | bytes 65568 | tf_op jit(solution)/shard_map/ppermute | solution.py:19
  95.2 3.1 %collective-permute-done.20 = bf16[64,288]{1,0:T(8,128)(2,1)S(1)} collective-permute-done((bf16[64,288]{1,0:T(8,128)(2,1)S(1)}, bf16[64,288]{1,0:T(8,128)(2,1)S(1)}, u32[]{:S(2)}, u32[]{:S(2)}) %collective-permute-start.20) | collective-permute-done | bytes 36896 | tf_op jit(solution)/shard_map/ppermute | solution.py:19
  100.5 1.6 %collective-permute-start.24 = (bf16[64,512]{1,0:T(8,128)(2,1)S(1)}, bf16[64,512]{1,0:T(8,128)(2,1)S(1)}, u32[]{:S(2)}, u32[]{:S(2)}) collective-permute-start(bf16[64,512]{1,0:T(8,128)(2,1)S(1)} %fusion.13), channel_id=1, source_target_pairs={{0,8},{8,0},{1,9},{9,1},{2,10},{10,2},{3,11},{11,3},{4,12},{12,4},... | collective-permute-start | bytes 196616 | tf_op jit(solution)/shard_map/ppermute | solution.py:19
  102.1 2.1 %collective-permute-done.22 = bf16[64,512]{1,0:T(8,128)(2,1)S(1)} collective-permute-done((bf16[64,512]{1,0:T(8,128)(2,1)S(1)}, bf16[64,512]{1,0:T(8,128)(2,1)S(1)}, u32[]{:S(2)}, u32[]{:S(2)}) %collective-permute-start.22) | collective-permute-done | bytes 65568 | tf_op jit(solution)/shard_map/ppermute | solution.py:19
  104.2 1.9 %collective-permute-done.24 = bf16[64,512]{1,0:T(8,128)(2,1)S(1)} collective-permute-done((bf16[64,512]{1,0:T(8,128)(2,1)S(1)}, bf16[64,512]{1,0:T(8,128)(2,1)S(1)}, u32[]{:S(2)}, u32[]{:S(2)}) %collective-permute-start.24) | collective-permute-done | bytes 65568 | tf_op jit(solution)/shard_map/ppermute | solution.py:19
  (114 shorter events, 30.8 us)
Async XLA Ops:
  3.1 33.2 %collective-permute-start.3 = (bf16[4,256,256]{2,1,0:T(8,128)(2,1)}, bf16[4,256,256]{2,1,0:T(8,128)(2,1)}, u32[]{:S(2)}, u32[]{:S(2)}) collective-permute-start(bf16[4,256,256]{2,1,0:T(8,128)(2,1)} %get-tuple-element.30), channel_id=1, source_target_pairs={{0,2},{2,0},{1,3},{3,1},{4,6},{6,4},{5,7},{7,5},{8,10},{10,8},{9,1... | collective-permute-start | bytes 1572872 | tf_op jit(solution)/shard_map/ppermute | solution.py:19
  8.2 20.6 %collective-permute-start = (bf16[1,128,1024]{2,1,0:T(8,128)(2,1)}, bf16[1,128,1024]{2,1,0:T(8,128)(2,1)S(1)}, u32[]{:S(2)}, u32[]{:S(2)}) collective-permute-start(bf16[1,128,1024]{2,1,0:T(8,128)(2,1)} %get-tuple-element.61), channel_id=1, source_target_pairs={{0,2},{1,3},{2,4},{3,5},{4,6},{5,7},{6,8},{7,9},{8,10},{9,11},{10,... | collective-permute-start | bytes 786440 | tf_op jit(solution)/shard_map/ppermute | solution.py:25
  10.3 18.5 %collective-permute-start.1 = (bf16[1,128,1024]{2,1,0:T(8,128)(2,1)}, bf16[1,128,1024]{2,1,0:T(8,128)(2,1)}, u32[]{:S(2)}, u32[]{:S(2)}) collective-permute-start(bf16[1,128,1024]{2,1,0:T(8,128)(2,1)} %get-tuple-element.60), channel_id=1, source_target_pairs={{2,0},{3,1},{4,2},{5,3},{6,4},{7,5},{8,6},{9,7},{10,8},{11,9},{12,... | collective-permute-start | bytes 786440 | tf_op jit(solution)/shard_map/ppermute | solution.py:25
  15.1 23.2 %collective-permute-start.6 = (bf16[2,2,2,64,512]{4,3,0,2,1:T(8,128)(2,1)}, bf16[2,2,2,64,512]{4,3,0,2,1:T(8,128)(2,1)}, u32[]{:S(2)}, u32[]{:S(2)}) collective-permute-start(bf16[2,2,2,64,512]{4,3,0,2,1:T(8,128)(2,1)} %copy.27), channel_id=1, source_target_pairs={{0,1},{1,0},{2,3},{3,2},{4,5},{5,4},{6,7},{7,6},{8,9},{9,8},{10,11... | collective-permute-start | bytes 1572872 | tf_op jit(solution)/shard_map/ppermute | solution.py:19
  29.6 6.7 %collective-permute-start.2 = (bf16[6,1024]{1,0:T(8,128)(2,1)S(1)}, bf16[6,1024]{1,0:T(8,128)(2,1)S(1)}, u32[]{:S(2)}, u32[]{:S(2)}) collective-permute-start(bf16[6,1024]{1,0:T(8,128)(2,1)S(1)} %pad_maximum_fusion.2), channel_id=1, source_target_pairs={{0,1},{1,0},{2,3},{3,2},{4,5},{5,4},{6,7},{7,6},{8,9},{9,8},{10,11... | collective-permute-start | bytes 36872 | tf_op jit(solution)/shard_map/ppermute | solution.py:19
  34.3 5.3 %collective-permute-start.5 = (bf16[2,2,2,64,512]{4,3,0,1,2:T(8,128)(2,1)}, bf16[2,2,2,64,512]{4,3,0,1,2:T(8,128)(2,1)}, u32[]{:S(2)}, u32[]{:S(2)}) collective-permute-start(bf16[2,2,2,64,512]{4,3,0,1,2:T(8,128)(2,1)} %copy.25), channel_id=1, source_target_pairs={{0,1},{1,0},{2,3},{3,2},{4,5},{5,4},{6,7},{7,6},{8,9},{9,8},{10,11... | collective-permute-start | bytes 1572872 | tf_op jit(solution)/shard_map/ppermute | solution.py:19
  55.3 12.3 %collective-permute-start.10 = (bf16[2,2,2,64,512]{4,3,0,2,1:T(8,128)(2,1)S(1)}, bf16[2,2,2,64,512]{4,3,0,2,1:T(8,128)(2,1)S(1)}, u32[]{:S(2)}, u32[]{:S(2)}) collective-permute-start(bf16[2,2,2,64,512]{4,3,0,2,1:T(8,128)(2,1)S(1)} %copy.31), channel_id=1, source_target_pairs={{0,1},{1,0},{2,3},{3,2},{4,5},{5,4},{6,7},{7,6},{8,9},{9,8},{10,11... | collective-permute-start | bytes 1572872 | tf_op jit(solution)/shard_map/ppermute | solution.py:19
  55.8 12.0 %collective-permute-start.9 = (bf16[2,2,2,64,512]{4,3,0,1,2:T(8,128)(2,1)S(1)}, bf16[2,2,2,64,512]{4,3,0,1,2:T(8,128)(2,1)S(1)}, u32[]{:S(2)}, u32[]{:S(2)}) collective-permute-start(bf16[2,2,2,64,512]{4,3,0,1,2:T(8,128)(2,1)S(1)} %copy.29), channel_id=1, source_target_pairs={{0,1},{1,0},{2,3},{3,2},{4,5},{5,4},{6,7},{7,6},{8,9},{9,8},{10,11... | collective-permute-start | bytes 1572872 | tf_op jit(solution)/shard_map/ppermute | solution.py:19
  56.0 11.4 %collective-permute-start.11 = (bf16[2,2,2,64,288]{4,3,2,1,0:T(8,128)(2,1)S(1)}, bf16[2,2,2,64,288]{4,3,2,1,0:T(8,128)(2,1)S(1)}, u32[]{:S(2)}, u32[]{:S(2)}) collective-permute-start(bf16[2,2,2,64,288]{4,3,2,1,0:T(8,128)(2,1)S(1)} %bitcast.133), channel_id=1, source_target_pairs={{0,1},{1,0},{2,3},{3,2},{4,5},{5,4},{6,7},{7,6},{8,9},{9,8},{10,11... | collective-permute-start | bytes 884744 | tf_op jit(solution)/shard_map/ppermute | solution.py:19
  56.5 10.8 %collective-permute-start.8 = (bf16[2,2,64,512]{3,2,0,1:T(8,128)(2,1)S(1)}, bf16[2,2,64,512]{3,2,0,1:T(8,128)(2,1)S(1)}, u32[]{:S(2)}, u32[]{:S(2)}) collective-permute-start(bf16[2,2,64,512]{3,2,0,1:T(8,128)(2,1)S(1)} %fusion.1), channel_id=1, source_target_pairs={{0,4},{4,0},{1,5},{5,1},{2,6},{6,2},{3,7},{7,3},{8,12},{12,8},{9,1... | collective-permute-start | bytes 786440 | tf_op jit(solution)/shard_map/ppermute | solution.py:19
  59.1 8.1 %collective-permute-start.7 = (bf16[2,2,64,512]{3,2,0,1:T(8,128)(2,1)S(1)}, bf16[2,2,64,512]{3,2,0,1:T(8,128)(2,1)S(1)}, u32[]{:S(2)}, u32[]{:S(2)}) collective-permute-start(bf16[2,2,64,512]{3,2,0,1:T(8,128)(2,1)S(1)} %fusion), channel_id=1, source_target_pairs={{0,2},{2,0},{1,3},{3,1},{4,6},{6,4},{5,7},{7,5},{8,10},{10,8},{9,1... | collective-permute-start | bytes 786440 | tf_op jit(solution)/shard_map/ppermute | solution.py:19
  68.0 11.3 %collective-permute-start.16 = (bf16[2,2,64,288]{3,2,1,0:T(8,128)(2,1)S(1)}, bf16[2,2,64,288]{3,2,1,0:T(8,128)(2,1)S(1)}, u32[]{:S(2)}, u32[]{:S(2)}) collective-permute-start(bf16[2,2,64,288]{3,2,1,0:T(8,128)(2,1)S(1)} %fusion.4), channel_id=1, source_target_pairs={{0,2},{2,0},{1,3},{3,1},{4,6},{6,4},{5,7},{7,5},{8,10},{10,8},{9,1... | collective-permute-start | bytes 442376 | tf_op jit(solution)/shard_map/ppermute | solution.py:19
  69.5 9.9 %collective-permute-start.15 = (bf16[2,2,64,512]{3,2,0,1:T(8,128)(2,1)S(1)}, bf16[2,2,64,512]{3,2,0,1:T(8,128)(2,1)S(1)}, u32[]{:S(2)}, u32[]{:S(2)}) collective-permute-start(bf16[2,2,64,512]{3,2,0,1:T(8,128)(2,1)S(1)} %fusion.3), channel_id=1, source_target_pairs={{0,4},{4,0},{1,5},{5,1},{2,6},{6,2},{3,7},{7,3},{8,12},{12,8},{9,1... | collective-permute-start | bytes 786440 | tf_op jit(solution)/shard_map/ppermute | solution.py:19
  70.0 8.7 %collective-permute-start.13 = (bf16[2,64,512]{2,1,0:T(8,128)(2,1)S(1)}, bf16[2,64,512]{2,1,0:T(8,128)(2,1)S(1)}, u32[]{:S(2)}, u32[]{:S(2)}) collective-permute-start(bf16[2,64,512]{2,1,0:T(8,128)(2,1)S(1)} %fusion.6), channel_id=1, source_target_pairs={{0,2},{2,0},{1,3},{3,1},{4,6},{6,4},{5,7},{7,5},{8,10},{10,8},{9,1... | collective-permute-start | bytes 393224 | tf_op jit(solution)/shard_map/ppermute | solution.py:19
  70.6 11.7 %collective-permute-start.14 = (bf16[2,2,64,512]{3,2,0,1:T(8,128)(2,1)S(1)}, bf16[2,2,64,512]{3,2,0,1:T(8,128)(2,1)S(1)}, u32[]{:S(2)}, u32[]{:S(2)}) collective-permute-start(bf16[2,2,64,512]{3,2,0,1:T(8,128)(2,1)S(1)} %fusion.2), channel_id=1, source_target_pairs={{0,2},{2,0},{1,3},{3,1},{4,6},{6,4},{5,7},{7,5},{8,10},{10,8},{9,1... | collective-permute-start | bytes 786440 | tf_op jit(solution)/shard_map/ppermute | solution.py:19
  72.2 7.0 %collective-permute-start.12 = (bf16[2,64,512]{2,1,0:T(8,128)(2,1)S(1)}, bf16[2,64,512]{2,1,0:T(8,128)(2,1)S(1)}, u32[]{:S(2)}, u32[]{:S(2)}) collective-permute-start(bf16[2,64,512]{2,1,0:T(8,128)(2,1)S(1)} %fusion.5), channel_id=1, source_target_pairs={{0,4},{4,0},{1,5},{5,1},{2,6},{6,2},{3,7},{7,3},{8,12},{12,8},{9,1... | collective-permute-start | bytes 393224 | tf_op jit(solution)/shard_map/ppermute | solution.py:19
  82.4 16.6 %collective-permute-start.21 = (bf16[2,64,512]{2,1,0:T(8,128)(2,1)S(1)}, bf16[2,64,512]{2,1,0:T(8,128)(2,1)S(1)}, u32[]{:S(2)}, u32[]{:S(2)}) collective-permute-start(bf16[2,64,512]{2,1,0:T(8,128)(2,1)S(1)} %fusion.7), channel_id=1, source_target_pairs={{0,4},{4,0},{1,5},{5,1},{2,6},{6,2},{3,7},{7,3},{8,12},{12,8},{9,1... | collective-permute-start | bytes 393224 | tf_op jit(solution)/shard_map/ppermute | solution.py:19
  83.1 17.4 %collective-permute-start.23 = (bf16[2,64,512]{2,1,0:T(8,128)(2,1)S(1)}, bf16[2,64,512]{2,1,0:T(8,128)(2,1)S(1)}, u32[]{:S(2)}, u32[]{:S(2)}) collective-permute-start(bf16[2,64,512]{2,1,0:T(8,128)(2,1)S(1)} %fusion.8), channel_id=1, source_target_pairs={{0,2},{2,0},{1,3},{3,1},{4,6},{6,4},{5,7},{7,5},{8,10},{10,8},{9,1... | collective-permute-start | bytes 393224 | tf_op jit(solution)/shard_map/ppermute | solution.py:19
  84.4 8.8 %collective-permute-start.19 = (bf16[2,64,288]{2,1,0:T(8,128)(2,1)S(1)}, bf16[2,64,288]{2,1,0:T(8,128)(2,1)S(1)}, u32[]{:S(2)}, u32[]{:S(2)}) collective-permute-start(bf16[2,64,288]{2,1,0:T(8,128)(2,1)S(1)} %fusion.9), channel_id=1, source_target_pairs={{0,4},{4,0},{1,5},{5,1},{2,6},{6,2},{3,7},{7,3},{8,12},{12,8},{9,1... | collective-permute-start | bytes 221192 | tf_op jit(solution)/shard_map/ppermute | solution.py:19
  86.0 5.2 %collective-permute-start.17 = (bf16[64,512]{1,0:T(8,128)(2,1)S(1)}, bf16[64,512]{1,0:T(8,128)(2,1)S(1)}, u32[]{:S(2)}, u32[]{:S(2)}) collective-permute-start(bf16[64,512]{1,0:T(8,128)(2,1)S(1)} %fusion.10), channel_id=1, source_target_pairs={{0,8},{8,0},{1,9},{9,1},{2,10},{10,2},{3,11},{11,3},{4,12},{12,4},... | collective-permute-start | bytes 196616 | tf_op jit(solution)/shard_map/ppermute | solution.py:19
  87.9 5.2 %collective-permute-start.18 = (bf16[64,512]{1,0:T(8,128)(2,1)S(1)}, bf16[64,512]{1,0:T(8,128)(2,1)S(1)}, u32[]{:S(2)}, u32[]{:S(2)}) collective-permute-start(bf16[64,512]{1,0:T(8,128)(2,1)S(1)} %fusion.11), channel_id=1, source_target_pairs={{0,8},{8,0},{1,9},{9,1},{2,10},{10,2},{3,11},{11,3},{4,12},{12,4},... | collective-permute-start | bytes 196616 | tf_op jit(solution)/shard_map/ppermute | solution.py:19
  93.2 5.1 %collective-permute-start.20 = (bf16[64,288]{1,0:T(8,128)(2,1)S(1)}, bf16[64,288]{1,0:T(8,128)(2,1)S(1)}, u32[]{:S(2)}, u32[]{:S(2)}) collective-permute-start(bf16[64,288]{1,0:T(8,128)(2,1)S(1)} %fusion.14), channel_id=1, source_target_pairs={{0,8},{8,0},{1,9},{9,1},{2,10},{10,2},{3,11},{11,3},{4,12},{12,4},... | collective-permute-start | bytes 110600 | tf_op jit(solution)/shard_map/ppermute | solution.py:19
  99.0 5.2 %collective-permute-start.22 = (bf16[64,512]{1,0:T(8,128)(2,1)S(1)}, bf16[64,512]{1,0:T(8,128)(2,1)S(1)}, u32[]{:S(2)}, u32[]{:S(2)}) collective-permute-start(bf16[64,512]{1,0:T(8,128)(2,1)S(1)} %fusion.12), channel_id=1, source_target_pairs={{0,8},{8,0},{1,9},{9,1},{2,10},{10,2},{3,11},{11,3},{4,12},{12,4},... | collective-permute-start | bytes 196616 | tf_op jit(solution)/shard_map/ppermute | solution.py:19
  100.5 5.7 %collective-permute-start.24 = (bf16[64,512]{1,0:T(8,128)(2,1)S(1)}, bf16[64,512]{1,0:T(8,128)(2,1)S(1)}, u32[]{:S(2)}, u32[]{:S(2)}) collective-permute-start(bf16[64,512]{1,0:T(8,128)(2,1)S(1)} %fusion.13), channel_id=1, source_target_pairs={{0,8},{8,0},{1,9},{9,1},{2,10},{10,2},{3,11},{11,3},{4,12},{12,4},... | collective-permute-start | bytes 196616 | tf_op jit(solution)/shard_map/ppermute | solution.py:19
  (14 other events, 56.6 us)

commit v7 on v5

--- a/solution.py
+++ b/solution.py
@@ -259,6 +259,9 @@
     top = from_behind(inner_tile[-1:], "space", 2)
     bottom = from_behind(inner_tile[:1], "space", -2)
 
+    third_terms = [wgrad_half(third_rows, grad_rows, at, unit, normalizer) for at in (0, 1)]
+    top, bottom, _ = lax.optimization_barrier((top, bottom, third_terms[1][0]))
+
     def edge(tile):
         return jnp.where(col_parity == 0, tile[:, -1], tile[:, 0])
 
@@ -285,7 +288,7 @@
     third = []
     third_left = []
     for at in (0, 1):
-        piece = halve_start(wgrad_half(third_rows, grad_rows, at, unit, normalizer), bits)
+        piece = halve_start(third_terms[at], bits)
         third.append(piece)
         third_left.append(list(range(1, bits))[::-1])
     first_terms = [wgrad_half(input_rows, first_rows, at, unit, normalizer) for at in (0, 1)]

time: 105 us -> 105 us (level)
  no operation moved by 1% of the time
where the time goes in v7:
time: 105 us
  waiting for transfers between devices  35.8 us (34%)
  starting transfers between devices  28 us (27%)
  Pallas kernels  17.2 us (16%)
  local copies, waits for them, and re-layouts  10.3 us (10%)
  other arithmetic  8.46 us (8%)
  matrix products  3.54 us (3%)
  between operations  1.33 us (1%)
    ppermute x23, starting transfers between devices, partner(): return lax.ppermute(block, axis, route)  24.7 us
    ppermute x23, waiting for transfers between devices, partner(): return lax.ppermute(block, axis, route)  22.2 us
    ppermute x2, waiting for transfers between devices, from_behind(): return lax.ppermute(array, axis, pairs)  13.6 us
    pallas_call x1, Pallas kernels, group_backward(): pl.pallas_call(functools.partial(group_kernel, tile_rows, width, taps //...  10.8 us
    pallas_call x4, Pallas kernels, wgrad_half(): pl.pallas_call(functools.partial(wgrad_kernel, unit, normalizer), grid=(c...  6.35 us
    unnamed x27, local copies, waits for them, and re-layouts  4.69 us
    ppermute x2, starting transfers between devices, from_behind(): return lax.ppermute(array, axis, pairs)  3.38 us
    add x5, other arithmetic, halve_start(): return shards_view(kept, bits - 1) + received.astype(jnp.float32)  3.07 us
  transfers between devices with their start and end apart: 25, of which 8 were waited for; matrix products, arithmetic and copies ran while one was open for 15% of the time, Pallas kernels for 3%

profile of v7, /device:TPU:0, one launch (start us, length us, event | category | flops | bytes accessed | tf_op | source)
XLA Modules:
  0.0 104.6 jit_solution(9527058747536284888)
XLA Ops:
  0.7 2.4 %constant_dynamic-slice_fusion.1 = (bf16[1,4,256,256]{3,2,1,0:T(8,128)(2,1)}, bf16[4,256,256]{2,1,0:T(8,128)(2,1)}) fusion(bf16[2,4,256,256]{3,2,1,0:T(8,128)(2,1)} %bitcast.131, s32[]{:T(128)S(6)} %select_n.235, s32[]{:T(128)S(6)} %select_n.218), kind=kLoop, calls=%fused_computation.66 | loop fusion | bytes 2097160 | tf_op jit(solution)/shard_map/jit(dynamic_index_in_dim)/dynamic_slice | solution.py:249
  3.1 2.9 %collective-permute-start.3 = (bf16[4,256,256]{2,1,0:T(8,128)(2,1)}, bf16[4,256,256]{2,1,0:T(8,128)(2,1)}, u32[]{:S(2)}, u32[]{:S(2)}) collective-permute-start(bf16[4,256,256]{2,1,0:T(8,128)(2,1)} %get-tuple-element.40), channel_id=1, source_target_pairs={{0,2},{2,0},{1,3},{3,1},{4,6},{6,4},{5,7},{7,5},{8,10},{10,8},{9,1... | collective-permute-start | bytes 1572872 | tf_op jit(solution)/shard_map/ppermute | solution.py:19
  8.2 2.1 %collective-permute-start = (bf16[1,128,1024]{2,1,0:T(8,128)(2,1)}, bf16[1,128,1024]{2,1,0:T(8,128)(2,1)S(1)}, u32[]{:S(2)}, u32[]{:S(2)}) collective-permute-start(bf16[1,128,1024]{2,1,0:T(8,128)(2,1)} %get-tuple-element.75), channel_id=1, source_target_pairs={{0,2},{1,3},{2,4},{3,5},{4,6},{5,7},{6,8},{7,9},{8,10},{9,11},{10,... | collective-permute-start | bytes 786440 | tf_op jit(solution)/shard_map/ppermute | solution.py:25
  11.6 1.6 %shard_map.102 = (bf16[512,512]{1,0:T(8,128)(2,1)S(1)}, f32[512,512]{1,0:T(8,128)S(1)}) custom-call(bf16[512,1024]{1,0:T(8,128)(2,1)S(1)} %bitcast.108, bf16[512,1024]{1,0:T(8,128)(2,1)S(1)} %bitcast.113), custom_call_target="tpu_custom_call" | custom-call | flops 536870912 | bytes 3145728 | tf_op jit(solution)/shard_map/pallas_call | solution.py:82
  15.2 13.6 %collective-permute-done = bf16[1,128,1024]{2,1,0:T(8,128)(2,1)S(1)} collective-permute-done((bf16[1,128,1024]{2,1,0:T(8,128)(2,1)}, bf16[1,128,1024]{2,1,0:T(8,128)(2,1)S(1)}, u32[]{:S(2)}, u32[]{:S(2)}) %collective-permute-start) | collective-permute-done | bytes 262176 | tf_op jit(solution)/shard_map/ppermute | solution.py:25
  30.9 1.6 %shard_map.105 = (bf16[512,512]{1,0:T(8,128)(2,1)S(1)}, f32[512,512]{1,0:T(8,128)S(1)}) custom-call(bf16[512,1024]{1,0:T(8,128)(2,1)S(1)} %bitcast.109, bf16[512,1024]{1,0:T(8,128)(2,1)S(1)} %bitcast.114), custom_call_target="tpu_custom_call" | custom-call | flops 536870912 | bytes 3145728 | tf_op jit(solution)/shard_map/pallas_call | solution.py:82
  36.3 1.8 %maximum_select_fusion = bf16[2,4,2,128,256]{4,3,2,1,0:T(8,128)(2,1)S(1)} fusion(bf16[1,4,2,128,256]{4,3,2,1,0:T(8,128)(2,1)} %bitcast.13, bf16[1,4,2,128,256]{4,3,2,1,0:T(8,128)(2,1)} %bitcast.130, pred[]{:T(512)S(6)} %eq.34), kind=kLoop, calls=%fused_computation.2 | loop fusion | flops 1572864 | bytes 2097153 | tf_op jit(solution)/shard_map/jit(_where)/select_n | solution.py:104
  41.2 10.8 %shard_map.103 = (bf16[512,1024]{1,0:T(8,128)(2,1)S(1)}, f32[1024,288]{1,0:T(8,128)S(1)}) custom-call(bf16[512,1024]{1,0:T(8,128)(2,1)S(1)} %copy-done.11, bf16[128,1024]{1,0:T(8,128)(2,1)S(1)} %bitcast.128, bf16[128,1024]{1,0:T(8,128)(2,1)} %bitcast.7.bottom_ref, f32[6,1024]{1,0:T(8,128)S(1)} %get-tuple-element.77.left_ref, ...), custom_call_target="tpu_custom_call" | custom-call | flops 12079595520 | bytes 4194304 | tf_op jit(solution)/shard_map/pallas_call | solution.py:205
  52.0 1.6 %shard_map.104 = (bf16[512,512]{1,0:T(8,128)(2,1)S(1)}, f32[512,512]{1,0:T(8,128)S(1)}) custom-call(bf16[512,1024]{1,0:T(8,128)(2,1)S(1)} %bitcast.110, bf16[512,1024]{1,0:T(8,128)(2,1)S(1)} %get-tuple-element.43.columns_ref), custom_call_target="tpu_custom_call" | custom-call | flops 536870912 | bytes 3145728 | tf_op jit(solution)/shard_map/pallas_call | solution.py:82
  53.6 1.6 %shard_map.106 = (bf16[512,512]{1,0:T(8,128)(2,1)S(1)}, f32[512,512]{1,0:T(8,128)S(1)}) custom-call(bf16[512,1024]{1,0:T(8,128)(2,1)S(1)} %bitcast.111, bf16[512,1024]{1,0:T(8,128)(2,1)S(1)} %get-tuple-element.43.columns_ref), custom_call_target="tpu_custom_call" | custom-call | flops 536870912 | bytes 3145728 | tf_op jit(solution)/shard_map/pallas_call | solution.py:82
  56.5 2.6 %collective-permute-start.8 = (bf16[2,2,64,512]{3,2,0,1:T(8,128)(2,1)S(1)}, bf16[2,2,64,512]{3,2,0,1:T(8,128)(2,1)S(1)}, u32[]{:S(2)}, u32[]{:S(2)}) collective-permute-start(bf16[2,2,64,512]{3,2,0,1:T(8,128)(2,1)S(1)} %fusion.1), channel_id=1, source_target_pairs={{0,4},{4,0},{1,5},{5,1},{2,6},{6,2},{3,7},{7,3},{8,12},{12,8},{9,1... | collective-permute-start | bytes 786440 | tf_op jit(solution)/shard_map/ppermute | solution.py:19
  60.6 2.3 %add_convert_fusion = bf16[512,1024]{1,0:T(8,128)(2,1)} fusion(bf16[512,1024]{1,0:T(8,128)(2,1)S(1)} %bitcast.115, bf16[512,1024]{1,0:T(8,128)(2,1)S(1)} %get-tuple-element.43.columns_ref, bf16[1024,1024]{1,0:T(8,128)(2,1)S(1)} %copy-done.12), kind=kOutput, calls=%fused_computation | convolution fusion | flops 1075314688 | bytes 5242880 | tf_op jit(solution)/shard_map/dot_general | solution.py:315
  62.9 4.3 %collective-permute-done.7 = bf16[2,2,64,512]{3,2,0,1:T(8,128)(2,1)S(1)} collective-permute-done((bf16[2,2,64,512]{3,2,0,1:T(8,128)(2,1)S(1)}, bf16[2,2,64,512]{3,2,0,1:T(8,128)(2,1)S(1)}, u32[]{:S(2)}, u32[]{:S(2)}) %collective-permute-start.7) | collective-permute-done | bytes 262176 | tf_op jit(solution)/shard_map/ppermute | solution.py:19
  68.0 1.5 %collective-permute-start.16 = (bf16[2,2,64,288]{3,2,1,0:T(8,128)(2,1)S(1)}, bf16[2,2,64,288]{3,2,1,0:T(8,128)(2,1)S(1)}, u32[]{:S(2)}, u32[]{:S(2)}) collective-permute-start(bf16[2,2,64,288]{3,2,1,0:T(8,128)(2,1)S(1)} %fusion.4), channel_id=1, source_target_pairs={{0,2},{2,0},{1,3},{3,1},{4,6},{6,4},{5,7},{7,5},{8,10},{10,8},{9,1... | collective-permute-start | bytes 442376 | tf_op jit(solution)/shard_map/ppermute | solution.py:19
  70.6 1.6 %collective-permute-start.14 = (bf16[2,2,64,512]{3,2,0,1:T(8,128)(2,1)S(1)}, bf16[2,2,64,512]{3,2,0,1:T(8,128)(2,1)S(1)}, u32[]{:S(2)}, u32[]{:S(2)}) collective-permute-start(bf16[2,2,64,512]{3,2,0,1:T(8,128)(2,1)S(1)} %fusion.2), channel_id=1, source_target_pairs={{0,2},{2,0},{1,3},{3,1},{4,6},{6,4},{5,7},{7,5},{8,10},{10,8},{9,1... | collective-permute-start | bytes 786440 | tf_op jit(solution)/shard_map/ppermute | solution.py:19
  72.2 1.6 %collective-permute-start.12 = (bf16[2,64,512]{2,1,0:T(8,128)(2,1)S(1)}, bf16[2,64,512]{2,1,0:T(8,128)(2,1)S(1)}, u32[]{:S(2)}, u32[]{:S(2)}) collective-permute-start(bf16[2,64,512]{2,1,0:T(8,128)(2,1)S(1)} %fusion.5), channel_id=1, source_target_pairs={{0,4},{4,0},{1,5},{5,1},{2,6},{6,2},{3,7},{7,3},{8,12},{12,8},{9,1... | collective-permute-start | bytes 393224 | tf_op jit(solution)/shard_map/ppermute | solution.py:19
  73.9 4.8 %collective-permute-done.13 = bf16[2,64,512]{2,1,0:T(8,128)(2,1)S(1)} collective-permute-done((bf16[2,64,512]{2,1,0:T(8,128)(2,1)S(1)}, bf16[2,64,512]{2,1,0:T(8,128)(2,1)S(1)}, u32[]{:S(2)}, u32[]{:S(2)}) %collective-permute-start.13) | collective-permute-done | bytes 131104 | tf_op jit(solution)/shard_map/ppermute | solution.py:19
  79.5 2.8 %collective-permute-done.14 = bf16[2,2,64,512]{3,2,0,1:T(8,128)(2,1)S(1)} collective-permute-done((bf16[2,2,64,512]{3,2,0,1:T(8,128)(2,1)S(1)}, bf16[2,2,64,512]{3,2,0,1:T(8,128)(2,1)S(1)}, u32[]{:S(2)}, u32[]{:S(2)}) %collective-permute-start.14) | collective-permute-done | bytes 262176 | tf_op jit(solution)/shard_map/ppermute | solution.py:19
  84.4 1.6 %collective-permute-start.19 = (bf16[2,64,512]{2,1,0:T(8,128)(2,1)S(1)}, bf16[2,64,512]{2,1,0:T(8,128)(2,1)S(1)}, u32[]{:S(2)}, u32[]{:S(2)}) collective-permute-start(bf16[2,64,512]{2,1,0:T(8,128)(2,1)S(1)} %fusion.7), channel_id=1, source_target_pairs={{0,4},{4,0},{1,5},{5,1},{2,6},{6,2},{3,7},{7,3},{8,12},{12,8},{9,1... | collective-permute-start | bytes 393224 | tf_op jit(solution)/shard_map/ppermute | solution.py:19
  86.1 1.9 %collective-permute-start.18 = (bf16[64,512]{1,0:T(8,128)(2,1)S(1)}, bf16[64,512]{1,0:T(8,128)(2,1)S(1)}, u32[]{:S(2)}, u32[]{:S(2)}) collective-permute-start(bf16[64,512]{1,0:T(8,128)(2,1)S(1)} %fusion.11), channel_id=1, source_target_pairs={{0,8},{8,0},{1,9},{9,1},{2,10},{10,2},{3,11},{11,3},{4,12},{12,4},... | collective-permute-start | bytes 196616 | tf_op jit(solution)/shard_map/ppermute | solution.py:19
  89.1 2.2 %collective-permute-done.18 = bf16[64,512]{1,0:T(8,128)(2,1)S(1)} collective-permute-done((bf16[64,512]{1,0:T(8,128)(2,1)S(1)}, bf16[64,512]{1,0:T(8,128)(2,1)S(1)}, u32[]{:S(2)}, u32[]{:S(2)}) %collective-permute-start.18) | collective-permute-done | bytes 65568 | tf_op jit(solution)/shard_map/ppermute | solution.py:19
  91.3 2.6 %collective-permute-done.17 = bf16[64,512]{1,0:T(8,128)(2,1)S(1)} collective-permute-done((bf16[64,512]{1,0:T(8,128)(2,1)S(1)}, bf16[64,512]{1,0:T(8,128)(2,1)S(1)}, u32[]{:S(2)}, u32[]{:S(2)}) %collective-permute-start.17) | collective-permute-done | bytes 65568 | tf_op jit(solution)/shard_map/ppermute | solution.py:19
  94.6 2.6 %collective-permute-start.24 = (bf16[64,512]{1,0:T(8,128)(2,1)S(1)}, bf16[64,512]{1,0:T(8,128)(2,1)S(1)}, u32[]{:S(2)}, u32[]{:S(2)}) collective-permute-start(bf16[64,512]{1,0:T(8,128)(2,1)S(1)} %fusion.13), channel_id=1, source_target_pairs={{0,8},{8,0},{1,9},{9,1},{2,10},{10,2},{3,11},{11,3},{4,12},{12,4},... | collective-permute-start | bytes 196616 | tf_op jit(solution)/shard_map/ppermute | solution.py:19
  98.4 4.8 %collective-permute-done.22 = bf16[64,288]{1,0:T(8,128)(2,1)S(1)} collective-permute-done((bf16[64,288]{1,0:T(8,128)(2,1)S(1)}, bf16[64,288]{1,0:T(8,128)(2,1)S(1)}, u32[]{:S(2)}, u32[]{:S(2)}) %collective-permute-start.22) | collective-permute-done | bytes 36896 | tf_op jit(solution)/shard_map/ppermute | solution.py:19
  (113 shorter events, 25.9 us)
Async XLA Ops:
  3.1 33.2 %collective-permute-start.3 = (bf16[4,256,256]{2,1,0:T(8,128)(2,1)}, bf16[4,256,256]{2,1,0:T(8,128)(2,1)}, u32[]{:S(2)}, u32[]{:S(2)}) collective-permute-start(bf16[4,256,256]{2,1,0:T(8,128)(2,1)} %get-tuple-element.40), channel_id=1, source_target_pairs={{0,2},{2,0},{1,3},{3,1},{4,6},{6,4},{5,7},{7,5},{8,10},{10,8},{9,1... | collective-permute-start | bytes 1572872 | tf_op jit(solution)/shard_map/ppermute | solution.py:19
  8.2 20.5 %collective-permute-start = (bf16[1,128,1024]{2,1,0:T(8,128)(2,1)}, bf16[1,128,1024]{2,1,0:T(8,128)(2,1)S(1)}, u32[]{:S(2)}, u32[]{:S(2)}) collective-permute-start(bf16[1,128,1024]{2,1,0:T(8,128)(2,1)} %get-tuple-element.75), channel_id=1, source_target_pairs={{0,2},{1,3},{2,4},{3,5},{4,6},{5,7},{6,8},{7,9},{8,10},{9,11},{10,... | collective-permute-start | bytes 786440 | tf_op jit(solution)/shard_map/ppermute | solution.py:25
  10.3 18.5 %collective-permute-start.1 = (bf16[1,128,1024]{2,1,0:T(8,128)(2,1)}, bf16[1,128,1024]{2,1,0:T(8,128)(2,1)}, u32[]{:S(2)}, u32[]{:S(2)}) collective-permute-start(bf16[1,128,1024]{2,1,0:T(8,128)(2,1)} %get-tuple-element.74), channel_id=1, source_target_pairs={{2,0},{3,1},{4,2},{5,3},{6,4},{7,5},{8,6},{9,7},{10,8},{11,9},{12,... | collective-permute-start | bytes 786440 | tf_op jit(solution)/shard_map/ppermute | solution.py:25
  15.1 23.2 %collective-permute-start.6 = (bf16[2,2,2,64,512]{4,3,0,2,1:T(8,128)(2,1)}, bf16[2,2,2,64,512]{4,3,0,2,1:T(8,128)(2,1)}, u32[]{:S(2)}, u32[]{:S(2)}) collective-permute-start(bf16[2,2,2,64,512]{4,3,0,2,1:T(8,128)(2,1)} %copy.27), channel_id=1, source_target_pairs={{0,1},{1,0},{2,3},{3,2},{4,5},{5,4},{6,7},{7,6},{8,9},{9,8},{10,11... | collective-permute-start | bytes 1572872 | tf_op jit(solution)/shard_map/ppermute | solution.py:19
  29.6 6.7 %collective-permute-start.2 = (bf16[6,1024]{1,0:T(8,128)(2,1)S(1)}, bf16[6,1024]{1,0:T(8,128)(2,1)S(1)}, u32[]{:S(2)}, u32[]{:S(2)}) collective-permute-start(bf16[6,1024]{1,0:T(8,128)(2,1)S(1)} %pad_maximum_fusion.2), channel_id=1, source_target_pairs={{0,1},{1,0},{2,3},{3,2},{4,5},{5,4},{6,7},{7,6},{8,9},{9,8},{10,11... | collective-permute-start | bytes 36872 | tf_op jit(solution)/shard_map/ppermute | solution.py:19
  34.3 5.3 %collective-permute-start.5 = (bf16[2,2,2,64,512]{4,3,0,1,2:T(8,128)(2,1)}, bf16[2,2,2,64,512]{4,3,0,1,2:T(8,128)(2,1)}, u32[]{:S(2)}, u32[]{:S(2)}) collective-permute-start(bf16[2,2,2,64,512]{4,3,0,1,2:T(8,128)(2,1)} %copy.25), channel_id=1, source_target_pairs={{0,1},{1,0},{2,3},{3,2},{4,5},{5,4},{6,7},{7,6},{8,9},{9,8},{10,11... | collective-permute-start | bytes 1572872 | tf_op jit(solution)/shard_map/ppermute | solution.py:19
  55.3 12.3 %collective-permute-start.10 = (bf16[2,2,2,64,512]{4,3,0,2,1:T(8,128)(2,1)S(1)}, bf16[2,2,2,64,512]{4,3,0,2,1:T(8,128)(2,1)S(1)}, u32[]{:S(2)}, u32[]{:S(2)}) collective-permute-start(bf16[2,2,2,64,512]{4,3,0,2,1:T(8,128)(2,1)S(1)} %copy.31), channel_id=1, source_target_pairs={{0,1},{1,0},{2,3},{3,2},{4,5},{5,4},{6,7},{7,6},{8,9},{9,8},{10,11... | collective-permute-start | bytes 1572872 | tf_op jit(solution)/shard_map/ppermute | solution.py:19
  55.8 11.7 %collective-permute-start.11 = (bf16[2,2,2,64,288]{4,3,2,1,0:T(8,128)(2,1)S(1)}, bf16[2,2,2,64,288]{4,3,2,1,0:T(8,128)(2,1)S(1)}, u32[]{:S(2)}, u32[]{:S(2)}) collective-permute-start(bf16[2,2,2,64,288]{4,3,2,1,0:T(8,128)(2,1)S(1)} %bitcast.133), channel_id=1, source_target_pairs={{0,1},{1,0},{2,3},{3,2},{4,5},{5,4},{6,7},{7,6},{8,9},{9,8},{10,11... | collective-permute-start | bytes 884744 | tf_op jit(solution)/shard_map/ppermute | solution.py:19
  56.0 11.7 %collective-permute-start.9 = (bf16[2,2,2,64,512]{4,3,0,1,2:T(8,128)(2,1)S(1)}, bf16[2,2,2,64,512]{4,3,0,1,2:T(8,128)(2,1)S(1)}, u32[]{:S(2)}, u32[]{:S(2)}) collective-permute-start(bf16[2,2,2,64,512]{4,3,0,1,2:T(8,128)(2,1)S(1)} %copy.29), channel_id=1, source_target_pairs={{0,1},{1,0},{2,3},{3,2},{4,5},{5,4},{6,7},{7,6},{8,9},{9,8},{10,11... | collective-permute-start | bytes 1572872 | tf_op jit(solution)/shard_map/ppermute | solution.py:19
  56.5 10.9 %collective-permute-start.8 = (bf16[2,2,64,512]{3,2,0,1:T(8,128)(2,1)S(1)}, bf16[2,2,64,512]{3,2,0,1:T(8,128)(2,1)S(1)}, u32[]{:S(2)}, u32[]{:S(2)}) collective-permute-start(bf16[2,2,64,512]{3,2,0,1:T(8,128)(2,1)S(1)} %fusion.1), channel_id=1, source_target_pairs={{0,4},{4,0},{1,5},{5,1},{2,6},{6,2},{3,7},{7,3},{8,12},{12,8},{9,1... | collective-permute-start | bytes 786440 | tf_op jit(solution)/shard_map/ppermute | solution.py:19
  59.2 8.1 %collective-permute-start.7 = (bf16[2,2,64,512]{3,2,0,1:T(8,128)(2,1)S(1)}, bf16[2,2,64,512]{3,2,0,1:T(8,128)(2,1)S(1)}, u32[]{:S(2)}, u32[]{:S(2)}) collective-permute-start(bf16[2,2,64,512]{3,2,0,1:T(8,128)(2,1)S(1)} %fusion), channel_id=1, source_target_pairs={{0,2},{2,0},{1,3},{3,1},{4,6},{6,4},{5,7},{7,5},{8,10},{10,8},{9,1... | collective-permute-start | bytes 786440 | tf_op jit(solution)/shard_map/ppermute | solution.py:19
  68.0 11.3 %collective-permute-start.16 = (bf16[2,2,64,288]{3,2,1,0:T(8,128)(2,1)S(1)}, bf16[2,2,64,288]{3,2,1,0:T(8,128)(2,1)S(1)}, u32[]{:S(2)}, u32[]{:S(2)}) collective-permute-start(bf16[2,2,64,288]{3,2,1,0:T(8,128)(2,1)S(1)} %fusion.4), channel_id=1, source_target_pairs={{0,2},{2,0},{1,3},{3,1},{4,6},{6,4},{5,7},{7,5},{8,10},{10,8},{9,1... | collective-permute-start | bytes 442376 | tf_op jit(solution)/shard_map/ppermute | solution.py:19
  69.5 9.9 %collective-permute-start.15 = (bf16[2,2,64,512]{3,2,0,1:T(8,128)(2,1)S(1)}, bf16[2,2,64,512]{3,2,0,1:T(8,128)(2,1)S(1)}, u32[]{:S(2)}, u32[]{:S(2)}) collective-permute-start(bf16[2,2,64,512]{3,2,0,1:T(8,128)(2,1)S(1)} %fusion.3), channel_id=1, source_target_pairs={{0,4},{4,0},{1,5},{5,1},{2,6},{6,2},{3,7},{7,3},{8,12},{12,8},{9,1... | collective-permute-start | bytes 786440 | tf_op jit(solution)/shard_map/ppermute | solution.py:19
  70.0 8.7 %collective-permute-start.13 = (bf16[2,64,512]{2,1,0:T(8,128)(2,1)S(1)}, bf16[2,64,512]{2,1,0:T(8,128)(2,1)S(1)}, u32[]{:S(2)}, u32[]{:S(2)}) collective-permute-start(bf16[2,64,512]{2,1,0:T(8,128)(2,1)S(1)} %fusion.6), channel_id=1, source_target_pairs={{0,2},{2,0},{1,3},{3,1},{4,6},{6,4},{5,7},{7,5},{8,10},{10,8},{9,1... | collective-permute-start | bytes 393224 | tf_op jit(solution)/shard_map/ppermute | solution.py:19
  70.6 11.7 %collective-permute-start.14 = (bf16[2,2,64,512]{3,2,0,1:T(8,128)(2,1)S(1)}, bf16[2,2,64,512]{3,2,0,1:T(8,128)(2,1)S(1)}, u32[]{:S(2)}, u32[]{:S(2)}) collective-permute-start(bf16[2,2,64,512]{3,2,0,1:T(8,128)(2,1)S(1)} %fusion.2), channel_id=1, source_target_pairs={{0,2},{2,0},{1,3},{3,1},{4,6},{6,4},{5,7},{7,5},{8,10},{10,8},{9,1... | collective-permute-start | bytes 786440 | tf_op jit(solution)/shard_map/ppermute | solution.py:19
  72.2 7.0 %collective-permute-start.12 = (bf16[2,64,512]{2,1,0:T(8,128)(2,1)S(1)}, bf16[2,64,512]{2,1,0:T(8,128)(2,1)S(1)}, u32[]{:S(2)}, u32[]{:S(2)}) collective-permute-start(bf16[2,64,512]{2,1,0:T(8,128)(2,1)S(1)} %fusion.5), channel_id=1, source_target_pairs={{0,4},{4,0},{1,5},{5,1},{2,6},{6,2},{3,7},{7,3},{8,12},{12,8},{9,1... | collective-permute-start | bytes 393224 | tf_op jit(solution)/shard_map/ppermute | solution.py:19
  82.4 11.6 %collective-permute-start.21 = (bf16[2,64,288]{2,1,0:T(8,128)(2,1)S(1)}, bf16[2,64,288]{2,1,0:T(8,128)(2,1)S(1)}, u32[]{:S(2)}, u32[]{:S(2)}) collective-permute-start(bf16[2,64,288]{2,1,0:T(8,128)(2,1)S(1)} %fusion.9), channel_id=1, source_target_pairs={{0,4},{4,0},{1,5},{5,1},{2,6},{6,2},{3,7},{7,3},{8,12},{12,8},{9,1... | collective-permute-start | bytes 221192 | tf_op jit(solution)/shard_map/ppermute | solution.py:19
  83.1 10.9 %collective-permute-start.20 = (bf16[2,64,512]{2,1,0:T(8,128)(2,1)S(1)}, bf16[2,64,512]{2,1,0:T(8,128)(2,1)S(1)}, u32[]{:S(2)}, u32[]{:S(2)}) collective-permute-start(bf16[2,64,512]{2,1,0:T(8,128)(2,1)S(1)} %fusion.8), channel_id=1, source_target_pairs={{0,2},{2,0},{1,3},{3,1},{4,6},{6,4},{5,7},{7,5},{8,10},{10,8},{9,1... | collective-permute-start | bytes 393224 | tf_op jit(solution)/shard_map/ppermute | solution.py:19
  84.4 9.7 %collective-permute-start.19 = (bf16[2,64,512]{2,1,0:T(8,128)(2,1)S(1)}, bf16[2,64,512]{2,1,0:T(8,128)(2,1)S(1)}, u32[]{:S(2)}, u32[]{:S(2)}) collective-permute-start(bf16[2,64,512]{2,1,0:T(8,128)(2,1)S(1)} %fusion.7), channel_id=1, source_target_pairs={{0,4},{4,0},{1,5},{5,1},{2,6},{6,2},{3,7},{7,3},{8,12},{12,8},{9,1... | collective-permute-start | bytes 393224 | tf_op jit(solution)/shard_map/ppermute | solution.py:19
  86.1 5.3 %collective-permute-start.18 = (bf16[64,512]{1,0:T(8,128)(2,1)S(1)}, bf16[64,512]{1,0:T(8,128)(2,1)S(1)}, u32[]{:S(2)}, u32[]{:S(2)}) collective-permute-start(bf16[64,512]{1,0:T(8,128)(2,1)S(1)} %fusion.11), channel_id=1, source_target_pairs={{0,8},{8,0},{1,9},{9,1},{2,10},{10,2},{3,11},{11,3},{4,12},{12,4},... | collective-permute-start | bytes 196616 | tf_op jit(solution)/shard_map/ppermute | solution.py:19
  87.9 6.0 %collective-permute-start.17 = (bf16[64,512]{1,0:T(8,128)(2,1)S(1)}, bf16[64,512]{1,0:T(8,128)(2,1)S(1)}, u32[]{:S(2)}, u32[]{:S(2)}) collective-permute-start(bf16[64,512]{1,0:T(8,128)(2,1)S(1)} %fusion.10), channel_id=1, source_target_pairs={{0,8},{8,0},{1,9},{9,1},{2,10},{10,2},{3,11},{11,3},{4,12},{12,4},... | collective-permute-start | bytes 196616 | tf_op jit(solution)/shard_map/ppermute | solution.py:19
  94.1 9.7 %collective-permute-start.23 = (bf16[64,512]{1,0:T(8,128)(2,1)S(1)}, bf16[64,512]{1,0:T(8,128)(2,1)S(1)}, u32[]{:S(2)}, u32[]{:S(2)}) collective-permute-start(bf16[64,512]{1,0:T(8,128)(2,1)S(1)} %fusion.12), channel_id=1, source_target_pairs={{0,8},{8,0},{1,9},{9,1},{2,10},{10,2},{3,11},{11,3},{4,12},{12,4},... | collective-permute-start | bytes 196616 | tf_op jit(solution)/shard_map/ppermute | solution.py:19
  94.6 9.3 %collective-permute-start.24 = (bf16[64,512]{1,0:T(8,128)(2,1)S(1)}, bf16[64,512]{1,0:T(8,128)(2,1)S(1)}, u32[]{:S(2)}, u32[]{:S(2)}) collective-permute-start(bf16[64,512]{1,0:T(8,128)(2,1)S(1)} %fusion.13), channel_id=1, source_target_pairs={{0,8},{8,0},{1,9},{9,1},{2,10},{10,2},{3,11},{11,3},{4,12},{12,4},... | collective-permute-start | bytes 196616 | tf_op jit(solution)/shard_map/ppermute | solution.py:19
  97.2 5.9 %collective-permute-start.22 = (bf16[64,288]{1,0:T(8,128)(2,1)S(1)}, bf16[64,288]{1,0:T(8,128)(2,1)S(1)}, u32[]{:S(2)}, u32[]{:S(2)}) collective-permute-start(bf16[64,288]{1,0:T(8,128)(2,1)S(1)} %fusion.14), channel_id=1, source_target_pairs={{0,8},{8,0},{1,9},{9,1},{2,10},{10,2},{3,11},{11,3},{4,12},{12,4},... | collective-permute-start | bytes 110600 | tf_op jit(solution)/shard_map/ppermute | solution.py:19
  (14 other events, 56.6 us)
